TPU v7x, 128 devices: a whole 4x4x4 slice. The times are simulated.
128 devices in a mesh: tm: 32 (over y, x, core), state: 4 (over z).
Axes of the slice: x: 4, y: 4, z: 4, core: 2. Of those that a mesh axis runs over, the one named last changes fastest.
Arguments:
- filtered_cov: float32 [128, 512, 512], P('tm', 'state'), may hold values from -4 to 5, as said below
- filtered_mean: float32 [128, 512], P('tm'), may hold values from -6 to 6
- noise_var: float32 [512], replicated, may hold values from 0.00390625 to 0.2
- trans_blocks: float32 [4, 2, 128, 128], replicated, may hold values from -1 to 2
- pattern: int32 [4, 2], replicated, may hold values from 0 to 3, as said below
Outputs:
- smooth_mean: float32 [128, 512], P('tm', 'state')
- smooth_cov: float32 [128, 512, 512], P('tm', 'state')
Inputs may be any that keep to these rules, and one draw needn't show every extreme that they name: `filtered_cov`: each matrix is symmetric, and every eigenvalue is at least 0.5. `pattern`: block row r names 2 different column blocks; slot 0 names r itself.
All inputs are finite; a program needn't handle non-finite values.
Results may differ from a plain program's by a relative error of at most 0.0003.
Values sent between devices are 32-bit elements; how exact they have to be, the bound alone decides.
A program may use at most 192 MiB of HBM per device.

v0:
```python
from functools import partial

import jax
import jax.numpy as jnp
from jax import lax
from jax.sharding import Mesh
from jax.sharding import PartitionSpec as P

TM = ("tm_0", "tm_1", "tm_2")


highest = lax.Precision.HIGHEST


def filled_with(x, identity):
    return jax.tree.map(
        lambda part, zero: jnp.zeros_like(part) + jnp.asarray(zero, part.dtype), x, identity
    )


def prefix_by_axis(x, axes, combine, identity):
    before = start = filled_with(x, identity)
    subtotal = x
    for axis in reversed(axes):
        peers, position = (lax.axis_size(axis), lax.axis_index(axis))
        pieces = jax.tree.map(lambda part: lax.all_gather(part, axis), subtotal)
        inside, subtotal = (start, start)
        for k in reversed(range(peers)):
            passed = k > position
            subtotal = combine(subtotal, jax.tree.map(lambda part: part[k], pieces))
            inside = jax.tree.map(lambda new, old: jnp.where(passed, new, old), subtotal, inside)
        before = combine(inside, before)
    return before


def left_apply(blocks, pattern, matrix):
    block_count = blocks.shape[0]
    block_size = blocks.shape[2]
    tile_rows = matrix.reshape(block_count, block_size, matrix.shape[-1])
    picked = tile_rows[pattern]
    result = jnp.einsum("rjab,rjbk->rak", blocks, picked, precision=highest)
    return result.reshape(matrix.shape[0], matrix.shape[-1])


def right_apply(blocks, pattern, matrix):
    block_count = blocks.shape[0]
    block_size = blocks.shape[2]
    tile_cols = matrix.reshape(matrix.shape[0], block_count, block_size)
    picked = tile_cols[:, pattern]
    result = jnp.einsum("krjb,rjab->kra", picked, blocks, precision=highest)
    return result.reshape(matrix.shape[0], matrix.shape[1])


def push_mean(blocks, pattern, mean_vec):
    return left_apply(blocks, pattern, mean_vec[:, None])[:, 0]


def solve_columns(tri_factor, right_side):
    return jax.scipy.linalg.cho_solve((tri_factor, True), right_side)


def compose(early_el, late_el):
    early_gain, early_offset, early_spread = early_el
    late_gain, late_offset, late_spread = late_el
    joined_gain = jnp.dot(early_gain, late_gain, precision=highest)
    joined_offset = jnp.dot(early_gain, late_offset, precision=highest) + early_offset
    weighted = jnp.dot(early_gain, late_spread, precision=highest)
    joined_spread = jnp.dot(weighted, early_gain.T, precision=highest) + early_spread
    return (joined_gain, joined_offset, joined_spread)


def on_device(filtered_cov, filtered_mean, noise_var, trans_blocks, pattern):
    local_steps = filtered_cov.shape[0]
    shard_rows = filtered_cov.shape[1]
    state_size = filtered_cov.shape[2]
    tm_devices = lax.axis_size(TM)
    row_start = lax.axis_index("state") * shard_rows
    step_start = lax.axis_index(TM) * local_steps
    cov_cols = jnp.swapaxes(filtered_cov, 1, 2)
    left_cols = jax.vmap(partial(left_apply, trans_blocks, pattern))(cov_cols)
    left_full = lax.all_gather(left_cols, "state", axis=2, tiled=True)
    predicted = (
        jax.vmap(partial(right_apply, trans_blocks, pattern))(left_full) + jnp.diag(noise_var)[None]
    )
    factor = jnp.linalg.cholesky(predicted)
    solved = jax.vmap(solve_columns)(factor, left_cols)
    moments = step_start + jnp.arange(local_steps, dtype=jnp.int32)
    keep_flag = (moments != local_steps * tm_devices - 1).astype(jnp.float32)
    gain_rows = jnp.swapaxes(solved, 1, 2) * keep_flag[:, None, None]
    pushed = jax.vmap(partial(push_mean, trans_blocks, pattern))(filtered_mean)
    mean_rows = lax.dynamic_slice_in_dim(filtered_mean, row_start, shard_rows, 1)
    offset_rows = mean_rows - jnp.einsum("sck,sk->sc", gain_rows, pushed, precision=highest)
    spread_rows = filtered_cov - jnp.einsum("sck,skl->scl", gain_rows, left_full, precision=highest)
    gain_full, offset_full, spread_full = (
        lax.all_gather(gain_rows, "state", axis=1, tiled=True),
        lax.all_gather(offset_rows, "state", axis=1, tiled=True),
        lax.all_gather(spread_rows, "state", axis=1, tiled=True),
    )
    identity_el = (
        jnp.eye(state_size, dtype=jnp.float32),
        jnp.zeros((state_size,), jnp.float32),
        jnp.zeros((state_size, state_size), jnp.float32),
    )

    def suffix_step(late_el, element):
        joined = compose(element, late_el)
        return (joined, joined)

    aggregate, suffixes = lax.scan(
        suffix_step, identity_el, (gain_full, offset_full, spread_full), reverse=True
    )

    def joined_scan(higher_el, lower_el):
        return compose(lower_el, higher_el)

    remote = prefix_by_axis(
        (aggregate[0], aggregate[1], aggregate[2]), TM, joined_scan, identity_el
    )
    suffix_gain = lax.dynamic_slice_in_dim(suffixes[0], row_start, shard_rows, 1)
    suffix_offset = lax.dynamic_slice_in_dim(suffixes[1], row_start, shard_rows, 1)
    suffix_spread = lax.dynamic_slice_in_dim(suffixes[2], row_start, shard_rows, 1)
    smooth_mean = jnp.einsum("sck,k->sc", suffix_gain, remote[1], precision=highest) + suffix_offset
    weighted = jnp.einsum("sck,kl->scl", suffix_gain, remote[2], precision=highest)
    smooth_cov = (
        jnp.einsum("scl,sml->scm", weighted, suffixes[0], precision=highest) + suffix_spread
    )
    return (smooth_mean, smooth_cov)


def solution(mesh):
    torus = Mesh(
        mesh.devices.reshape(4, 4, 2, mesh.shape["state"]), ("tm_0", "tm_1", "tm_2", "state")
    )
    return jax.shard_map(
        on_device,
        mesh=torus,
        in_specs=(P(TM, "state", None), P(TM, None), P(), P(), P()),
        out_specs=(P(TM, "state"), P(TM, "state", None)),
        check_vma=False,
    )
```

profile of v0, /device:TPU:1, one launch (start us, length us, event | category | flops | bytes accessed | tf_op | source)
XLA Modules:
  0.0 1064.7 jit_solution(2076647335803064573)
XLA Ops:
  11.7 2.9 convolution_bitcast_fusion.1
  16.5 52.8 %all-gather.22.cloned.1.call-done = f32[4,512,512]{2,1,0:T(8,128)} async-done(((f32[4,512,128]{2,1,0:T(8,128)}), f32[4,512,512]{2,1,0:T(8,128)}) %all-gather.22.cloned.1.call-update) | async-done | bytes 4194320 | tf_op jit(solution)/shard_map/all_gather | solution.py:81
  69.3 4.6 copy_bitcast_fusion
  73.9 6.6 gather_fusion.1
  80.4 11.1 %convolution_bitcast_fusion = f32[4,512,4,128]{1,3,0,2:T(8,128)S(1)} fusion(f32[4,512,4,2,128]{4,1,0,3,2:T(8,128)} %bitcast.277, f32[4,2,128,128]{3,2,1,0:T(8,128)S(1)} %copy-done), kind=kOutput, calls=%fused_computation.34 | convolution fusion | flops 3221225472 | bytes 13107200 | tf_op jit(solution)/shard_map/vmap(krjb,rjab->kra)/dot_general | solution.py:50
  94.0 2.6 bitcast_add_fusion.1
  96.6 5.3 copy.78
  101.9 4.6 fusion.19
  108.6 46.9 %custom-call.38 = f32[4,128,128]{2,1,0:T(8,128)S(1)} custom-call(f32[4,128,128]{2,1,0:T(8,128)S(1)} %cholesky.271), custom_call_target="Cholesky" | custom-call | tf_op jit(solution)/shard_map/jit(cholesky)/cholesky | solution.py:85
  155.5 39.8 %custom-call.39 = f32[4,1,128,128]{2,3,1,0:T(8,128)S(1)} custom-call(f32[4,1,128,128]{3,2,1,0:T(8,128)S(1)} %select_bitcast_fusion.2), custom_call_target="InvertDiagBlocksLowerTriangular" | custom-call | tf_op jit(solution)/shard_map/jit(cholesky)/cholesky | solution.py:85
  197.8 2.9 constant_dynamic-update-slice_fusion.3
  202.8 46.9 %custom-call.40 = f32[4,128,128]{2,1,0:T(8,128)S(1)} custom-call(f32[4,128,128]{2,1,0:T(8,128)S(1)} %cholesky.275), custom_call_target="Cholesky" | custom-call | tf_op jit(solution)/shard_map/jit(cholesky)/cholesky | solution.py:85
  250.4 39.3 %custom-call.41 = f32[4,1,128,128]{2,3,1,0:T(8,128)S(1)} custom-call(f32[4,1,128,128]{3,2,1,0:T(8,128)S(1)} %get-tuple-element.337), custom_call_target="InvertDiagBlocksLowerTriangular" | custom-call | tf_op jit(solution)/shard_map/jit(cholesky)/cholesky | solution.py:85
  291.3 2.6 convolution_subtract_fusion.2
  293.9 47.1 %custom-call.42 = f32[4,128,128]{2,1,0:T(8,128)S(1)} custom-call(f32[4,128,128]{2,1,0:T(8,128)S(1)} %cholesky.280), custom_call_target="Cholesky" | custom-call | tf_op jit(solution)/shard_map/jit(cholesky)/cholesky | solution.py:85
  341.7 39.3 %custom-call.43 = f32[4,1,128,128]{2,3,1,0:T(8,128)S(1)} custom-call(f32[4,1,128,128]{3,2,1,0:T(8,128)S(1)} %get-tuple-element.335), custom_call_target="InvertDiagBlocksLowerTriangular" | custom-call | tf_op jit(solution)/shard_map/jit(cholesky)/cholesky | solution.py:85
  384.7 47.1 %custom-call.44 = f32[4,128,128]{2,1,0:T(8,128)S(1)} custom-call(f32[4,128,128]{2,1,0:T(8,128)S(1)} %convolution_subtract_fusion.7), custom_call_target="Cholesky" | custom-call | tf_op jit(solution)/shard_map/jit(cholesky)/cholesky | solution.py:85
  433.0 5.1 select_select_fusion
  438.1 15.3 %while.26 = (s32[]{:T(128)}, f32[4,512,512]{2,1,0:T(8,128)}, s32[4,2]{0,1:T(2,128)S(1)}, f32[4,4,128,128]{3,2,0,1:T(8,128)}, s32[]{:T(128)}) while((s32[]{:T(128)}, f32[4,512,512]{2,1,0:T(8,128)}, s32[4,2]{0,1:T(2,128)S(1)}, f32[4,4,128,128]{3,2,0,1:T(8,128)}, s32[]{:T(128)}) %tuple.84), condition=%wide.while_cond, body=%wide.while_body.sunk | while | flops 2 | bytes 525421 | solution.py:59
  438.7 3.2 bitcast_dynamic-update-slice_fusion.6
  442.6 3.2 bitcast_dynamic-update-slice_fusion.6
  446.4 3.2 bitcast_dynamic-update-slice_fusion.6
  450.3 3.1 bitcast_dynamic-update-slice_fusion.6
  453.4 158.0 %custom-call.45 = f32[4,4,128,128]{2,3,1,0:T(8,128)S(1)} custom-call(f32[4,4,128,128]{3,2,1,0:T(8,128)} %bitcast.331), custom_call_target="InvertDiagBlocksLowerTriangular" | custom-call | tf_op jit(solution)/shard_map/vmap(jit(_cho_solve))/triangular_solve | solution.py:59
  625.2 6.0 convolution_subtract_fusion
  633.3 8.1 all_gather.68
  641.5 35.8 %all-gather.24.cloned.1.call-done = f32[4,512,512]{1,2,0:T(8,128)} async-done(((f32[4,128,512]{1,2,0:T(8,128)}), f32[4,512,512]{1,2,0:T(8,128)}) %all-gather.24.cloned.1.call-update) | async-done | bytes 4194320 | tf_op jit(solution)/shard_map/all_gather | solution.py:95
  677.3 52.1 %all-gather.26.cloned.1.call-done = f32[4,512,512]{2,1,0:T(8,128)} async-done(((f32[4,128,512]{2,1,0:T(8,128)}), f32[4,512,512]{2,1,0:T(8,128)}) %all-gather.26.cloned.1.call-update) | async-done | bytes 4194320 | tf_op jit(solution)/shard_map/all_gather | solution.py:97
  734.4 56.6 %while.27 = (s32[]{:T(128)}, f32[512,512]{1,0:T(8,128)S(1)}, f32[512]{0:T(512)S(1)}, f32[512,512]{1,0:T(8,128)}, f32[4,512,512]{2,1,0:T(8,128)}, /*index=5*/f32[...) while((s32[]{:T(128)}, f32[512,512]{1,0:T(8,128)S(1)}, ...), condition=%wide.region_9.10_spmd.clone, body=%wide.region_8.9_spmd.clone.sunk | while | flops 4835509248 | bytes 15753388 | solution.py:109
  736.5 3.1 fusion.284
  739.5 4.1 bitcast_dynamic-update-slice_fusion.7
  743.6 4.7 bitcast_dynamic-update-slice_fusion.8
  750.4 3.4 fusion.284
  753.8 4.1 bitcast_dynamic-update-slice_fusion.7
  757.8 4.7 bitcast_dynamic-update-slice_fusion.8
  764.6 3.4 fusion.284
  768.0 4.1 bitcast_dynamic-update-slice_fusion.7
  772.1 4.7 bitcast_dynamic-update-slice_fusion.8
  778.8 3.4 fusion.284
  782.2 4.1 bitcast_dynamic-update-slice_fusion.7
  786.3 4.7 bitcast_dynamic-update-slice_fusion.8
  792.9 13.4 %all-gather.28.cloned.1.call-done = f32[1024,512]{1,0:T(8,128)} async-done(((f32[512,512]{1,0:T(8,128)}), f32[1024,512]{1,0:T(8,128)}) %all-gather.28.cloned.1.call-update) | async-done | bytes 2097168 | tf_op jit(solution)/shard_map/all_gather | solution.py:26
  809.6 4.1 fusion.109
  813.8 2.8 fusion.99
  816.5 6.5 all-gather.34.cloned.1.call-done
  823.0 3.5 convolution_add_fusion.10
  829.4 2.8 convolution_add_fusion.9
  832.3 41.2 %all-gather.30.cloned.1.call-done = f32[2048,512]{1,0:T(8,128)} async-done(((f32[512,512]{1,0:T(8,128)}), f32[2048,512]{1,0:T(8,128)}) %all-gather.30.cloned.1.call-update) | async-done | bytes 4194320 | tf_op jit(solution)/shard_map/all_gather | solution.py:26
  876.8 3.1 fusion.82
  883.7 2.8 fusion.96
  886.6 2.7 all-gather.9
  889.4 4.0 fusion.72
  893.4 30.3 %all-gather.36.cloned.1.call-done = f32[2048,512]{1,0:T(8,128)} async-done(((f32[512,512]{1,0:T(8,128)}), f32[2048,512]{1,0:T(8,128)}) %all-gather.36.cloned.1.call-update) | async-done | bytes 4194320 | tf_op jit(solution)/shard_map/all_gather | solution.py:26
  923.7 3.9 convolution_add_fusion.11
  929.4 3.2 convolution_add_fusion.8
  939.5 2.9 convolution_add_fusion.6
  944.5 9.2 all-gather.10
  962.4 10.0 all-gather.11
  975.4 2.9 fusion.27
  988.3 4.1 fusion.52
  992.3 32.4 %all-gather.38.cloned.1.call-done = f32[2048,512]{1,0:T(8,128)} async-done(((f32[512,512]{1,0:T(8,128)}), f32[2048,512]{1,0:T(8,128)}) %all-gather.38.cloned.1.call-update) | async-done | bytes 4194320 | tf_op jit(solution)/shard_map/all_gather | solution.py:26
  1024.8 3.9 convolution_add_fusion.12
  1031.0 3.3 convolution_add_fusion.5
  1051.3 6.7 convolution_add_fusion.1
  (240 shorter events, 121.2 us)
Async XLA Ops:
  7.2 4.6 copy-start
  7.2 62.1 %all-gather.22.cloned.1.call-start = ((), (), s32[]{:S(2)}) async-start(), calls=%async_computation | async-start | bytes 5242880 | tf_op jit(solution)/shard_map/all_gather | solution.py:81
  11.7 4.0 copy-start.40
  15.7 661.6 %all-gather.24.cloned.1.call-start = ((), (), s32[]{:S(2)}) async-start(), calls=%async_computation.1 | async-start | bytes 5242880 | tf_op jit(solution)/shard_map/all_gather | solution.py:95
  92.0 2.0 copy-start.7
  106.6 2.0 copy-start.11
  433.0 178.4 %copy-start.23 = (f32[4,4,128,128]{3,2,1,0:T(8,128)S(1)}, f32[4,4,128,128]{3,2,1,0:T(8,128)}, u32[]{:S(2)}) copy-start(f32[4,4,128,128]{3,2,1,0:T(8,128)} %copy.73) | copy-start | bytes 3145732
  611.4 5.2 copy-start.10
  619.5 5.7 copy-start.35
  622.8 0.7 copy-start.36
  624.6 6.6 copy-start.39
  624.7 7.9 copy-start.37
  624.7 104.8 %all-gather.26.cloned.1.call-start = ((), (), s32[]{:S(2)}) async-start(), calls=%async_computation.2 | async-start | bytes 5242880 | tf_op jit(solution)/shard_map/all_gather | solution.py:97
  631.2 175.1 %all-gather.28.cloned.1.call-start = ((), (), s32[]{:S(2)}) async-start(), calls=%async_computation.3 | async-start | bytes 3145728 | tf_op jit(solution)/shard_map/all_gather | solution.py:26
  791.0 1.0 copy-start.5
  792.1 30.9 %all-gather.34.cloned.1.call-start = ((), (), s32[]{:S(2)}) async-start(), calls=%async_computation.6 | async-start | bytes 3145728 | tf_op jit(solution)/shard_map/all_gather | solution.py:26
  792.7 80.8 %all-gather.30.cloned.1.call-start = ((), (), s32[]{:S(2)}) async-start(), calls=%async_computation.4 | async-start | bytes 5242880 | tf_op jit(solution)/shard_map/all_gather | solution.py:26
  806.3 7.5 copy-start.8
  808.6 1.0 copy-start.16
  813.7 110.0 %all-gather.36.cloned.1.call-start = ((), (), s32[]{:S(2)}) async-start(), calls=%async_computation.7 | async-start | bytes 5242880 | tf_op jit(solution)/shard_map/all_gather | solution.py:26
  823.0 6.4 copy-start.38
  826.6 1.0 copy-start.22
  832.2 146.0 %all-gather.32.cloned.1.call-start = ((), (), s32[]{:S(2)}) async-start(), calls=%async_computation.5 | async-start | bytes 5242880 | tf_op jit(solution)/shard_map/all_gather | solution.py:26
  873.5 7.4 copy-start.2
  875.8 1.0 copy-start.20
  879.9 1.0 copy-start.12
  882.7 1.1 copy-start.14
  886.6 138.2 %all-gather.38.cloned.1.call-start = ((), (), s32[]{:S(2)}) async-start(), calls=%async_computation.8 | async-start | bytes 5242880 | tf_op jit(solution)/shard_map/all_gather | solution.py:26
  923.7 3.9 copy-start.3
  927.6 7.0 copy-start.24
  929.4 5.1 copy-start.34
  932.7 6.8 copy-start.26
  936.4 1.0 copy-start.28
  942.4 14.6 %copy-start.17 = (f32[512,512]{1,0:T(8,128)S(1)}, f32[512,512]{1,0:T(8,128)}, u32[]{:S(2)}) copy-start(f32[512,512]{1,0:T(8,128)} %copy-done.16) | copy-start | bytes 3145732
  942.5 14.6 %copy-start.18 = (f32[512,512]{1,0:T(8,128)S(1)}, f32[512,512]{1,0:T(8,128)}, u32[]{:S(2)}) copy-start(f32[512,512]{1,0:T(8,128)} %fusion.109) | copy-start | bytes 3145732
  954.0 4.3 copy-start.4
  957.1 16.2 %copy-start.13 = (f32[512,512]{1,0:T(8,128)S(1)}, f32[512,512]{1,0:T(8,128)}, u32[]{:S(2)}) copy-start(f32[512,512]{1,0:T(8,128)} %copy-done.12) | copy-start | bytes 3145732
  957.1 16.2 %copy-start.15 = (f32[512,512]{1,0:T(8,128)S(1)}, f32[512,512]{1,0:T(8,128)}, u32[]{:S(2)}) copy-start(f32[512,512]{1,0:T(8,128)} %copy-done.14) | copy-start | bytes 3145732
  957.1 16.2 %copy-start.19 = (f32[512,512]{1,0:T(8,128)S(1)}, f32[512,512]{1,0:T(8,128)}, u32[]{:S(2)}) copy-start(f32[512,512]{1,0:T(8,128)} %fusion.96) | copy-start | bytes 3145732
  957.1 16.2 %copy-start.21 = (f32[512,512]{1,0:T(8,128)S(1)}, f32[512,512]{1,0:T(8,128)}, u32[]{:S(2)}) copy-start(f32[512,512]{1,0:T(8,128)} %copy-done.20) | copy-start | bytes 3145732
  961.3 14.0 %copy-start.25 = (f32[512,512]{1,0:T(8,128)S(1)}, f32[512,512]{1,0:T(8,128)}, u32[]{:S(2)}) copy-start(f32[512,512]{1,0:T(8,128)} %copy-done.24) | copy-start | bytes 3145732
  961.3 14.0 %copy-start.27 = (f32[512,512]{1,0:T(8,128)S(1)}, f32[512,512]{1,0:T(8,128)}, u32[]{:S(2)}) copy-start(f32[512,512]{1,0:T(8,128)} %copy-done.26) | copy-start | bytes 3145732
  961.3 14.0 %copy-start.29 = (f32[512,512]{1,0:T(8,128)S(1)}, f32[512,512]{1,0:T(8,128)}, u32[]{:S(2)}) copy-start(f32[512,512]{1,0:T(8,128)} %copy-done.28) | copy-start | bytes 3145732
  961.3 14.0 %copy-start.30 = (f32[512,512]{1,0:T(8,128)S(1)}, f32[512,512]{1,0:T(8,128)}, u32[]{:S(2)}) copy-start(f32[512,512]{1,0:T(8,128)} %convolution_add_fusion.6) | copy-start | bytes 3145732
  1024.8 3.9 copy-start.6
  1031.0 5.2 copy-start.33
  1042.0 4.0 copy-start.9
  1042.0 5.0 copy-start.31
  1042.0 5.0 copy-start.32
  1048.8 9.1 copy-start.1
Sparse Core Ops, SparseCore 0:
  15.8 53.4 all-gather.21
  624.8 52.4 all-gather.23
  679.0 50.4 all-gather.25
  792.2 14.0 all-gather.27
  808.4 14.6 all-gather.33
  824.5 48.9 all-gather.29
  875.1 48.5 all-gather.35
  925.9 48.6 all-gather.31
  976.3 48.4 all-gather.37
where the time goes:
time: 1080 us; the launch traced here: 1060 us
  other arithmetic  482 us (45%)
  waiting for transfers between devices  265 us (25%)
  matrix products  213 us (20%)
  local copies, waits for them, and re-layouts  57.9 us (5%)
  blocking collectives  30 us (3%)
  between operations  15.1 us (1%)
    another operation x16, other arithmetic, on_device(): factor = jnp.linalg.cholesky(predicted)  309 us
    another operation x4, other arithmetic, solve_columns(): return jax.scipy.linalg.cho_solve((tri_factor, True), right_side)  163 us
    all_gather x6, waiting for transfers between devices, prefix_by_axis(): pieces = jax.tree.map(lambda part: lax.all_gather(part, axis), subtotal)  124 us
    dot_general x17, matrix products, compose(): jnp.dot(weighted, early_gain.T, precision=highest) + early_spread  54 us
    all_gather x1, waiting for transfers between devices, on_device(): left_full = lax.all_gather(left_cols, 'state', axis=2, tiled=True)  52.8 us
    all_gather x1, waiting for transfers between devices, on_device(): lax.all_gather(spread_rows, 'state', axis=1, tiled=True)  52.1 us
    dot_general x17, matrix products, compose(): weighted = jnp.dot(early_gain, late_spread, precision=highest)  43.8 us
    dot_general x12, matrix products, compose(): joined_gain = jnp.dot(early_gain, late_gain, precision=highest)  35.9 us
  transfers between devices with their start and end apart: 9, of which 8 were waited for; matrix products, arithmetic and copies ran while one was open for 8% of the time, Pallas kernels for 0%

commit v1 on v0

v1 whole, which is shorter than its diff:
```python
from functools import partial

import jax
import jax.numpy as jnp
from jax import lax
from jax.experimental import pallas as pl
from jax.experimental.pallas import tpu as pltpu
from jax.sharding import Mesh
from jax.sharding import PartitionSpec as P

N = 512
B = 128
LROW = 512
GROW = 832
ROWS = 896
HALF = ROWS // 2
SH = ROWS // 8
MESH = pl.DeviceIdType.MESH
F32 = jnp.float32
BF16 = jnp.bfloat16
ANY = pl.BlockSpec(memory_space=pl.ANY)
VM = pl.BlockSpec(memory_space=pltpu.VMEM)
SM = pl.BlockSpec(memory_space=pltpu.SMEM)
TM = ("tm_0", "tm_1", "tm_2")


def split(x):
    high = x.astype(BF16)
    return high, (x - high.astype(F32)).astype(BF16)


def dg(a, b, cb=0):
    return lax.dot_general(a, b, (((1,), (cb,)), ((), ())), preferred_element_type=F32)


def dot_s(a, b, cb=0):
    return dg(a[0], b[0], cb) + (dg(a[0], b[1], cb) + dg(a[1], b[0], cb))


def dot3(a, b, cb=0):
    return dot_s(split(a), split(b), cb)


def packed_blocks():
    out = []
    for j in range(4):
        out.append((0, j, LROW, j, 128, 0))
    for lane, (i, j) in enumerate(((1, 1), (1, 2), (1, 3), (2, 2))):
        out.append((i, j, LROW + 128, lane, 128, 0))
    for lane, (i, j, r) in enumerate(((2, 3, 0), (2, 3, 64), (3, 3, 0), (3, 3, 64))):
        out.append((i, j, LROW + 256, lane, 64, r))
    return out


def pack_spread(ref, full):
    for i, j, row, lane, rows, r0 in packed_blocks():
        ref[row : row + rows, lane * B : lane * B + B] = full(i * B + r0, rows, j * B)


def unpack_spread(load, full_ref):
    for i, j, row, lane, rows, r0 in packed_blocks():
        block = load(row, rows, lane * B)
        full_ref[i * B + r0 : i * B + r0 + rows, j * B : j * B + B] = block
    for i in range(4):
        for j in range(i + 1, 4):
            block = full_ref[i * B : i * B + B, j * B : j * B + B]
            full_ref[j * B : j * B + B, i * B : i * B + B] = jnp.transpose(block)


def inverse128(block):
    row_id = lax.broadcasted_iota(jnp.int32, (8, B), 0)
    lane_id = lax.broadcasted_iota(jnp.int32, (8, B), 1)
    vs = tuple(block[8 * b : 8 * b + 8, :] for b in range(16))

    def body(_, vs):
        vs = list(vs)
        for i in range(0, 8, 2):
            r0 = jnp.broadcast_to(vs[0][i : i + 1, :], (8, B))
            r1 = jnp.broadcast_to(vs[0][i + 1 : i + 2, :], (8, B))
            c0 = [jnp.broadcast_to(v[:, i : i + 1], (8, B)) for v in vs]
            c1 = [jnp.broadcast_to(v[:, i + 1 : i + 2], (8, B)) for v in vs]
            a = jnp.broadcast_to(c0[0][i : i + 1, :], (8, B))
            b = jnp.broadcast_to(c0[0][i + 1 : i + 2, :], (8, B))
            d = jnp.broadcast_to(c1[0][i + 1 : i + 2, :], (8, B))
            inv = 1.0 / (a * d - b * b)
            ia, ib, idd = d * inv, -b * inv, a * inv
            is0, is1 = lane_id == i, lane_id == i + 1
            n0 = ia * r0 + ib * r1
            n1 = ib * r0 + idd * r1
            n0 = jnp.where(is0, -ia, jnp.where(is1, -ib, n0))
            n1 = jnp.where(is0, -ib, jnp.where(is1, -idd, n1))
            for k in range(16):
                base = jnp.where(is0 | is1, 0.0, vs[k])
                new = base - (c0[k] * n0 + c1[k] * n1)
                if k == 0:
                    new = jnp.where(row_id == i, n0, jnp.where(row_id == i + 1, n1, new))
                vs[k] = new
        vs = [pltpu.roll(v, B - 8, 1) for v in vs]
        return tuple(vs[1:] + vs[:1])

    vs = lax.fori_loop(0, 16, body, vs)
    return -jnp.concatenate(vs, axis=0)


def element_kernel(ids, pattern, cov, mean_a, mean_b, noise, blocks, out, left, pred, sol, upd):
    tb = lambda r, j: split(blocks[r, j])

    def rows_of(ref, block):
        return ref[pl.ds(pl.multiple_of(block * B, B), B), :]

    def lanes_of(ref, row, rows, block):
        return ref[row : row + rows, pl.ds(pl.multiple_of(block * B, B), B)]

    mean = jnp.where(ids[0] == 1, mean_a[pl.ds(ids[1], 1), :], mean_b[pl.ds(ids[1], 1), :])
    upd[0:8, :] = jnp.broadcast_to(mean, (8, N))
    pushed = []
    for r in range(4):
        t0, t1 = tb(r, 0), tb(r, 1)
        left[r * B : r * B + B, :] = dot_s(t0, split(rows_of(cov, pattern[r, 0]))) + dot_s(
            t1, split(rows_of(cov, pattern[r, 1]))
        )
        pushed.append(
            dot_s(split(lanes_of(upd, 0, 8, pattern[r, 0])), t0, 1)
            + dot_s(split(lanes_of(upd, 0, 8, pattern[r, 1])), t1, 1)
        )
    pushed = jnp.concatenate(pushed, axis=1)
    eye = lax.broadcasted_iota(jnp.int32, (B, B), 0) == lax.broadcasted_iota(jnp.int32, (B, B), 1)
    for r in range(4):
        rows = (r + 1) * B
        value = dot_s(split(lanes_of(left, 0, rows, pattern[r, 0])), tb(r, 0), 1) + dot_s(
            split(lanes_of(left, 0, rows, pattern[r, 1])), tb(r, 1), 1
        )
        pred[0:rows, r * B : r * B + B] = value
        q = jnp.where(eye, jnp.broadcast_to(noise[0:1, r * B : r * B + B], (B, B)), 0.0)
        pred[r * B : rows, r * B : r * B + B] += q
    sol[...] = left[...]
    for k in range(4):
        k0, k1 = k * B, k * B + B
        inv = split(inverse128(pred[k0:k1, k0:k1]))
        rhs = split(sol[k0:k1, :])
        ub = dot_s(inv, rhs)
        sol[k0:k1, :] = ub
        if k < 3:
            ubs = split(ub)
            tail = pred[k0:k1, k1:]
            ut = dot_s(inv, split(tail))
            uts = split(ut)
            st = split(jnp.transpose(tail))
            pred[k1:, k1:] -= dot_s(st, uts)
            sol[k1:, :] -= dot_s(st, ubs)
            pred[k0:k1, k1:] = ut
    for k in (2, 1, 0):
        k0, k1 = k * B, k * B + B
        sol[k0:k1, :] -= dot3(pred[k0:k1, k1:], sol[k1:, :])
    keep = ids[2].astype(F32)
    for i in range(4):
        for j in range(4):
            out[i * B : i * B + B, j * B : j * B + B] = (
                jnp.transpose(sol[j * B : j * B + B, i * B : i * B + B]) * keep
            )
    out[GROW : GROW + 8, :] = jnp.broadcast_to(mean, (8, N)) - keep * dot3(pushed, sol[...])
    out[GROW + 8 :, :] = jnp.zeros((ROWS - GROW - 8, N), F32)
    ls = split(left[...])
    for i in range(4):
        pred[i * B : i * B + B, :] = cov[i * B : i * B + B, :] - dot_s(
            split(out[i * B : i * B + B, :]), ls
        )
    pack_spread(out, lambda r, n, c: pred[r : r + n, c : c + B])


def scan_kernel(count, want_total, want_rest, ids, own, others, *refs):
    outs, (se, sl, sg, rh, rl, eh, el, lk) = refs[: want_total + want_rest], refs[want_total + want_rest :]
    rest_ref = outs[-1]
    me = ids[0]

    def load(k, row, rows, lane=0, lanes=N):
        slot = k if count > 2 else 0
        return jnp.where(
            k == me, own[row : row + rows, lane : lane + lanes], others[slot, row : row + rows, lane : lane + lanes]
        )

    def store(ref, slot):
        ref[0:N, :] = se[slot]
        pack_spread(ref, lambda r, n, c: sl[slot, r : r + n, c : c + B])
        ref[GROW : GROW + 8, :] = sg[slot]
        ref[GROW + 8 :, :] = jnp.zeros((ROWS - GROW - 8, N), F32)

    if want_rest:

        @pl.when(me == count - 1)
        def _():
            same = lax.broadcasted_iota(jnp.int32, (N, N), 0) == lax.broadcasted_iota(jnp.int32, (N, N), 1)
            rest_ref[0:N, :] = same.astype(F32)
            rest_ref[N:, :] = jnp.zeros((ROWS - N, N), F32)

    last = count - 1
    se[0] = load(last, 0, N)
    unpack_spread(lambda r, n, c: load(last, r, n, c, B), sl.at[0])
    sg[0] = load(last, GROW, 8)

    def step(t, _):
        k = count - 2 - t
        now = lax.rem(t, 2)
        new = 1 - now
        if want_rest:

            @pl.when(k == me)
            def _():
                store(rest_ref, now)

        for r in range(4):
            rows = slice(r * B, r * B + B)
            h, l = split(se[now, rows, :])
            rh[rows, 0:N], rl[rows, 0:N] = h, l
            h, l = split(sl[now, rows, :])
            rh[rows, N:], rl[rows, N:] = h, l
            h, l = split(load(k, r * B, B))
            eh[rows, :], el[rows, :] = h, l
        unpack_spread(lambda r, n, c: load(k, r, n, c, B), lk)
        sg[new] = dot_s(split(sg[now]), (eh[...], el[...]), 1) + load(k, GROW, 8)

        def rows_step(r, _):
            rows = pl.ds(pl.multiple_of(r * B, B), B)
            both = dot_s((eh[rows, :], el[rows, :]), (rh[...], rl[...]))
            se[new, rows, :] = both[:, :N]
            sl[new, rows, :] = dot_s(split(both[:, N:]), (eh[...], el[...]), 1) + lk[rows, :]
            return 0

        lax.fori_loop(0, 4, rows_step, 0)
        return 0

    steps = count - 1
    if want_total:
        lax.fori_loop(0, steps, step, 0)
        store(outs[0], steps % 2)
    else:
        lax.fori_loop(0, steps, step, 0)


def apply_kernel(ids, later, across, down, pair, own, out, cov, mean, w, eh, el, lk):
    unpack_spread(lambda r, n, c: later[r : r + n, c : c + B], cov)
    mean[...] = later[GROW : GROW + 8, :]

    def push(load):
        for r in range(4):
            rows = slice(r * B, r * B + B)
            h, l = split(load(r * B, B))
            eh[rows, :], el[rows, :] = h, l
            h, l = split(cov[rows, :])
            w[0, rows, :], w[1, rows, :] = h, l
        unpack_spread(lambda r, n, c: load(r, n, c, B), lk)
        mean[...] = dot_s(split(mean[...]), (eh[...], el[...]), 1) + load(GROW, 8)

        def rows_step(r, _):
            rows = pl.ds(pl.multiple_of(r * B, B), B)
            half = dot_s((eh[rows, :], el[rows, :]), (w[0], w[1]))
            cov[rows, :] = dot_s(split(half), (eh[...], el[...]), 1) + lk[rows, :]
            return 0

        lax.fori_loop(0, 4, rows_step, 0)

    push(lambda r, n, c=0, m=N: across[r : r + n, c : c + m])
    push(lambda r, n, c=0, m=N: down[r : r + n, c : c + m])
    push(lambda r, n, c=0, m=N: jnp.where(ids[0] == 0, pair[r : r + n, c : c + m], own[r : r + n, c : c + m]))
    for z in range(4):
        out[z, 0:B, :] = cov[z * B : z * B + B, :]
        out[z, B : B + 8, :] = mean[...]


def greet(peers):
    barrier = pltpu.get_barrier_semaphore()
    for peer in peers:
        pl.semaphore_signal(barrier, inc=1, device_id=peer, device_id_type=MESH)
    pl.semaphore_wait(barrier, len(peers))


def column_peers(z, c):
    return [
        {"state": lax.rem(z + dz, 4), "tm_2": c if dc == 0 else 1 - c}
        for dz in range(4)
        for dc in range(2)
        if dz or dc
    ]


def remote(src, dst, send, recv, peer):
    return pltpu.make_async_remote_copy(
        src_ref=src, dst_ref=dst, send_sem=send, recv_sem=recv, device_id=peer, device_id_type=MESH
    )


def gather_step_kernel(cov, mean, out, mean_out, send, recv, local, msend, mrecv):
    z, c = lax.axis_index("state"), lax.axis_index("tm_2")
    greet(column_peers(z, c))
    other = remote(mean, mean_out, msend, mrecv, {"tm_2": 1 - c})
    other.start()

    def copy(i):
        dz = 2 * c + i // 2
        return remote(cov.at[i], out.at[z], send.at[i], recv.at[z], {"state": dz, "tm_2": i % 2})

    def mine(i):
        return (z == 2 * c + i // 2) & (c == i % 2)

    for i in range(4):

        @pl.when(mine(i))
        def _():
            pltpu.make_async_copy(cov.at[i], out.at[z], local).start()

        @pl.when(jnp.logical_not(mine(i)))
        def _():
            copy(i).start()

    for i in range(4):

        @pl.when(mine(i))
        def _():
            pltpu.make_async_copy(cov.at[i], out.at[z], local).wait()

        @pl.when(jnp.logical_not(mine(i)))
        def _():
            copy(i).wait_send()

    source_core = z // 2
    for s in range(4):

        @pl.when(jnp.logical_not((z == s) & (c == source_core)))
        def _():
            remote(cov.at[0], out.at[s], send.at[0], recv.at[s], {"state": 0, "tm_2": 0}).wait_recv()

    other.wait()


def scatter_step_kernel(slabs, out, send, recv, local):
    z, c = lax.axis_index("state"), lax.axis_index("tm_2")
    greet(column_peers(z, c))
    core = z // 2
    slot = 2 * lax.rem(z, 2) + c

    def copy(t):
        return remote(slabs.at[t], out.at[slot], send.at[t], recv.at[slot], {"state": t, "tm_2": core})

    def mine(t):
        return (z == t) & (c == core)

    for t in range(4):

        @pl.when(mine(t))
        def _():
            pltpu.make_async_copy(slabs.at[t], out.at[slot], local).start()

        @pl.when(jnp.logical_not(mine(t)))
        def _():
            copy(t).start()

    for t in range(4):

        @pl.when(mine(t))
        def _():
            pltpu.make_async_copy(slabs.at[t], out.at[slot], local).wait()

        @pl.when(jnp.logical_not(mine(t)))
        def _():
            copy(t).wait_send()

    for i in range(4):

        @pl.when(jnp.logical_not((z == 2 * c + i // 2) & (c == i % 2)))
        def _():
            remote(slabs.at[0], out.at[i], send.at[0], recv.at[i], {"state": 0, "tm_2": 0}).wait_recv()


def swap_kernel(x, out, send, recv):
    peer = {"tm_2": 1 - lax.axis_index("tm_2")}
    greet([peer])
    copy = remote(x, out.at[0], send, recv, peer)
    copy.start()
    copy.wait()


class Copies:
    def __init__(self, out, send, recv):
        self.out, self.send, self.recv, self.used, self.sent = out, send, recv, 0, []

    def put(self, peer, slot, row, rows, src=None):
        n, self.used = self.used, self.used + 1
        place = self.out.at[slot, pl.ds(pl.multiple_of(row, 8), rows), :]
        copy = remote(place if src is None else src, place, self.send.at[n], self.recv.at[n], peer)
        copy.start()
        self.sent.append(copy)
        return n

    def arrived(self, n, slot, row, rows):
        place = self.out.at[slot, pl.ds(pl.multiple_of(row, 8), rows), :]
        remote(place, place, self.send.at[n], self.recv.at[n], {"tm_2": 0}).wait_recv()

    def finish(self):
        for copy in self.sent:
            copy.wait_send()


def gather_z_kernel(x, out, send, recv):
    z, c = lax.axis_index("state"), lax.axis_index("tm_2")
    up, down = {"state": lax.rem(z + 1, 4)}, {"state": lax.rem(z + 3, 4)}
    twin = {"tm_2": 1 - c}
    zu, zd, zo = lax.rem(z + 1, 4), lax.rem(z + 3, 4), lax.rem(z + 2, 4)
    greet([up, down, twin])
    cp = Copies(out, send, recv)
    q = HALF // 2
    mine, theirs = c * HALF, (1 - c) * HALF
    first, second = [], []
    for part in (0, 1):
        row = mine + part * q
        src = x.at[pl.ds(pl.multiple_of(row, 8), q), :]
        first.append(cp.put(up, z, row, q, src))
        row = mine + (1 - part) * q
        src = x.at[pl.ds(pl.multiple_of(row, 8), q), :]
        second.append(cp.put(down, z, row, q, src))
    tail = []
    twins = []
    for part in (0, 1):
        row = mine + part * q
        cp.arrived(first[part], zd, row, q)
        if part == 0:
            up_tail = cp.put(up, zd, row, q)
        twins.append((cp.put(twin, zd, row, q), zd, theirs + part * q))
        row = mine + (1 - part) * q
        cp.arrived(second[part], zu, row, q)
        if part == 0:
            down_tail = cp.put(down, zu, row, q)
        twins.append((cp.put(twin, zu, row, q), zu, theirs + (1 - part) * q))
    cp.arrived(up_tail, zo, mine, q)
    twins.append((cp.put(twin, zo, mine, q), zo, theirs))
    cp.arrived(down_tail, zo, mine + q, q)
    twins.append((cp.put(twin, zo, mine + q, q), zo, theirs + q))
    for n, slot, row in twins:
        cp.arrived(n, slot, row, q)
    cp.finish()


def gather_ring_kernel(axis, x, out, send, recv):
    z, c, a = lax.axis_index("state"), lax.axis_index("tm_2"), lax.axis_index(axis)
    zu, zd = lax.rem(z + 1, 4), lax.rem(z + 3, 4)
    zo = lax.rem(z + 2, 4)
    au, ad, ao = lax.rem(a + 1, 4), lax.rem(a + 3, 4), lax.rem(a + 2, 4)
    up, down = {axis: au}, {axis: ad}
    above, below, twin = {"state": zu}, {"state": zd}, {"tm_2": 1 - c}
    greet([up, down, above, below, twin])
    cp = Copies(out, send, recv)
    row = lambda quarter, core: quarter * (2 * SH) + core * SH
    h = SH // 2
    quarters = (z, zu)
    from_down, from_up = [], []
    for k, quarter in enumerate(quarters):
        r = row(quarter, c)
        src = x.at[pl.ds(pl.multiple_of(r, 8), SH), :]
        from_down.append(cp.put(up, a, r, SH, src))
        from_up.append(cp.put(down, a, r, SH, src))
    twins, zs, opp = [], [], []

    def spread(k, slot, off, rows):
        r = row(quarters[k], c) + off
        n = cp.put(above if k == 0 else below, slot, r, rows)
        zs.append((n, slot, row(zd if k == 0 else zo, c) + off, row(zd if k == 0 else zo, 1 - c) + off, rows))
        twins.append((cp.put(twin, slot, r, rows), slot, row(quarters[k], 1 - c) + off, rows))

    for k, quarter in enumerate(quarters):
        r = row(quarter, c)
        cp.arrived(from_down[k], ad, r, SH)
        opp.append((k, 0, cp.put(up, ad, r, h)))
        spread(k, ad, 0, SH)
        cp.arrived(from_up[k], au, r, SH)
        opp.append((k, h, cp.put(down, au, r + h, h)))
        spread(k, au, 0, SH)

    def take(entry):
        n, slot, r, r_twin, rows = entry
        cp.arrived(n, slot, r, rows)
        twins.append((cp.put(twin, slot, r, rows), slot, r_twin, rows))

    for k, off, n in opp:
        cp.arrived(n, ao, row(quarters[k], c) + off, h)
        spread(k, ao, off, h)
    for entry in zs:
        take(entry)
    for n, slot, r, rows in twins:
        cp.arrived(n, slot, r, rows)
    cp.finish()


def shape(*dims, dtype=F32):
    return jax.ShapeDtypeStruct(dims, dtype)


def params(limit=None, **more):
    return pltpu.CompilerParams(vmem_limit_bytes=limit, **more)


DMA = pltpu.SemaphoreType.DMA


def comm(kernel, name, collective_id, outs, scratch, *args, out_spec=ANY):
    return pl.pallas_call(
        kernel,
        name=name,
        out_shape=outs,
        in_specs=[ANY] * len(args),
        out_specs=jax.tree.map(lambda _: out_spec, outs),
        scratch_shapes=scratch,
        compiler_params=pltpu.CompilerParams(collective_id=collective_id, has_side_effects=True),
    )(*args)


BIG = 56 * 1024 * 1024
WORK = [
    pltpu.VMEM((512, 512), BF16),
    pltpu.VMEM((512, 512), BF16),
    pltpu.VMEM((512, 512), F32),
]


def scan(name, count, want_total, want_rest, ids, own, others):
    packet = shape(ROWS, N)
    return pl.pallas_call(
        partial(scan_kernel, count, want_total, want_rest),
        name=name,
        out_shape=[packet] * (want_total + want_rest),
        in_specs=[SM, VM, VM],
        out_specs=[VM] * (want_total + want_rest),
        scratch_shapes=[
            pltpu.VMEM((2, N, N), F32),
            pltpu.VMEM((2, N, N), F32),
            pltpu.VMEM((2, 8, N), F32),
            pltpu.VMEM((N, 2 * N), BF16),
            pltpu.VMEM((N, 2 * N), BF16),
        ]
        + WORK,
        compiler_params=params(BIG),
    )(ids, own, others)


def on_device(filtered_cov, filtered_mean, noise_var, trans_blocks, pattern):
    y, x, c, z = (lax.axis_index(a) for a in ("tm_0", "tm_1", "tm_2", "state"))
    cov, twin_mean = comm(
        gather_step_kernel,
        "gather_step",
        0,
        (shape(4, B, N), shape(4, N)),
        [DMA((4,)), DMA((4,)), DMA, DMA, DMA],
        filtered_cov,
        filtered_mean,
        out_spec=VM,
    )
    step = 8 * (4 * y + x) + 2 * z + c
    ids = jnp.stack([(z // 2 == c).astype(jnp.int32), lax.rem(2 * z + c, 4), (step != 127).astype(jnp.int32)])
    own = pl.pallas_call(
        element_kernel,
        name="element",
        out_shape=shape(ROWS, N),
        in_specs=[SM, SM] + [VM] * 5,
        out_specs=VM,
        scratch_shapes=[pltpu.VMEM((N, N), F32)] * 3 + [pltpu.VMEM((8, N), F32)],
        compiler_params=params(BIG),
    )(ids, pattern, cov.reshape(N, N), filtered_mean, twin_mean, noise_var.reshape(1, N), trans_blocks)
    twin = comm(swap_kernel, "swap", 1, shape(1, ROWS, N), [DMA, DMA], own)
    one = lambda v: v.reshape(1).astype(jnp.int32)
    (pair,) = scan("scan_core", 2, True, False, one(c), own, twin)
    pairs = comm(gather_z_kernel, "gather_z", 2, shape(4, ROWS, N), [DMA((12,)), DMA((12,))], pair)
    column, down = scan("scan_z", 4, True, True, one(z), pair, pairs)
    columns = comm(
        partial(gather_ring_kernel, "tm_1"), "gather_x", 3, shape(4, ROWS, N), [DMA((32,)), DMA((32,))], column
    )
    row, across = scan("scan_x", 4, True, True, one(x), column, columns)
    rows = comm(partial(gather_ring_kernel, "tm_0"), "gather_y", 4, shape(4, ROWS, N), [DMA((32,)), DMA((32,))], row)
    (later,) = scan("scan_y", 4, False, True, one(y), row, rows)
    slabs = pl.pallas_call(
        apply_kernel,
        name="apply",
        out_shape=shape(4, B + 8, N),
        in_specs=[SM] + [VM] * 5,
        out_specs=VM,
        scratch_shapes=[pltpu.VMEM((N, N), F32), pltpu.VMEM((8, N), F32), pltpu.VMEM((2, N, N), BF16)] + WORK,
        compiler_params=params(BIG),
    )(one(c), later, across, down, pair, own)
    out = comm(scatter_step_kernel, "scatter_step", 5, shape(4, B + 8, N), [DMA((4,)), DMA((4,)), DMA], slabs, out_spec=VM)
    smooth_mean = lax.dynamic_slice_in_dim(out[:, B, :], z * B, B, 1)
    return smooth_mean, out[:, :B, :]


def solution(mesh):
    torus = Mesh(
        mesh.devices.reshape(4, 4, 2, mesh.shape["state"]), ("tm_0", "tm_1", "tm_2", "state")
    )
    return jax.shard_map(
        on_device,
        mesh=torus,
        in_specs=(P(TM, "state", None), P(TM, None), P(), P(), P()),
        out_specs=(P(TM, "state"), P(TM, "state", None)),
        check_vma=False,
    )
```

time: 1080 us -> 295 us (0.27); the launches traced: 1060 us -> 294 us
  other arithmetic: 482 us -> 0.59 us
  Pallas kernels: 0 us -> 288 us
  waiting for transfers between devices: 265 us -> 0 us
  matrix products: 213 us -> 0 us
  local copies, waits for them, and re-layouts: 57.9 us -> 5.02 us
  blocking collectives: 30 us -> 0 us
  between operations: 15.1 us -> 0.72 us
    another operation x20 -> x1, other arithmetic: 472 us -> 0.59 us  [on_device(): jnp.stack([(z // 2 == c).astype(jnp.int32), lax.rem(2 * z + c, 4), (step...]
    pallas_call x0 -> x12, Pallas kernels: none -> 288 us  [the longest x6 145 us: comm(): pl.pallas_call(kernel, name=name, out_shape=outs, in_specs=[ANY] * len(ar...]
    all_gather x9 -> x0, waiting for transfers between devices: 264 us -> none  [the longest x6 124 us: prefix_by_axis(): pieces = jax.tree.map(lambda part: lax.all_gather(part, axis), subtotal)]
    dot_general x71 -> x0, matrix products: 189 us -> none  [the longest x17 54 us: compose(): jnp.dot(weighted, early_gain.T, precision=highest) + early_spread]
    all_gather x4 -> x0, blocking collectives: 30 us -> none  [the longest x3 21.9 us: prefix_by_axis(): pieces = jax.tree.map(lambda part: lax.all_gather(part, axis), subtotal)]
    another operation x20 -> x0, matrix products: 24 us -> none  [the longest x6 12.7 us: on_device(): factor = jnp.linalg.cholesky(predicted)]
    another operation x19 -> x0, local copies, waits for them, and re-layouts: 22.9 us -> none
  transfers between devices with their start and end apart: 9 -> 0, of which waited for: 8 -> 0; matrix products, arithmetic and copies ran while one was open for 8% -> 0% of each run, Pallas kernels for 0% -> 0%
where the time goes in v1:
time: 295 us; the launch traced here: 294 us
  Pallas kernels  288 us (98%)
  local copies, waits for them, and re-layouts  5.02 us (2%)
    pallas_call x6, Pallas kernels, comm(): pl.pallas_call(kernel, name=name, out_shape=outs, in_specs=[ANY] * len(ar...  145 us
    pallas_call x4, Pallas kernels, scan(): pl.pallas_call(partial(scan_kernel, count, want_total, want_rest), name=n...  76.6 us
    pallas_call x1, Pallas kernels, on_device(): pl.pallas_call(element_kernel, name='element', out_shape=shape(ROWS, N),...  47.8 us
    pallas_call x1, Pallas kernels, on_device(): pl.pallas_call(apply_kernel, name='apply', out_shape=shape(4, B + 8, N),...  18.1 us

profile of v1, /device:TPU:1, one launch (start us, length us, event | category | flops | bytes accessed | tf_op | source)
XLA Modules:
  0.0 294.3 jit_solution(14883050901515866531)
XLA Ops:
  0.7 0.6 pad_add_fusion.ids
  1.3 1.3 copy.7.pattern
  2.6 19.8 %gather_step.1 = (f32[4,128,512]{2,1,0:T(8,128)}, f32[4,512]{1,0:T(4,128)}) custom-call(f32[4,128,512]{2,1,0:T(8,128)} %cov.1, f32[4,512]{1,0:T(4,128)} %mean_a.1), custom_call_target="tpu_custom_call" | custom-call | tf_op jit(solution)/shard_map/gather_step/pallas_call | solution.py:504
  22.4 47.8 %element.1.x.own = f32[896,512]{1,0:T(8,128)} custom-call(s32[3]{0:T(128)} %pad_add_fusion.ids, s32[4,2]{1,0:T(4,128)} %copy.7.pattern, f32[512,512]{1,0:T(8,128)} %bitcast.10, f32[4,512]{1,0:T(4,128)} %mean_a.1, f32[4,512]{1,0:T(4,128)} %get-tuple-element.9.mean_b, f32[1,512]{1,0:T(1,128)} %bitcast.12, f32[4,2,128,128]{3,2,1,0:T(8,128)} %blocks.1), custom_call_target="tpu_custom_call" | custom-call | tf_op jit(solution)/shard_map/element/pallas_call | solution.py:557
  70.2 4.1 %swap.1.others = f32[1,896,512]{2,1,0:T(8,128)} custom-call(f32[896,512]{1,0:T(8,128)} %element.1.x.own), custom_call_target="tpu_custom_call" | custom-call | tf_op jit(solution)/shard_map/swap/pallas_call | solution.py:504
  74.4 8.9 %scan_core.1.x.own.pair = f32[896,512]{1,0:T(8,128)} custom-call(s32[1]{0:T(128)} %bitcast.ids, f32[896,512]{1,0:T(8,128)} %element.1.x.own, f32[1,896,512]{2,1,0:T(8,128)} %swap.1.others), custom_call_target="tpu_custom_call" | custom-call | tf_op jit(solution)/shard_map/scan_core/pallas_call | solution.py:525
  83.3 36.7 %gather_z.1.others = f32[4,896,512]{2,1,0:T(8,128)} custom-call(f32[896,512]{1,0:T(8,128)} %scan_core.1.x.own.pair), custom_call_target="tpu_custom_call" | custom-call | tf_op jit(solution)/shard_map/gather_z/pallas_call | solution.py:504
  120.0 22.7 %scan_z.1 = (f32[896,512]{1,0:T(8,128)}, f32[896,512]{1,0:T(8,128)}) custom-call(s32[1]{0:T(128)} %bitcast.3.ids, f32[896,512]{1,0:T(8,128)} %scan_core.1.x.own.pair, f32[4,896,512]{2,1,0:T(8,128)} %gather_z.1.others), custom_call_target="tpu_custom_call" | custom-call | tf_op jit(solution)/shard_map/scan_z/pallas_call | solution.py:525
  142.7 33.3 %gather_x.1.others = f32[4,896,512]{2,1,0:T(8,128)} custom-call(f32[896,512]{1,0:T(8,128)} %get-tuple-element.10.x.own), custom_call_target="tpu_custom_call" | custom-call | tf_op jit(solution)/shard_map/gather_x/pallas_call | solution.py:504
  176.0 22.8 %scan_x.1 = (f32[896,512]{1,0:T(8,128)}, f32[896,512]{1,0:T(8,128)}) custom-call(s32[1]{0:T(128)} %bitcast.2.ids, f32[896,512]{1,0:T(8,128)} %get-tuple-element.10.x.own, f32[4,896,512]{2,1,0:T(8,128)} %gather_x.1.others), custom_call_target="tpu_custom_call" | custom-call | tf_op jit(solution)/shard_map/scan_x/pallas_call | solution.py:525
  198.8 34.1 %gather_y.1.others = f32[4,896,512]{2,1,0:T(8,128)} custom-call(f32[896,512]{1,0:T(8,128)} %get-tuple-element.11.x.own), custom_call_target="tpu_custom_call" | custom-call | tf_op jit(solution)/shard_map/gather_y/pallas_call | solution.py:504
  232.9 22.2 %scan_y.1.later = f32[896,512]{1,0:T(8,128)} custom-call(s32[1]{0:T(128)} %bitcast.1.ids, f32[896,512]{1,0:T(8,128)} %get-tuple-element.11.x.own, f32[4,896,512]{2,1,0:T(8,128)} %gather_y.1.others), custom_call_target="tpu_custom_call" | custom-call | tf_op jit(solution)/shard_map/scan_y/pallas_call | solution.py:525
  255.1 18.1 %apply.1.slabs = f32[4,136,512]{2,1,0:T(8,128)} custom-call(s32[1]{0:T(128)} %bitcast.ids, f32[896,512]{1,0:T(8,128)} %scan_y.1.later, f32[896,512]{1,0:T(8,128)} %get-tuple-element.12.across, f32[896,512]{1,0:T(8,128)} %get-tuple-element.13.down, f32[896,512]{1,0:T(8,128)} %scan_core.1.x.own.pair, f32[896,512]{1,0:T(8,128)} %element.1.x.own), custom_call_target="tpu_custom_call" | custom-call | tf_op jit(solution)/shard_map/apply/pallas_call | solution.py:577
  273.1 17.4 %scatter_step.1 = f32[4,136,512]{2,1,0:T(8,128)} custom-call(f32[4,136,512]{2,1,0:T(8,128)} %apply.1.slabs), custom_call_target="tpu_custom_call" | custom-call | tf_op jit(solution)/shard_map/scatter_step/pallas_call | solution.py:504
  290.6 0.8 slice.6
  291.4 2.3 slice.7
  293.7 0.6 constant_dynamic-slice_fusion

commit v2 on v1

--- a/solution.py
+++ b/solution.py
@@ -41,6 +41,12 @@
     return dot_s(split(a), split(b), cb)
 
 
+def dot6(a, b, cb=0, ca=1):
+    return lax.dot_general(
+        a, b, (((ca,), (cb,)), ((), ())), precision=lax.Precision.HIGHEST, preferred_element_type=F32
+    )
+
+
 def packed_blocks():
     out = []
     for j in range(4):
@@ -67,43 +73,82 @@
             full_ref[j * B : j * B + B, i * B : i * B + B] = jnp.transpose(block)
 
 
+def small_mul(a, b):
+    return [
+        [sum((a[i][t] * b[t][j] for t in range(1, len(b))), a[i][0] * b[0][j]) for j in range(len(b[0]))]
+        for i in range(len(a))
+    ]
+
+
+def small_inverse(m):
+    n = len(m)
+    if n == 2:
+        a, b, d = m[0][0], m[0][1], m[1][1]
+        inv = 1.0 / (a * d - b * b)
+        return [[d * inv, -b * inv], [-b * inv, a * inv]]
+    h = n // 2
+    upper = [row[h:] for row in m[:h]]
+    lower = [[upper[j][i] for j in range(h)] for i in range(h)]
+    first = small_inverse([row[:h] for row in m[:h]])
+    q = small_mul(lower, first)
+    qb = small_mul(q, upper)
+    schur = [[m[h + min(i, j)][h + max(i, j)] - qb[min(i, j)][max(i, j)] for j in range(h)] for i in range(h)]
+    second = small_inverse(schur)
+    sq = small_mul(second, q)
+    qsq = small_mul([[q[j][i] for j in range(h)] for i in range(h)], sq)
+    out = [[None] * n for _ in range(n)]
+    for i in range(h):
+        for j in range(h):
+            out[i][j] = first[i][j] + qsq[i][j]
+            out[h + i][h + j] = second[i][j]
+            out[h + i][j] = out[j][h + i] = -sq[i][j]
+    return out
+
+
+PANEL = 64
+
+
 def inverse128(block):
+    groups = PANEL // 8
     row_id = lax.broadcasted_iota(jnp.int32, (8, B), 0)
     lane_id = lax.broadcasted_iota(jnp.int32, (8, B), 1)
-    vs = tuple(block[8 * b : 8 * b + 8, :] for b in range(16))
-
-    def body(_, vs):
-        vs = list(vs)
-        for i in range(0, 8, 2):
-            r0 = jnp.broadcast_to(vs[0][i : i + 1, :], (8, B))
-            r1 = jnp.broadcast_to(vs[0][i + 1 : i + 2, :], (8, B))
-            c0 = [jnp.broadcast_to(v[:, i : i + 1], (8, B)) for v in vs]
-            c1 = [jnp.broadcast_to(v[:, i + 1 : i + 2], (8, B)) for v in vs]
-            a = jnp.broadcast_to(c0[0][i : i + 1, :], (8, B))
-            b = jnp.broadcast_to(c0[0][i + 1 : i + 2, :], (8, B))
-            d = jnp.broadcast_to(c1[0][i + 1 : i + 2, :], (8, B))
-            inv = 1.0 / (a * d - b * b)
-            ia, ib, idd = d * inv, -b * inv, a * inv
-            is0, is1 = lane_id == i, lane_id == i + 1
-            n0 = ia * r0 + ib * r1
-            n1 = ib * r0 + idd * r1
-            n0 = jnp.where(is0, -ia, jnp.where(is1, -ib, n0))
-            n1 = jnp.where(is0, -ib, jnp.where(is1, -idd, n1))
-            for k in range(16):
-                base = jnp.where(is0 | is1, 0.0, vs[k])
-                new = base - (c0[k] * n0 + c1[k] * n1)
-                if k == 0:
-                    new = jnp.where(row_id == i, n0, jnp.where(row_id == i + 1, n1, new))
+    lanes = lax.broadcasted_iota(jnp.int32, (B, B), 1)
+
+    def body(_, x):
+        top = x[:PANEL, :]
+        vs = [x[8 * k : 8 * k + 8, :] for k in range(groups)]
+        for q in range(groups):
+            at = 8 * q
+            cols = [[jnp.broadcast_to(v[:, at + s : at + s + 1], (8, B)) for v in vs] for s in range(8)]
+            rows = [jnp.broadcast_to(vs[q][s : s + 1, :], (8, B)) for s in range(8)]
+            m = [[None] * 8 for _ in range(8)]
+            for s in range(8):
+                for t in range(s, 8):
+                    m[s][t] = m[t][s] = jnp.broadcast_to(cols[s][q][t : t + 1, :], (8, B))
+            inv = small_inverse(m)
+            new_rows = [n[0] for n in small_mul(inv, [[r] for r in rows])]
+            for s in range(8):
+                for t in range(8):
+                    new_rows[s] = jnp.where(lane_id == at + t, -inv[s][t], new_rows[s])
+            inside = (lane_id >= at) & (lane_id < at + 8)
+            for k in range(groups):
+                if k == q:
+                    new = new_rows[0]
+                    for s in range(1, 8):
+                        new = jnp.where(row_id == s, new_rows[s], new)
+                else:
+                    new = jnp.where(inside, 0.0, vs[k])
+                    new -= sum((cols[s][k] * new_rows[s] for s in range(1, 8)), cols[0][k] * new_rows[0])
                 vs[k] = new
-        vs = [pltpu.roll(v, B - 8, 1) for v in vs]
-        return tuple(vs[1:] + vs[:1])
-
-    vs = lax.fori_loop(0, 16, body, vs)
-    return -jnp.concatenate(vs, axis=0)
+        done = jnp.concatenate(vs, axis=0)
+        rest = jnp.where(lanes < PANEL, 0.0, x) - dot6(top, done, 0, 0)
+        return pltpu.roll(jnp.concatenate([rest[PANEL:, :], done], axis=0), B - PANEL, 1)
+
+    return -lax.fori_loop(0, B // PANEL, body, block)
 
 
 def element_kernel(ids, pattern, cov, mean_a, mean_b, noise, blocks, out, left, pred, sol, upd):
-    tb = lambda r, j: split(blocks[r, j])
+    tb = lambda r, j: blocks[r, j]
 
     def rows_of(ref, block):
         return ref[pl.ds(pl.multiple_of(block * B, B), B), :]
@@ -116,19 +161,19 @@
     pushed = []
     for r in range(4):
         t0, t1 = tb(r, 0), tb(r, 1)
-        left[r * B : r * B + B, :] = dot_s(t0, split(rows_of(cov, pattern[r, 0]))) + dot_s(
-            t1, split(rows_of(cov, pattern[r, 1]))
+        left[r * B : r * B + B, :] = dot6(t0, rows_of(cov, pattern[r, 0])) + dot6(
+            t1, rows_of(cov, pattern[r, 1])
         )
         pushed.append(
-            dot_s(split(lanes_of(upd, 0, 8, pattern[r, 0])), t0, 1)
-            + dot_s(split(lanes_of(upd, 0, 8, pattern[r, 1])), t1, 1)
+            dot6(lanes_of(upd, 0, 8, pattern[r, 0]), t0, 1)
+            + dot6(lanes_of(upd, 0, 8, pattern[r, 1]), t1, 1)
         )
     pushed = jnp.concatenate(pushed, axis=1)
     eye = lax.broadcasted_iota(jnp.int32, (B, B), 0) == lax.broadcasted_iota(jnp.int32, (B, B), 1)
     for r in range(4):
         rows = (r + 1) * B
-        value = dot_s(split(lanes_of(left, 0, rows, pattern[r, 0])), tb(r, 0), 1) + dot_s(
-            split(lanes_of(left, 0, rows, pattern[r, 1])), tb(r, 1), 1
+        value = dot6(lanes_of(left, 0, rows, pattern[r, 0]), tb(r, 0), 1) + dot6(
+            lanes_of(left, 0, rows, pattern[r, 1]), tb(r, 1), 1
         )
         pred[0:rows, r * B : r * B + B] = value
         q = jnp.where(eye, jnp.broadcast_to(noise[0:1, r * B : r * B + B], (B, B)), 0.0)
@@ -136,35 +181,28 @@
     sol[...] = left[...]
     for k in range(4):
         k0, k1 = k * B, k * B + B
-        inv = split(inverse128(pred[k0:k1, k0:k1]))
-        rhs = split(sol[k0:k1, :])
-        ub = dot_s(inv, rhs)
+        inv = inverse128(pred[k0:k1, k0:k1])
+        ub = dot6(inv, sol[k0:k1, :])
         sol[k0:k1, :] = ub
         if k < 3:
-            ubs = split(ub)
             tail = pred[k0:k1, k1:]
-            ut = dot_s(inv, split(tail))
-            uts = split(ut)
-            st = split(jnp.transpose(tail))
-            pred[k1:, k1:] -= dot_s(st, uts)
-            sol[k1:, :] -= dot_s(st, ubs)
+            ut = dot6(inv, tail)
+            st = jnp.transpose(tail)
+            pred[k1:, k1:] -= dot6(st, ut)
+            sol[k1:, :] -= dot6(st, ub)
             pred[k0:k1, k1:] = ut
     for k in (2, 1, 0):
         k0, k1 = k * B, k * B + B
-        sol[k0:k1, :] -= dot3(pred[k0:k1, k1:], sol[k1:, :])
+        sol[k0:k1, :] -= dot6(pred[k0:k1, k1:], sol[k1:, :])
     keep = ids[2].astype(F32)
     for i in range(4):
         for j in range(4):
             out[i * B : i * B + B, j * B : j * B + B] = (
                 jnp.transpose(sol[j * B : j * B + B, i * B : i * B + B]) * keep
             )
-    out[GROW : GROW + 8, :] = jnp.broadcast_to(mean, (8, N)) - keep * dot3(pushed, sol[...])
+    out[GROW : GROW + 8, :] = jnp.broadcast_to(mean, (8, N)) - keep * dot6(pushed, sol[...])
     out[GROW + 8 :, :] = jnp.zeros((ROWS - GROW - 8, N), F32)
-    ls = split(left[...])
-    for i in range(4):
-        pred[i * B : i * B + B, :] = cov[i * B : i * B + B, :] - dot_s(
-            split(out[i * B : i * B + B, :]), ls
-        )
+    pred[...] = cov[...] - dot6(out[0:N, :], left[...])
     pack_spread(out, lambda r, n, c: pred[r : r + n, c : c + B])
 
 
@@ -219,14 +257,10 @@
         unpack_spread(lambda r, n, c: load(k, r, n, c, B), lk)
         sg[new] = dot_s(split(sg[now]), (eh[...], el[...]), 1) + load(k, GROW, 8)
 
-        def rows_step(r, _):
-            rows = pl.ds(pl.multiple_of(r * B, B), B)
-            both = dot_s((eh[rows, :], el[rows, :]), (rh[...], rl[...]))
-            se[new, rows, :] = both[:, :N]
-            sl[new, rows, :] = dot_s(split(both[:, N:]), (eh[...], el[...]), 1) + lk[rows, :]
-            return 0
-
-        lax.fori_loop(0, 4, rows_step, 0)
+        e = (eh[...], el[...])
+        se[new] = dot_s(e, (rh[:, :N], rl[:, :N]))
+        half = split(dot_s(e, (rh[:, N:], rl[:, N:])))
+        sl[new] = dot_s(half, e, 1) + lk[...]
         return 0
 
     steps = count - 1
@@ -251,13 +285,8 @@
         unpack_spread(lambda r, n, c: load(r, n, c, B), lk)
         mean[...] = dot_s(split(mean[...]), (eh[...], el[...]), 1) + load(GROW, 8)
 
-        def rows_step(r, _):
-            rows = pl.ds(pl.multiple_of(r * B, B), B)
-            half = dot_s((eh[rows, :], el[rows, :]), (w[0], w[1]))
-            cov[rows, :] = dot_s(split(half), (eh[...], el[...]), 1) + lk[rows, :]
-            return 0
-
-        lax.fori_loop(0, 4, rows_step, 0)
+        e = (eh[...], el[...])
+        cov[...] = dot_s(split(dot_s(e, (w[0], w[1]))), e, 1) + lk[...]
 
     push(lambda r, n, c=0, m=N: across[r : r + n, c : c + m])
     push(lambda r, n, c=0, m=N: down[r : r + n, c : c + m])
@@ -407,83 +436,94 @@
     zu, zd, zo = lax.rem(z + 1, 4), lax.rem(z + 3, 4), lax.rem(z + 2, 4)
     greet([up, down, twin])
     cp = Copies(out, send, recv)
-    q = HALF // 2
+    parts, q = 4, HALF // 4
     mine, theirs = c * HALF, (1 - c) * HALF
-    first, second = [], []
-    for part in (0, 1):
-        row = mine + part * q
-        src = x.at[pl.ds(pl.multiple_of(row, 8), q), :]
-        first.append(cp.put(up, z, row, q, src))
-        row = mine + (1 - part) * q
-        src = x.at[pl.ds(pl.multiple_of(row, 8), q), :]
-        second.append(cp.put(down, z, row, q, src))
-    tail = []
-    twins = []
-    for part in (0, 1):
-        row = mine + part * q
-        cp.arrived(first[part], zd, row, q)
-        if part == 0:
-            up_tail = cp.put(up, zd, row, q)
-        twins.append((cp.put(twin, zd, row, q), zd, theirs + part * q))
-        row = mine + (1 - part) * q
-        cp.arrived(second[part], zu, row, q)
-        if part == 0:
-            down_tail = cp.put(down, zu, row, q)
-        twins.append((cp.put(twin, zu, row, q), zu, theirs + (1 - part) * q))
-    cp.arrived(up_tail, zo, mine, q)
-    twins.append((cp.put(twin, zo, mine, q), zo, theirs))
-    cp.arrived(down_tail, zo, mine + q, q)
-    twins.append((cp.put(twin, zo, mine + q, q), zo, theirs + q))
+    ups, downs, tails, twins = [], [], [], []
+
+    def source(row):
+        return x.at[pl.ds(pl.multiple_of(row, 8), q), :]
+
+    for j in range(parts):
+        row = mine + j * q
+        ups.append((cp.put(up, z, row, q, source(row)), j))
+        row = mine + (parts - 1 - j) * q
+        downs.append((cp.put(down, z, row, q, source(row)), parts - 1 - j))
+
+    def hand(slot, j):
+        twins.append((cp.put(twin, slot, mine + j * q, q), slot, theirs + j * q))
+
+    for (nu, ju), (nd, jd) in zip(ups, downs):
+        cp.arrived(nu, zd, mine + ju * q, q)
+        if ju < parts // 2:
+            tails.append((cp.put(up, zd, mine + ju * q, q), ju))
+        hand(zd, ju)
+        cp.arrived(nd, zu, mine + jd * q, q)
+        if jd >= parts // 2:
+            tails.append((cp.put(down, zu, mine + jd * q, q), jd))
+        hand(zu, jd)
+    for n, j in tails:
+        cp.arrived(n, zo, mine + j * q, q)
+        hand(zo, j)
     for n, slot, row in twins:
         cp.arrived(n, slot, row, q)
     cp.finish()
 
 
+PIECES = ((0, 56), (56, 56))
+
+
 def gather_ring_kernel(axis, x, out, send, recv):
     z, c, a = lax.axis_index("state"), lax.axis_index("tm_2"), lax.axis_index(axis)
-    zu, zd = lax.rem(z + 1, 4), lax.rem(z + 3, 4)
-    zo = lax.rem(z + 2, 4)
+    zu, zd, zo = lax.rem(z + 1, 4), lax.rem(z + 3, 4), lax.rem(z + 2, 4)
     au, ad, ao = lax.rem(a + 1, 4), lax.rem(a + 3, 4), lax.rem(a + 2, 4)
     up, down = {axis: au}, {axis: ad}
     above, below, twin = {"state": zu}, {"state": zd}, {"tm_2": 1 - c}
     greet([up, down, above, below, twin])
     cp = Copies(out, send, recv)
     row = lambda quarter, core: quarter * (2 * SH) + core * SH
-    h = SH // 2
     quarters = (z, zu)
-    from_down, from_up = [], []
-    for k, quarter in enumerate(quarters):
-        r = row(quarter, c)
-        src = x.at[pl.ds(pl.multiple_of(r, 8), SH), :]
-        from_down.append(cp.put(up, a, r, SH, src))
-        from_up.append(cp.put(down, a, r, SH, src))
-    twins, zs, opp = [], [], []
-
-    def spread(k, slot, off, rows):
+    coming = (zd, zo)
+    pieces = len(PIECES)
+    order_up = list(range(pieces))
+    order_down = order_up[::-1]
+    ups, downs, twins, zs, tails = [], [], [], [], []
+    for ju, jd in zip(order_up, order_down):
+        for k in (0, 1):
+            for into, peer, j in ((ups, up, ju), (downs, down, jd)):
+                off, rows = PIECES[j]
+                r = row(quarters[k], c) + off
+                into.append((cp.put(peer, a, r, rows, x.at[pl.ds(pl.multiple_of(r, 8), rows), :]), k, j))
+
+    def spread(k, slot, j):
+        off, rows = PIECES[j]
         r = row(quarters[k], c) + off
-        n = cp.put(above if k == 0 else below, slot, r, rows)
-        zs.append((n, slot, row(zd if k == 0 else zo, c) + off, row(zd if k == 0 else zo, 1 - c) + off, rows))
+        zs.append((cp.put(below if k else above, slot, r, rows), slot, k, j))
         twins.append((cp.put(twin, slot, r, rows), slot, row(quarters[k], 1 - c) + off, rows))
 
-    for k, quarter in enumerate(quarters):
-        r = row(quarter, c)
-        cp.arrived(from_down[k], ad, r, SH)
-        opp.append((k, 0, cp.put(up, ad, r, h)))
-        spread(k, ad, 0, SH)
-        cp.arrived(from_up[k], au, r, SH)
-        opp.append((k, h, cp.put(down, au, r + h, h)))
-        spread(k, au, 0, SH)
-
-    def take(entry):
-        n, slot, r, r_twin, rows = entry
-        cp.arrived(n, slot, r, rows)
-        twins.append((cp.put(twin, slot, r, rows), slot, r_twin, rows))
-
-    for k, off, n in opp:
-        cp.arrived(n, ao, row(quarters[k], c) + off, h)
-        spread(k, ao, off, h)
-    for entry in zs:
-        take(entry)
+    def take(count):
+        while len(zs) > count:
+            n, slot, k, j = zs.pop(0)
+            off, rows = PIECES[j]
+            r = row(coming[k], c) + off
+            cp.arrived(n, slot, r, rows)
+            twins.append((cp.put(twin, slot, r, rows), slot, row(coming[k], 1 - c) + off, rows))
+
+    for (nu, k, ju), (nd, _, jd) in zip(ups, downs):
+        off, rows = PIECES[ju]
+        cp.arrived(nu, ad, row(quarters[k], c) + off, rows)
+        if ju < pieces // 2:
+            tails.append((cp.put(up, ad, row(quarters[k], c) + off, rows), k, ju))
+        spread(k, ad, ju)
+        off, rows = PIECES[jd]
+        cp.arrived(nd, au, row(quarters[k], c) + off, rows)
+        if jd >= pieces // 2:
+            tails.append((cp.put(down, au, row(quarters[k], c) + off, rows), k, jd))
+        spread(k, au, jd)
+    for n, k, j in tails:
+        off, rows = PIECES[j]
+        cp.arrived(n, ao, row(quarters[k], c) + off, rows)
+        spread(k, ao, j)
+    take(0)
     for n, slot, r, rows in twins:
         cp.arrived(n, slot, r, rows)
     cp.finish()
@@ -566,13 +606,13 @@
     twin = comm(swap_kernel, "swap", 1, shape(1, ROWS, N), [DMA, DMA], own)
     one = lambda v: v.reshape(1).astype(jnp.int32)
     (pair,) = scan("scan_core", 2, True, False, one(c), own, twin)
-    pairs = comm(gather_z_kernel, "gather_z", 2, shape(4, ROWS, N), [DMA((12,)), DMA((12,))], pair)
+    pairs = comm(gather_z_kernel, "gather_z", 2, shape(4, ROWS, N), [DMA((24,)), DMA((24,))], pair)
     column, down = scan("scan_z", 4, True, True, one(z), pair, pairs)
     columns = comm(
-        partial(gather_ring_kernel, "tm_1"), "gather_x", 3, shape(4, ROWS, N), [DMA((32,)), DMA((32,))], column
+        partial(gather_ring_kernel, "tm_1"), "gather_x", 3, shape(4, ROWS, N), [DMA((48,)), DMA((48,))], column
     )
     row, across = scan("scan_x", 4, True, True, one(x), column, columns)
-    rows = comm(partial(gather_ring_kernel, "tm_0"), "gather_y", 4, shape(4, ROWS, N), [DMA((32,)), DMA((32,))], row)
+    rows = comm(partial(gather_ring_kernel, "tm_0"), "gather_y", 4, shape(4, ROWS, N), [DMA((48,)), DMA((48,))], row)
     (later,) = scan("scan_y", 4, False, True, one(y), row, rows)
     slabs = pl.pallas_call(
         apply_kernel,

time: 295 us -> 245 us (0.83); the launches traced: 294 us -> 241 us
  Pallas kernels: 288 us -> 234 us
    pallas_call x4, Pallas kernels: 76.6 us -> 48.8 us  [scan(): pl.pallas_call(partial(scan_kernel, count, want_total, want_rest), name=n...]
    pallas_call x1, Pallas kernels: 47.8 us -> 38.5 us  [on_device(): pl.pallas_call(element_kernel, name='element', out_shape=shape(ROWS, N),...]
    pallas_call x6, Pallas kernels: 145 us -> 136 us  [comm(): pl.pallas_call(kernel, name=name, out_shape=outs, in_specs=[ANY] * len(ar...]
    pallas_call x1, Pallas kernels: 18.1 us -> 11 us  [on_device(): pl.pallas_call(apply_kernel, name='apply', out_shape=shape(4, B + 8, N),...]
where the time goes in v2:
time: 245 us; the launch traced here: 241 us
  Pallas kernels  234 us (96%)
  local copies, waits for them, and re-layouts  5.02 us (2%)
    pallas_call x6, Pallas kernels, comm(): pl.pallas_call(kernel, name=name, out_shape=outs, in_specs=[ANY] * len(ar...  136 us
    pallas_call x4, Pallas kernels, scan(): pl.pallas_call(partial(scan_kernel, count, want_total, want_rest), name=n...  48.8 us
    pallas_call x1, Pallas kernels, on_device(): pl.pallas_call(element_kernel, name='element', out_shape=shape(ROWS, N),...  38.5 us
    pallas_call x1, Pallas kernels, on_device(): pl.pallas_call(apply_kernel, name='apply', out_shape=shape(4, B + 8, N),...  11 us

profile of v2, /device:TPU:1, one launch (start us, length us, event | category | flops | bytes accessed | tf_op | source)
XLA Modules:
  0.0 241.2 jit_solution(8302469012521479043)
XLA Ops:
  0.7 0.6 pad_add_fusion.ids
  1.3 1.3 copy.7.pattern
  2.6 19.8 %gather_step.1 = (f32[4,128,512]{2,1,0:T(8,128)}, f32[4,512]{1,0:T(4,128)}) custom-call(f32[4,128,512]{2,1,0:T(8,128)} %cov.1, f32[4,512]{1,0:T(4,128)} %mean_a.1), custom_call_target="tpu_custom_call" | custom-call | tf_op jit(solution)/shard_map/gather_step/pallas_call | solution.py:544
  22.4 38.5 %element.1.x.own = f32[896,512]{1,0:T(8,128)} custom-call(s32[3]{0:T(128)} %pad_add_fusion.ids, s32[4,2]{1,0:T(4,128)} %copy.7.pattern, f32[512,512]{1,0:T(8,128)} %bitcast.10, f32[4,512]{1,0:T(4,128)} %mean_a.1, f32[4,512]{1,0:T(4,128)} %get-tuple-element.9.mean_b, f32[1,512]{1,0:T(1,128)} %bitcast.12, f32[4,2,128,128]{3,2,1,0:T(8,128)} %blocks.1), custom_call_target="tpu_custom_call" | custom-call | tf_op jit(solution)/shard_map/element/pallas_call | solution.py:597
  60.9 4.1 %swap.1.others = f32[1,896,512]{2,1,0:T(8,128)} custom-call(f32[896,512]{1,0:T(8,128)} %element.1.x.own), custom_call_target="tpu_custom_call" | custom-call | tf_op jit(solution)/shard_map/swap/pallas_call | solution.py:544
  65.0 6.4 %scan_core.1.x.own.pair = f32[896,512]{1,0:T(8,128)} custom-call(s32[1]{0:T(128)} %bitcast.ids, f32[896,512]{1,0:T(8,128)} %element.1.x.own, f32[1,896,512]{2,1,0:T(8,128)} %swap.1.others), custom_call_target="tpu_custom_call" | custom-call | tf_op jit(solution)/shard_map/scan_core/pallas_call | solution.py:565
  71.4 36.2 %gather_z.1.others = f32[4,896,512]{2,1,0:T(8,128)} custom-call(f32[896,512]{1,0:T(8,128)} %scan_core.1.x.own.pair), custom_call_target="tpu_custom_call" | custom-call | tf_op jit(solution)/shard_map/gather_z/pallas_call | solution.py:544
  107.7 14.5 %scan_z.1 = (f32[896,512]{1,0:T(8,128)}, f32[896,512]{1,0:T(8,128)}) custom-call(s32[1]{0:T(128)} %bitcast.3.ids, f32[896,512]{1,0:T(8,128)} %scan_core.1.x.own.pair, f32[4,896,512]{2,1,0:T(8,128)} %gather_z.1.others), custom_call_target="tpu_custom_call" | custom-call | tf_op jit(solution)/shard_map/scan_z/pallas_call | solution.py:565
  122.2 28.7 %gather_x.1.others = f32[4,896,512]{2,1,0:T(8,128)} custom-call(f32[896,512]{1,0:T(8,128)} %get-tuple-element.10.x.own), custom_call_target="tpu_custom_call" | custom-call | tf_op jit(solution)/shard_map/gather_x/pallas_call | solution.py:544
  150.8 14.8 %scan_x.1 = (f32[896,512]{1,0:T(8,128)}, f32[896,512]{1,0:T(8,128)}) custom-call(s32[1]{0:T(128)} %bitcast.2.ids, f32[896,512]{1,0:T(8,128)} %get-tuple-element.10.x.own, f32[4,896,512]{2,1,0:T(8,128)} %gather_x.1.others), custom_call_target="tpu_custom_call" | custom-call | tf_op jit(solution)/shard_map/scan_x/pallas_call | solution.py:565
  165.6 29.5 %gather_y.1.others = f32[4,896,512]{2,1,0:T(8,128)} custom-call(f32[896,512]{1,0:T(8,128)} %get-tuple-element.11.x.own), custom_call_target="tpu_custom_call" | custom-call | tf_op jit(solution)/shard_map/gather_y/pallas_call | solution.py:544
  195.2 13.1 %scan_y.1.later = f32[896,512]{1,0:T(8,128)} custom-call(s32[1]{0:T(128)} %bitcast.1.ids, f32[896,512]{1,0:T(8,128)} %get-tuple-element.11.x.own, f32[4,896,512]{2,1,0:T(8,128)} %gather_y.1.others), custom_call_target="tpu_custom_call" | custom-call | tf_op jit(solution)/shard_map/scan_y/pallas_call | solution.py:565
  208.3 11.0 %apply.1.slabs = f32[4,136,512]{2,1,0:T(8,128)} custom-call(s32[1]{0:T(128)} %bitcast.ids, f32[896,512]{1,0:T(8,128)} %scan_y.1.later, f32[896,512]{1,0:T(8,128)} %get-tuple-element.12.across, f32[896,512]{1,0:T(8,128)} %get-tuple-element.13.down, f32[896,512]{1,0:T(8,128)} %scan_core.1.x.own.pair, f32[896,512]{1,0:T(8,128)} %element.1.x.own), custom_call_target="tpu_custom_call" | custom-call | tf_op jit(solution)/shard_map/apply/pallas_call | solution.py:617
  219.3 17.8 %scatter_step.1 = f32[4,136,512]{2,1,0:T(8,128)} custom-call(f32[4,136,512]{2,1,0:T(8,128)} %apply.1.slabs), custom_call_target="tpu_custom_call" | custom-call | tf_op jit(solution)/shard_map/scatter_step/pallas_call | solution.py:544
  237.1 0.8 slice.6
  237.9 2.3 slice.7
  240.2 0.6 constant_dynamic-slice_fusion

commit v3 on v2

--- a/solution.py
+++ b/solution.py
@@ -13,7 +13,8 @@
 LROW = 512
 GROW = 832
 ROWS = 896
-HALF = ROWS // 2
+HALF = 424
+PARTS = ((0, 112), (112, 104), (216, 104), (320, 104))
 SH = ROWS // 8
 MESH = pl.DeviceIdType.MESH
 F32 = jnp.float32
@@ -147,7 +148,14 @@
     return -lax.fori_loop(0, B // PANEL, body, block)
 
 
-def element_kernel(ids, pattern, cov, mean_a, mean_b, noise, blocks, out, left, pred, sol, upd):
+def element_kernel(pattern, cov_in, mean_a, mean_b, noise, blocks, out, left, pred, sol, upd, cov, inv_ref):
+    y, x, c, z = (lax.axis_index(a) for a in ("tm_0", "tm_1", "tm_2", "state"))
+    for i in range(4):
+        for t in range(3):
+            lanes = slice((i + t) % 4 * B, (i + t) % 4 * B + B)
+            cov[i * B : i * B + B, lanes] = cov_in[i, :, lanes]
+        j = (i + 3) % 4
+        cov[i * B : i * B + B, j * B : j * B + B] = jnp.transpose(cov_in[j, :, i * B : i * B + B])
     tb = lambda r, j: blocks[r, j]
 
     def rows_of(ref, block):
@@ -156,7 +164,8 @@
     def lanes_of(ref, row, rows, block):
         return ref[row : row + rows, pl.ds(pl.multiple_of(block * B, B), B)]
 
-    mean = jnp.where(ids[0] == 1, mean_a[pl.ds(ids[1], 1), :], mean_b[pl.ds(ids[1], 1), :])
+    place = lax.rem(2 * z + c, 4)
+    mean = jnp.where(z // 2 == c, mean_a[pl.ds(place, 1), :], mean_b[pl.ds(place, 1), :])
     upd[0:8, :] = jnp.broadcast_to(mean, (8, N))
     pushed = []
     for r in range(4):
@@ -179,22 +188,33 @@
         q = jnp.where(eye, jnp.broadcast_to(noise[0:1, r * B : r * B + B], (B, B)), 0.0)
         pred[r * B : rows, r * B : r * B + B] += q
     sol[...] = left[...]
-    for k in range(4):
-        k0, k1 = k * B, k * B + B
-        inv = inverse128(pred[k0:k1, k0:k1])
-        ub = dot6(inv, sol[k0:k1, :])
-        sol[k0:k1, :] = ub
-        if k < 3:
-            tail = pred[k0:k1, k1:]
-            ut = dot6(inv, tail)
-            st = jnp.transpose(tail)
-            pred[k1:, k1:] -= dot6(st, ut)
-            sol[k1:, :] -= dot6(st, ub)
-            pred[k0:k1, k1:] = ut
+
+    def eliminate(k, _):
+        at = pl.ds(pl.multiple_of(k * B, B), B)
+        inv_ref[...] = inverse128(pred[at, at])
+        for kk in range(4):
+
+            @pl.when(k == kk)
+            def _():
+                k0, k1 = kk * B, kk * B + B
+                inv = inv_ref[...]
+                ub = dot6(inv, sol[k0:k1, :])
+                sol[k0:k1, :] = ub
+                if kk < 3:
+                    tail = pred[k0:k1, k1:]
+                    ut = dot6(inv, tail)
+                    st = jnp.transpose(tail)
+                    pred[k1:, k1:] -= dot6(st, ut)
+                    sol[k1:, :] -= dot6(st, ub)
+                    pred[k0:k1, k1:] = ut
+
+        return 0
+
+    lax.fori_loop(0, 4, eliminate, 0)
     for k in (2, 1, 0):
         k0, k1 = k * B, k * B + B
         sol[k0:k1, :] -= dot6(pred[k0:k1, k1:], sol[k1:, :])
-    keep = ids[2].astype(F32)
+    keep = (8 * (4 * y + x) + 2 * z + c != 127).astype(F32)
     for i in range(4):
         for j in range(4):
             out[i * B : i * B + B, j * B : j * B + B] = (
@@ -206,10 +226,10 @@
     pack_spread(out, lambda r, n, c: pred[r : r + n, c : c + B])
 
 
-def scan_kernel(count, want_total, want_rest, ids, own, others, *refs):
+def scan_kernel(axis, count, want_total, want_rest, own, others, *refs):
     outs, (se, sl, sg, rh, rl, eh, el, lk) = refs[: want_total + want_rest], refs[want_total + want_rest :]
     rest_ref = outs[-1]
-    me = ids[0]
+    me = lax.axis_index(axis)
 
     def load(k, row, rows, lane=0, lanes=N):
         slot = k if count > 2 else 0
@@ -271,29 +291,42 @@
         lax.fori_loop(0, steps, step, 0)
 
 
-def apply_kernel(ids, later, across, down, pair, own, out, cov, mean, w, eh, el, lk):
+def apply_kernel(later, across, down, pair, own, out, mean_out, cov, mean, add, w, eh, el, lk):
     unpack_spread(lambda r, n, c: later[r : r + n, c : c + B], cov)
     mean[...] = later[GROW : GROW + 8, :]
 
-    def push(load):
+    def take(load):
         for r in range(4):
             rows = slice(r * B, r * B + B)
             h, l = split(load(r * B, B))
             eh[rows, :], el[rows, :] = h, l
+        unpack_spread(lambda r, n, c: load(r, n, c, B), lk)
+        add[...] = load(GROW, 8)
+
+    loads = (
+        lambda r, n, c=0, m=N: across[r : r + n, c : c + m],
+        lambda r, n, c=0, m=N: down[r : r + n, c : c + m],
+        lambda r, n, c=0, m=N: jnp.where(
+            lax.axis_index("tm_2") == 0, pair[r : r + n, c : c + m], own[r : r + n, c : c + m]
+        ),
+    )
+
+    def push(t, _):
+        for k in range(3):
+            pl.when(t == k)(partial(take, loads[k]))
+        for r in range(4):
+            rows = slice(r * B, r * B + B)
             h, l = split(cov[rows, :])
             w[0, rows, :], w[1, rows, :] = h, l
-        unpack_spread(lambda r, n, c: load(r, n, c, B), lk)
-        mean[...] = dot_s(split(mean[...]), (eh[...], el[...]), 1) + load(GROW, 8)
-
         e = (eh[...], el[...])
+        mean[...] = dot_s(split(mean[...]), e, 1) + add[...]
         cov[...] = dot_s(split(dot_s(e, (w[0], w[1]))), e, 1) + lk[...]
-
-    push(lambda r, n, c=0, m=N: across[r : r + n, c : c + m])
-    push(lambda r, n, c=0, m=N: down[r : r + n, c : c + m])
-    push(lambda r, n, c=0, m=N: jnp.where(ids[0] == 0, pair[r : r + n, c : c + m], own[r : r + n, c : c + m]))
+        return 0
+
+    lax.fori_loop(0, 3, push, 0)
     for z in range(4):
-        out[z, 0:B, :] = cov[z * B : z * B + B, :]
-        out[z, B : B + 8, :] = mean[...]
+        out[z] = cov[z * B : z * B + B, :]
+    mean_out[...] = mean[...]
 
 
 def greet(peers):
@@ -318,86 +351,158 @@
     )
 
 
-def gather_step_kernel(cov, mean, out, mean_out, send, recv, local, msend, mrecv):
+def lanes_of_block(ref, j):
+    return ref.at[:, pl.ds(pl.multiple_of(lax.rem(j, 4) * B, B), B)]
+
+
+def gather_step_kernel(cov, mean, out, mean_out, relay, send, recv, relay_send, relay_recv, local, msend, mrecv):
     z, c = lax.axis_index("state"), lax.axis_index("tm_2")
     greet(column_peers(z, c))
     other = remote(mean, mean_out, msend, mrecv, {"tm_2": 1 - c})
     other.start()
 
-    def copy(i):
-        dz = 2 * c + i // 2
-        return remote(cov.at[i], out.at[z], send.at[i], recv.at[z], {"state": dz, "tm_2": i % 2})
-
-    def mine(i):
-        return (z == 2 * c + i // 2) & (c == i % 2)
+    def start(src, dst, row, ssem, rsem, peer):
+        for t in range(3):
+            remote(lanes_of_block(src, row + t), lanes_of_block(dst, row + t), ssem, rsem, peer).start()
+
+    def whole(ref, ssem, rsem):
+        part = ref.at[:, 0 : 3 * B]
+        return remote(part, part, ssem, rsem, {"state": 0, "tm_2": 0})
+
+    def target(i):
+        dz, e = 2 * c + i // 2, i % 2
+        mine = (z == dz) & (c == e)
+        far = lax.rem(dz + 4 - z, 4) == 2
+        return dz, e, mine, far
 
     for i in range(4):
-
-        @pl.when(mine(i))
+        dz, e, mine, far = target(i)
+
+        @pl.when(far)
+        def _():
+            start(cov.at[i], relay.at[e], z, send.at[i], relay_recv.at[e], {"state": lax.rem(z + (3 if e else 1), 4)})
+
+    for i in range(4):
+        dz, e, mine, far = target(i)
+
+        @pl.when(mine)
         def _():
             pltpu.make_async_copy(cov.at[i], out.at[z], local).start()
 
-        @pl.when(jnp.logical_not(mine(i)))
-        def _():
-            copy(i).start()
+        @pl.when(jnp.logical_not(mine | far))
+        def _():
+            start(cov.at[i], out.at[z], z, send.at[i], recv.at[z], {"state": dz, "tm_2": e})
+
+    duties = []
+    for e in range(2):
+        source, dz = lax.rem(z + (1 if e else 3), 4), lax.rem(z + (3 if e else 1), 4)
+        duty = source // 2 != c
+        duties.append(duty)
+
+        @pl.when(duty)
+        def _():
+            whole(relay.at[e], send.at[0], relay_recv.at[e]).wait_recv()
+            start(relay.at[e], out.at[source], source, relay_send.at[e], recv.at[source], {"state": dz, "tm_2": e})
 
     for i in range(4):
-
-        @pl.when(mine(i))
+        dz, e, mine, far = target(i)
+
+        @pl.when(mine)
         def _():
             pltpu.make_async_copy(cov.at[i], out.at[z], local).wait()
 
-        @pl.when(jnp.logical_not(mine(i)))
-        def _():
-            copy(i).wait_send()
+        @pl.when(jnp.logical_not(mine))
+        def _():
+            whole(cov.at[i], send.at[i], recv.at[0]).wait_send()
+
+    for e in range(2):
+
+        @pl.when(duties[e])
+        def _():
+            whole(relay.at[e], relay_send.at[e], recv.at[0]).wait_send()
 
     source_core = z // 2
     for s in range(4):
 
         @pl.when(jnp.logical_not((z == s) & (c == source_core)))
         def _():
-            remote(cov.at[0], out.at[s], send.at[0], recv.at[s], {"state": 0, "tm_2": 0}).wait_recv()
+            whole(out.at[s], send.at[0], recv.at[s]).wait_recv()
 
     other.wait()
 
 
-def scatter_step_kernel(slabs, out, send, recv, local):
+def scatter_step_kernel(slabs, mean, out, mean_out, relay, send, recv, relay_send, relay_recv, local, msend, mrecv):
     z, c = lax.axis_index("state"), lax.axis_index("tm_2")
     greet(column_peers(z, c))
     core = z // 2
     slot = 2 * lax.rem(z, 2) + c
+    opposite = lax.rem(z + 2, 4)
+    onward = lax.rem(z + 1 + 2 * c, 4)
+    far = remote(slabs.at[opposite], relay, relay_send.at[0], relay_recv, {"state": onward})
+    far.start()
 
     def copy(t):
         return remote(slabs.at[t], out.at[slot], send.at[t], recv.at[slot], {"state": t, "tm_2": core})
 
+    def mean_copy(t):
+        return remote(mean, mean_out.at[slot], msend.at[t], mrecv.at[slot], {"state": t, "tm_2": core})
+
     def mine(t):
         return (z == t) & (c == core)
 
+    def copies(t):
+        return pltpu.make_async_copy(slabs.at[t], out.at[slot], local.at[0]), pltpu.make_async_copy(
+            mean, mean_out.at[slot], local.at[1]
+        )
+
     for t in range(4):
 
         @pl.when(mine(t))
         def _():
-            pltpu.make_async_copy(slabs.at[t], out.at[slot], local).start()
+            for copy_here in copies(t):
+                copy_here.start()
 
         @pl.when(jnp.logical_not(mine(t)))
         def _():
+            mean_copy(t).start()
+
+        @pl.when(jnp.logical_not(mine(t)) & (t != opposite))
+        def _():
             copy(t).start()
 
+    source = lax.rem(z + 3 + 2 * c, 4)
+    far.wait_recv()
+    on = remote(
+        relay,
+        out.at[2 * lax.rem(source, 2) + c],
+        relay_send.at[1],
+        recv.at[2 * lax.rem(source, 2) + c],
+        {"state": onward, "tm_2": source // 2},
+    )
+    on.start()
     for t in range(4):
 
         @pl.when(mine(t))
         def _():
-            pltpu.make_async_copy(slabs.at[t], out.at[slot], local).wait()
+            for copy_here in copies(t):
+                copy_here.wait()
 
         @pl.when(jnp.logical_not(mine(t)))
         def _():
+            mean_copy(t).wait_send()
+
+        @pl.when(jnp.logical_not(mine(t)) & (t != opposite))
+        def _():
             copy(t).wait_send()
 
+    far.wait_send()
+    on.wait_send()
     for i in range(4):
 
         @pl.when(jnp.logical_not((z == 2 * c + i // 2) & (c == i % 2)))
         def _():
             remote(slabs.at[0], out.at[i], send.at[0], recv.at[i], {"state": 0, "tm_2": 0}).wait_recv()
+            remote(mean, mean_out.at[i], msend.at[0], mrecv.at[i], {"state": 0, "tm_2": 0}).wait_recv()
 
 
 def swap_kernel(x, out, send, recv):
@@ -436,40 +541,42 @@
     zu, zd, zo = lax.rem(z + 1, 4), lax.rem(z + 3, 4), lax.rem(z + 2, 4)
     greet([up, down, twin])
     cp = Copies(out, send, recv)
-    parts, q = 4, HALF // 4
     mine, theirs = c * HALF, (1 - c) * HALF
     ups, downs, tails, twins = [], [], [], []
 
-    def source(row):
-        return x.at[pl.ds(pl.multiple_of(row, 8), q), :]
-
-    for j in range(parts):
-        row = mine + j * q
-        ups.append((cp.put(up, z, row, q, source(row)), j))
-        row = mine + (parts - 1 - j) * q
-        downs.append((cp.put(down, z, row, q, source(row)), parts - 1 - j))
-
-    def hand(slot, j):
-        twins.append((cp.put(twin, slot, mine + j * q, q), slot, theirs + j * q))
-
-    for (nu, ju), (nd, jd) in zip(ups, downs):
-        cp.arrived(nu, zd, mine + ju * q, q)
-        if ju < parts // 2:
-            tails.append((cp.put(up, zd, mine + ju * q, q), ju))
-        hand(zd, ju)
-        cp.arrived(nd, zu, mine + jd * q, q)
-        if jd >= parts // 2:
-            tails.append((cp.put(down, zu, mine + jd * q, q), jd))
-        hand(zu, jd)
-    for n, j in tails:
-        cp.arrived(n, zo, mine + j * q, q)
-        hand(zo, j)
-    for n, slot, row in twins:
-        cp.arrived(n, slot, row, q)
+    def source(row, rows):
+        return x.at[pl.ds(pl.multiple_of(row, 8), rows), :]
+
+    for up_part, down_part in zip(PARTS, PARTS[::-1]):
+        off, rows = up_part
+        ups.append((cp.put(up, z, mine + off, rows, source(mine + off, rows)), up_part))
+        off, rows = down_part
+        downs.append((cp.put(down, z, mine + off, rows, source(mine + off, rows)), down_part))
+
+    def hand(slot, part):
+        off, rows = part
+        twins.append((cp.put(twin, slot, mine + off, rows), slot, theirs + off, rows))
+
+    for j, ((nu, up_part), (nd, down_part)) in enumerate(zip(ups, downs)):
+        off, rows = up_part
+        cp.arrived(nu, zd, mine + off, rows)
+        if j < len(PARTS) // 2:
+            tails.append((cp.put(up, zd, mine + off, rows), up_part))
+        hand(zd, up_part)
+        off, rows = down_part
+        cp.arrived(nd, zu, mine + off, rows)
+        if j < len(PARTS) // 2:
+            tails.append((cp.put(down, zu, mine + off, rows), down_part))
+        hand(zu, down_part)
+    for n, part in tails:
+        cp.arrived(n, zo, mine + part[0], part[1])
+        hand(zo, part)
+    for n, slot, row, rows in twins:
+        cp.arrived(n, slot, row, rows)
     cp.finish()
 
 
-PIECES = ((0, 56), (56, 56))
+PIECES = ((0, 32), (32, 24), (56, 32), (88, 24))
 
 
 def gather_ring_kernel(axis, x, out, send, recv):
@@ -523,6 +630,7 @@
         off, rows = PIECES[j]
         cp.arrived(n, ao, row(quarters[k], c) + off, rows)
         spread(k, ao, j)
+        take(len(zs) - 2)
     take(0)
     for n, slot, r, rows in twins:
         cp.arrived(n, slot, r, rows)
@@ -548,11 +656,13 @@
         in_specs=[ANY] * len(args),
         out_specs=jax.tree.map(lambda _: out_spec, outs),
         scratch_shapes=scratch,
-        compiler_params=pltpu.CompilerParams(collective_id=collective_id, has_side_effects=True),
+        compiler_params=pltpu.CompilerParams(
+            collective_id=collective_id, has_side_effects=True, vmem_limit_bytes=4 * 1024 * 1024
+        ),
     )(*args)
 
 
-BIG = 56 * 1024 * 1024
+BIG = 32 * 1024 * 1024
 WORK = [
     pltpu.VMEM((512, 512), BF16),
     pltpu.VMEM((512, 512), BF16),
@@ -560,13 +670,13 @@
 ]
 
 
-def scan(name, count, want_total, want_rest, ids, own, others):
+def scan(name, axis, count, want_total, want_rest, own, others):
     packet = shape(ROWS, N)
     return pl.pallas_call(
-        partial(scan_kernel, count, want_total, want_rest),
+        partial(scan_kernel, axis, count, want_total, want_rest),
         name=name,
         out_shape=[packet] * (want_total + want_rest),
-        in_specs=[SM, VM, VM],
+        in_specs=[VM, VM],
         out_specs=[VM] * (want_total + want_rest),
         scratch_shapes=[
             pltpu.VMEM((2, N, N), F32),
@@ -577,55 +687,61 @@
         ]
         + WORK,
         compiler_params=params(BIG),
-    )(ids, own, others)
+    )(own, others)
 
 
 def on_device(filtered_cov, filtered_mean, noise_var, trans_blocks, pattern):
-    y, x, c, z = (lax.axis_index(a) for a in ("tm_0", "tm_1", "tm_2", "state"))
+    z = lax.axis_index("state")
     cov, twin_mean = comm(
         gather_step_kernel,
         "gather_step",
         0,
         (shape(4, B, N), shape(4, N)),
-        [DMA((4,)), DMA((4,)), DMA, DMA, DMA],
+        [pltpu.VMEM((2, B, N), F32), DMA((4,)), DMA((4,)), DMA((2,)), DMA((2,)), DMA, DMA, DMA],
         filtered_cov,
         filtered_mean,
         out_spec=VM,
     )
-    step = 8 * (4 * y + x) + 2 * z + c
-    ids = jnp.stack([(z // 2 == c).astype(jnp.int32), lax.rem(2 * z + c, 4), (step != 127).astype(jnp.int32)])
     own = pl.pallas_call(
         element_kernel,
         name="element",
         out_shape=shape(ROWS, N),
-        in_specs=[SM, SM] + [VM] * 5,
+        in_specs=[SM] + [VM] * 5,
         out_specs=VM,
-        scratch_shapes=[pltpu.VMEM((N, N), F32)] * 3 + [pltpu.VMEM((8, N), F32)],
+        scratch_shapes=[pltpu.VMEM((N, N), F32)] * 3 + [pltpu.VMEM((8, N), F32), pltpu.VMEM((N, N), F32), pltpu.VMEM((B, B), F32)],
         compiler_params=params(BIG),
-    )(ids, pattern, cov.reshape(N, N), filtered_mean, twin_mean, noise_var.reshape(1, N), trans_blocks)
+    )(pattern, cov, filtered_mean, twin_mean, noise_var.reshape(1, N), trans_blocks)
     twin = comm(swap_kernel, "swap", 1, shape(1, ROWS, N), [DMA, DMA], own)
-    one = lambda v: v.reshape(1).astype(jnp.int32)
-    (pair,) = scan("scan_core", 2, True, False, one(c), own, twin)
+    (pair,) = scan("scan_core", "tm_2", 2, True, False, own, twin)
     pairs = comm(gather_z_kernel, "gather_z", 2, shape(4, ROWS, N), [DMA((24,)), DMA((24,))], pair)
-    column, down = scan("scan_z", 4, True, True, one(z), pair, pairs)
+    column, down = scan("scan_z", "state", 4, True, True, pair, pairs)
     columns = comm(
-        partial(gather_ring_kernel, "tm_1"), "gather_x", 3, shape(4, ROWS, N), [DMA((48,)), DMA((48,))], column
-    )
-    row, across = scan("scan_x", 4, True, True, one(x), column, columns)
-    rows = comm(partial(gather_ring_kernel, "tm_0"), "gather_y", 4, shape(4, ROWS, N), [DMA((48,)), DMA((48,))], row)
-    (later,) = scan("scan_y", 4, False, True, one(y), row, rows)
-    slabs = pl.pallas_call(
+        partial(gather_ring_kernel, "tm_1"), "gather_x", 3, shape(4, ROWS, N), [DMA((96,)), DMA((96,))], column
+    )
+    row, across = scan("scan_x", "tm_1", 4, True, True, column, columns)
+    rows = comm(partial(gather_ring_kernel, "tm_0"), "gather_y", 4, shape(4, ROWS, N), [DMA((96,)), DMA((96,))], row)
+    (later,) = scan("scan_y", "tm_0", 4, False, True, row, rows)
+    slabs, mean = pl.pallas_call(
         apply_kernel,
         name="apply",
-        out_shape=shape(4, B + 8, N),
-        in_specs=[SM] + [VM] * 5,
-        out_specs=VM,
-        scratch_shapes=[pltpu.VMEM((N, N), F32), pltpu.VMEM((8, N), F32), pltpu.VMEM((2, N, N), BF16)] + WORK,
+        out_shape=(shape(4, B, N), shape(8, N)),
+        in_specs=[VM] * 5,
+        out_specs=(VM, VM),
+        scratch_shapes=[pltpu.VMEM((N, N), F32), pltpu.VMEM((8, N), F32), pltpu.VMEM((8, N), F32), pltpu.VMEM((2, N, N), BF16)]
+        + WORK,
         compiler_params=params(BIG),
-    )(one(c), later, across, down, pair, own)
-    out = comm(scatter_step_kernel, "scatter_step", 5, shape(4, B + 8, N), [DMA((4,)), DMA((4,)), DMA], slabs, out_spec=VM)
-    smooth_mean = lax.dynamic_slice_in_dim(out[:, B, :], z * B, B, 1)
-    return smooth_mean, out[:, :B, :]
+    )(later, across, down, pair, own)
+    smooth_cov, means = comm(
+        scatter_step_kernel,
+        "scatter_step",
+        5,
+        (shape(4, B, N), shape(4, 8, N)),
+        [pltpu.VMEM((B, N), F32), DMA((4,)), DMA((4,)), DMA((2,)), DMA, DMA((2,)), DMA((4,)), DMA((4,))],
+        slabs,
+        mean,
+        out_spec=VM,
+    )
+    return lax.dynamic_slice_in_dim(means[:, 0, :], z * B, B, 1), smooth_cov
 
 
 def solution(mesh):

time: 245 us -> 210 us (0.86); the launches traced: 241 us -> 210 us
  Pallas kernels: 234 us -> 202 us
    pallas_call x5, Pallas kernels: 59.7 us -> 40.3 us  [the longest x4 32.3 us: scan(): pl.pallas_call(partial(scan_kernel, axis, count, want_total, want_rest),...]
    pallas_call x6, Pallas kernels: 136 us -> 126 us  [comm(): pl.pallas_call(kernel, name=name, out_shape=outs, in_specs=[ANY] * len(ar...]
    unnamed x1 -> x12, local copies, waits for them, and re-layouts: 1.34 us -> 6.07 us
    slice x2 -> x1, local copies, waits for them, and re-layouts: 3.11 us -> 0.01 us  [on_device(): return (lax.dynamic_slice_in_dim(means[:, 0, :], z * B, B, 1), smooth_cov)]
where the time goes in v3:
time: 210 us
  Pallas kernels  202 us (96%)
  local copies, waits for them, and re-layouts  6.66 us (3%)
    pallas_call x6, Pallas kernels, comm(): pl.pallas_call(kernel, name=name, out_shape=outs, in_specs=[ANY] * len(ar...  126 us
    pallas_call x1, Pallas kernels, on_device(): pl.pallas_call(element_kernel, name='element', out_shape=shape(ROWS, N),...  36.3 us
    pallas_call x4, Pallas kernels, scan(): pl.pallas_call(partial(scan_kernel, axis, count, want_total, want_rest),...  32.3 us
    pallas_call x1, Pallas kernels, on_device(): pl.pallas_call(apply_kernel, name='apply', out_shape=(shape(4, B, N), sha...  8.02 us
    unnamed x12, local copies, waits for them, and re-layouts  6.07 us

profile of v3, /device:TPU:1, one launch (start us, length us, event | category | flops | bytes accessed | tf_op | source)
XLA Modules:
  0.0 209.7 jit_solution(16648461124703800578)
XLA Ops:
  0.6 0.0 copy-start
  0.6 1.2 copy-done
  1.9 0.0 copy-start.2
  1.9 0.7 copy-done.2
  2.6 15.5 %gather_step.1 = (f32[4,128,512]{2,1,0:T(8,128)S(1)}, f32[4,512]{1,0:T(4,128)S(1)}) custom-call(f32[4,128,512]{2,1,0:T(8,128)S(1)} %copy-done, f32[4,512]{1,0:T(4,128)S(1)} %copy-done.2), custom_call_target="tpu_custom_call" | custom-call | tf_op jit(solution)/shard_map/gather_step/pallas_call | solution.py:652
  18.1 0.8 copy.7.pattern
  18.9 0.0 copy-start.1
  18.9 1.0 copy-done.1
  19.9 0.0 copy-start.3
  19.9 0.7 copy-done.3
  20.6 0.0 copy-start.4
  20.6 0.7 copy-done.4
  21.3 36.3 %element.1.x.own = f32[896,512]{1,0:T(8,128)S(1)} custom-call(s32[4,2]{1,0:T(4,128)S(1)} %copy.7.pattern, f32[4,128,512]{2,1,0:T(8,128)S(1)} %get-tuple-element.12.cov_in, f32[4,512]{1,0:T(4,128)S(1)} %copy-done.3, f32[4,512]{1,0:T(4,128)S(1)} %get-tuple-element.13.mean_b, f32[1,512]{1,0:T(1,128)S(1)} %bitcast.2, f32[4,2,128,128]{3,2,1,0:T(8,128)S(1)} %copy-done.1), custom_call_target="tpu_custom_call" | custom-call | tf_op jit(solution)/shard_map/element/pallas_call | solution.py:705
  57.6 5.1 %swap.1.others = f32[1,896,512]{2,1,0:T(8,128)S(1)} custom-call(f32[896,512]{1,0:T(8,128)S(1)} %element.1.x.own), custom_call_target="tpu_custom_call" | custom-call | tf_op jit(solution)/shard_map/swap/pallas_call | solution.py:652
  62.6 3.1 %scan_core.1.x.own.pair = f32[896,512]{1,0:T(8,128)S(1)} custom-call(f32[896,512]{1,0:T(8,128)S(1)} %element.1.x.own, f32[1,896,512]{2,1,0:T(8,128)S(1)} %swap.1.others), custom_call_target="tpu_custom_call" | custom-call | tf_op jit(solution)/shard_map/scan_core/pallas_call | solution.py:675
  65.7 34.2 %gather_z.1.others = f32[4,896,512]{2,1,0:T(8,128)S(1)} custom-call(f32[896,512]{1,0:T(8,128)S(1)} %scan_core.1.x.own.pair), custom_call_target="tpu_custom_call" | custom-call | tf_op jit(solution)/shard_map/gather_z/pallas_call | solution.py:652
  100.0 9.8 %scan_z.1 = (f32[896,512]{1,0:T(8,128)S(1)}, f32[896,512]{1,0:T(8,128)S(1)}) custom-call(f32[896,512]{1,0:T(8,128)S(1)} %scan_core.1.x.own.pair, f32[4,896,512]{2,1,0:T(8,128)S(1)} %gather_z.1.others), custom_call_target="tpu_custom_call" | custom-call | tf_op jit(solution)/shard_map/scan_z/pallas_call | solution.py:675
  109.8 27.0 %gather_x.1.others = f32[4,896,512]{2,1,0:T(8,128)S(1)} custom-call(f32[896,512]{1,0:T(8,128)S(1)} %get-tuple-element.14.x.own), custom_call_target="tpu_custom_call" | custom-call | tf_op jit(solution)/shard_map/gather_x/pallas_call | solution.py:652
  136.8 9.6 %scan_x.1 = (f32[896,512]{1,0:T(8,128)S(1)}, f32[896,512]{1,0:T(8,128)S(1)}) custom-call(f32[896,512]{1,0:T(8,128)S(1)} %get-tuple-element.14.x.own, f32[4,896,512]{2,1,0:T(8,128)S(1)} %gather_x.1.others), custom_call_target="tpu_custom_call" | custom-call | tf_op jit(solution)/shard_map/scan_x/pallas_call | solution.py:675
  146.4 27.8 %gather_y.1.others = f32[4,896,512]{2,1,0:T(8,128)S(1)} custom-call(f32[896,512]{1,0:T(8,128)S(1)} %get-tuple-element.15.x.own), custom_call_target="tpu_custom_call" | custom-call | tf_op jit(solution)/shard_map/gather_y/pallas_call | solution.py:652
  174.2 9.7 %scan_y.1.later = f32[896,512]{1,0:T(8,128)S(1)} custom-call(f32[896,512]{1,0:T(8,128)S(1)} %get-tuple-element.15.x.own, f32[4,896,512]{2,1,0:T(8,128)S(1)} %gather_y.1.others), custom_call_target="tpu_custom_call" | custom-call | tf_op jit(solution)/shard_map/scan_y/pallas_call | solution.py:675
  184.0 8.0 %apply.1 = (f32[4,128,512]{2,1,0:T(8,128)S(1)}, f32[8,512]{1,0:T(8,128)S(1)}) custom-call(f32[896,512]{1,0:T(8,128)S(1)} %scan_y.1.later, f32[896,512]{1,0:T(8,128)S(1)} %get-tuple-element.16.across, f32[896,512]{1,0:T(8,128)S(1)} %get-tuple-element.17.down, f32[896,512]{1,0:T(8,128)S(1)} %scan_core.1.x.own.pair, f32[896,512]{1,0:T(8,128)S(1)} %element.1.x.own), custom_call_target="tpu_custom_call" | custom-call | tf_op jit(solution)/shard_map/apply/pallas_call | solution.py:724
  192.0 16.1 %scatter_step.1 = (f32[4,128,512]{2,1,0:T(8,128)S(1)}, f32[4,8,512]{2,1,0:T(8,128)S(1)}) custom-call(f32[4,128,512]{2,1,0:T(8,128)S(1)} %get-tuple-element.18.slabs, f32[8,512]{1,0:T(8,128)S(1)} %get-tuple-element.19.mean), custom_call_target="tpu_custom_call" | custom-call | tf_op jit(solution)/shard_map/scatter_step/pallas_call | solution.py:652
  208.2 0.6 constant_dynamic-slice_fusion
  208.8 1.0 copy.9
  (1 shorter events, 0.0 us)
Async XLA Ops:
  0.6 1.2 copy-start
  1.9 0.7 copy-start.2
  18.9 1.0 copy-start.1
  19.9 0.7 copy-start.3
  20.6 0.7 copy-start.4

commit v4 on v3

--- a/solution.py
+++ b/solution.py
@@ -13,9 +13,6 @@
 LROW = 512
 GROW = 832
 ROWS = 896
-HALF = 424
-PARTS = ((0, 112), (112, 104), (216, 104), (320, 104))
-SH = ROWS // 8
 MESH = pl.DeviceIdType.MESH
 F32 = jnp.float32
 BF16 = jnp.bfloat16
@@ -226,69 +223,97 @@
     pack_spread(out, lambda r, n, c: pred[r : r + n, c : c + B])
 
 
-def scan_kernel(axis, count, want_total, want_rest, own, others, *refs):
-    outs, (se, sl, sg, rh, rl, eh, el, lk) = refs[: want_total + want_rest], refs[want_total + want_rest :]
-    rest_ref = outs[-1]
-    me = lax.axis_index(axis)
+def suffixes(count, me, own, other, total, rest, work, ready=lambda part: None, done=lambda part: None):
+    se, sl, sg, rh, rl, eh, el, lk = work
 
     def load(k, row, rows, lane=0, lanes=N):
-        slot = k if count > 2 else 0
-        return jnp.where(
-            k == me, own[row : row + rows, lane : lane + lanes], others[slot, row : row + rows, lane : lane + lanes]
-        )
-
-    def store(ref, slot):
-        ref[0:N, :] = se[slot]
+        return jnp.where(k == me, own[row : row + rows, lane : lane + lanes], other(k, row, rows, lane, lanes))
+
+    last, steps = count - 1, count - 1
+
+    def split_into(high, low, value):
+        for r in range(4):
+            rows = slice(r * B, r * B + B)
+            high[rows, :], low[rows, :] = split(value(rows))
+
+    if rest is not None:
+
+        @pl.when(me == last)
+        def _():
+            same = lax.broadcasted_iota(jnp.int32, (N, N), 0) == lax.broadcasted_iota(jnp.int32, (N, N), 1)
+            rest[0:N, :] = same.astype(F32)
+            rest[N:, :] = jnp.zeros((ROWS - N, N), F32)
+
+    def gains(t, _):
+        k = last - 1 - t
+        now = lax.rem(t, 2)
+        if rest is not None:
+
+            @pl.when(k == me)
+            def _():
+                rest[0:N, :] = se[now]
+
+        split_into(eh.at[k], el.at[k], lambda rows: load(k, rows.start, B))
+        split_into(rh, rl, lambda rows: se[now, rows, :])
+        se[1 - now] = dot_s((eh[k], el[k]), (rh[...], rl[...]))
+        return 0
+
+    ready(0)
+    if total is not None:
+        se[0] = load(last, 0, N)
+        lax.fori_loop(0, steps, gains, 0)
+        total[0:N, :] = se[steps % 2]
+        done(0)
+    else:
+
+        def just_split(t, _):
+            k = last - 1 - t
+            split_into(eh.at[k], el.at[k], lambda rows: load(k, rows.start, B))
+            return 0
+
+        lax.fori_loop(0, steps, just_split, 0)
+    ready(1)
+    unpack_spread(lambda r, n, c: load(last, r, n, c, B), sl.at[0])
+    sg[0] = load(last, GROW, 8)
+
+    def keep(ref, slot):
         pack_spread(ref, lambda r, n, c: sl[slot, r : r + n, c : c + B])
         ref[GROW : GROW + 8, :] = sg[slot]
         ref[GROW + 8 :, :] = jnp.zeros((ROWS - GROW - 8, N), F32)
 
-    if want_rest:
-
-        @pl.when(me == count - 1)
-        def _():
-            same = lax.broadcasted_iota(jnp.int32, (N, N), 0) == lax.broadcasted_iota(jnp.int32, (N, N), 1)
-            rest_ref[0:N, :] = same.astype(F32)
-            rest_ref[N:, :] = jnp.zeros((ROWS - N, N), F32)
-
-    last = count - 1
-    se[0] = load(last, 0, N)
-    unpack_spread(lambda r, n, c: load(last, r, n, c, B), sl.at[0])
-    sg[0] = load(last, GROW, 8)
-
-    def step(t, _):
-        k = count - 2 - t
+    def spreads(t, _):
+        k = last - 1 - t
         now = lax.rem(t, 2)
-        new = 1 - now
-        if want_rest:
+        if rest is not None:
 
             @pl.when(k == me)
             def _():
-                store(rest_ref, now)
-
-        for r in range(4):
-            rows = slice(r * B, r * B + B)
-            h, l = split(se[now, rows, :])
-            rh[rows, 0:N], rl[rows, 0:N] = h, l
-            h, l = split(sl[now, rows, :])
-            rh[rows, N:], rl[rows, N:] = h, l
-            h, l = split(load(k, r * B, B))
-            eh[rows, :], el[rows, :] = h, l
+                keep(rest, now)
+
+        split_into(rh, rl, lambda rows: sl[now, rows, :])
         unpack_spread(lambda r, n, c: load(k, r, n, c, B), lk)
-        sg[new] = dot_s(split(sg[now]), (eh[...], el[...]), 1) + load(k, GROW, 8)
-
-        e = (eh[...], el[...])
-        se[new] = dot_s(e, (rh[:, :N], rl[:, :N]))
-        half = split(dot_s(e, (rh[:, N:], rl[:, N:])))
-        sl[new] = dot_s(half, e, 1) + lk[...]
+        e = (eh[k], el[k])
+        sg[1 - now] = dot_s(split(sg[now]), e, 1) + load(k, GROW, 8)
+        half = split(dot_s(e, (rh[...], rl[...])))
+        sl[1 - now] = dot_s(half, e, 1) + lk[...]
         return 0
 
-    steps = count - 1
-    if want_total:
-        lax.fori_loop(0, steps, step, 0)
-        store(outs[0], steps % 2)
-    else:
-        lax.fori_loop(0, steps, step, 0)
+    lax.fori_loop(0, steps, spreads, 0)
+    if total is not None:
+        keep(total, steps % 2)
+        done(1)
+
+
+def scan_kernel(own, others, rest, *work):
+    suffixes(
+        4,
+        lax.axis_index("tm_0"),
+        own,
+        lambda k, row, rows, lane, lanes: others[k, row : row + rows, lane : lane + lanes],
+        None,
+        rest,
+        work,
+    )
 
 
 def apply_kernel(later, across, down, pair, own, out, mean_out, cov, mean, add, w, eh, el, lk):
@@ -505,14 +530,6 @@
             remote(mean, mean_out.at[i], msend.at[0], mrecv.at[i], {"state": 0, "tm_2": 0}).wait_recv()
 
 
-def swap_kernel(x, out, send, recv):
-    peer = {"tm_2": 1 - lax.axis_index("tm_2")}
-    greet([peer])
-    copy = remote(x, out.at[0], send, recv, peer)
-    copy.start()
-    copy.wait()
-
-
 class Copies:
     def __init__(self, out, send, recv):
         self.out, self.send, self.recv, self.used, self.sent = out, send, recv, 0, []
@@ -534,106 +551,138 @@
             copy.wait_send()
 
 
-def gather_z_kernel(x, out, send, recv):
+Z_PIECES = (((0, 64), (64, 64), (128, 64), (192, 64)), ((0, 48), (48, 40), (88, 40), (128, 40)))
+Z_HALF = (256, 168)
+
+
+def pair_kernel(own, total, out, twin_buf, *refs):
+    work, (swap_send, swap_recv, send, recv) = refs[:8], refs[8:]
     z, c = lax.axis_index("state"), lax.axis_index("tm_2")
-    up, down = {"state": lax.rem(z + 1, 4)}, {"state": lax.rem(z + 3, 4)}
-    twin = {"tm_2": 1 - c}
     zu, zd, zo = lax.rem(z + 1, 4), lax.rem(z + 3, 4), lax.rem(z + 2, 4)
+    up, down, twin = {"state": zu}, {"state": zd}, {"tm_2": 1 - c}
     greet([up, down, twin])
+    swaps = []
+    for part, rows in ((0, pl.ds(0, N)), (1, pl.ds(N, ROWS - N))):
+        swaps.append(remote(own.at[rows], twin_buf.at[rows], swap_send.at[part], swap_recv.at[part], twin))
+        swaps[part].start()
     cp = Copies(out, send, recv)
-    mine, theirs = c * HALF, (1 - c) * HALF
     ups, downs, tails, twins = [], [], [], []
 
-    def source(row, rows):
-        return x.at[pl.ds(pl.multiple_of(row, 8), rows), :]
-
-    for up_part, down_part in zip(PARTS, PARTS[::-1]):
-        off, rows = up_part
-        ups.append((cp.put(up, z, mine + off, rows, source(mine + off, rows)), up_part))
-        off, rows = down_part
-        downs.append((cp.put(down, z, mine + off, rows, source(mine + off, rows)), down_part))
-
-    def hand(slot, part):
-        off, rows = part
-        twins.append((cp.put(twin, slot, mine + off, rows), slot, theirs + off, rows))
-
-    for j, ((nu, up_part), (nd, down_part)) in enumerate(zip(ups, downs)):
-        off, rows = up_part
-        cp.arrived(nu, zd, mine + off, rows)
-        if j < len(PARTS) // 2:
-            tails.append((cp.put(up, zd, mine + off, rows), up_part))
-        hand(zd, up_part)
-        off, rows = down_part
-        cp.arrived(nd, zu, mine + off, rows)
-        if j < len(PARTS) // 2:
-            tails.append((cp.put(down, zu, mine + off, rows), down_part))
-        hand(zu, down_part)
-    for n, part in tails:
-        cp.arrived(n, zo, mine + part[0], part[1])
-        hand(zo, part)
-    for n, slot, row, rows in twins:
+    def rows_of(part, core, piece):
+        return (N if part else 0) + core * Z_HALF[part] + piece[0], piece[1]
+
+    def first_hop(part):
+        pieces = Z_PIECES[part]
+        for j, (a, b) in enumerate(zip(pieces, pieces[::-1])):
+            for into, peer, piece in ((ups, up, a), (downs, down, b)):
+                row, rows = rows_of(part, c, piece)
+                n = cp.put(peer, z, row, rows, total.at[pl.ds(pl.multiple_of(row, 8), rows), :])
+                into.append((n, part, piece, j < len(pieces) // 2))
+
+    suffixes(
+        2,
+        c,
+        own,
+        lambda k, row, rows, lane, lanes: twin_buf[row : row + rows, lane : lane + lanes],
+        total,
+        None,
+        work,
+        lambda part: swaps[part].wait(),
+        first_hop,
+    )
+
+    def hand(slot, part, piece):
+        row, rows = rows_of(part, c, piece)
+        twins.append((cp.put(twin, slot, row, rows), slot, rows_of(part, 1 - c, piece)))
+
+    for pair in zip(ups, downs):
+        for (n, part, piece, further), slot, peer in zip(pair, (zd, zu), (up, down)):
+            row, rows = rows_of(part, c, piece)
+            cp.arrived(n, slot, row, rows)
+            if further:
+                tails.append((cp.put(peer, slot, row, rows), part, piece))
+            hand(slot, part, piece)
+    for n, part, piece in tails:
+        row, rows = rows_of(part, c, piece)
+        cp.arrived(n, zo, row, rows)
+        hand(zo, part, piece)
+    for n, slot, (row, rows) in twins:
         cp.arrived(n, slot, row, rows)
     cp.finish()
 
 
-PIECES = ((0, 32), (32, 24), (56, 32), (88, 24))
-
-
-def gather_ring_kernel(axis, x, out, send, recv):
+R_PIECES = (((0, 32), (32, 32)), ((0, 24), (24, 24)))
+R_EIGHTH = (64, 48)
+
+
+def ring_kernel(mine, axis, own, others, rest, out, total, *refs):
+    work, (send, recv) = refs[:8], refs[8:]
     z, c, a = lax.axis_index("state"), lax.axis_index("tm_2"), lax.axis_index(axis)
     zu, zd, zo = lax.rem(z + 1, 4), lax.rem(z + 3, 4), lax.rem(z + 2, 4)
     au, ad, ao = lax.rem(a + 1, 4), lax.rem(a + 3, 4), lax.rem(a + 2, 4)
     up, down = {axis: au}, {axis: ad}
     above, below, twin = {"state": zu}, {"state": zd}, {"tm_2": 1 - c}
-    greet([up, down, above, below, twin])
+    peers = [up, down, above, below, twin]
+    barrier = pltpu.get_barrier_semaphore()
+    for peer in peers:
+        pl.semaphore_signal(barrier, inc=1, device_id=peer, device_id_type=MESH)
     cp = Copies(out, send, recv)
-    row = lambda quarter, core: quarter * (2 * SH) + core * SH
     quarters = (z, zu)
     coming = (zd, zo)
-    pieces = len(PIECES)
-    order_up = list(range(pieces))
-    order_down = order_up[::-1]
     ups, downs, twins, zs, tails = [], [], [], [], []
-    for ju, jd in zip(order_up, order_down):
-        for k in (0, 1):
-            for into, peer, j in ((ups, up, ju), (downs, down, jd)):
-                off, rows = PIECES[j]
-                r = row(quarters[k], c) + off
-                into.append((cp.put(peer, a, r, rows, x.at[pl.ds(pl.multiple_of(r, 8), rows), :]), k, j))
-
-    def spread(k, slot, j):
-        off, rows = PIECES[j]
-        r = row(quarters[k], c) + off
-        zs.append((cp.put(below if k else above, slot, r, rows), slot, k, j))
-        twins.append((cp.put(twin, slot, r, rows), slot, row(quarters[k], 1 - c) + off, rows))
+
+    def rows_of(part, quarter, core, piece):
+        return (N if part else 0) + (2 * quarter + core) * R_EIGHTH[part] + piece[0], piece[1]
+
+    def first_hop(part):
+        if part == 0:
+            pl.semaphore_wait(barrier, len(peers))
+        pieces = R_PIECES[part]
+        for j, pair in enumerate(zip(pieces, pieces[::-1])):
+            for k in (0, 1):
+                for into, peer, piece in zip((ups, downs), (up, down), pair):
+                    row, rows = rows_of(part, quarters[k], c, piece)
+                    n = cp.put(peer, a, row, rows, total.at[pl.ds(pl.multiple_of(row, 8), rows), :])
+                    into.append((n, part, k, piece, j < len(pieces) // 2))
+
+    suffixes(
+        4,
+        lax.axis_index(mine),
+        own,
+        lambda k, row, rows, lane, lanes: others[k, row : row + rows, lane : lane + lanes],
+        total,
+        rest,
+        work,
+        done=first_hop,
+    )
+
+    def spread(slot, part, k, piece):
+        row, rows = rows_of(part, quarters[k], c, piece)
+        zs.append((cp.put(below if k else above, slot, row, rows), slot, part, k, piece))
+        twins.append((cp.put(twin, slot, row, rows), slot, rows_of(part, quarters[k], 1 - c, piece)))
 
     def take(count):
         while len(zs) > count:
-            n, slot, k, j = zs.pop(0)
-            off, rows = PIECES[j]
-            r = row(coming[k], c) + off
-            cp.arrived(n, slot, r, rows)
-            twins.append((cp.put(twin, slot, r, rows), slot, row(coming[k], 1 - c) + off, rows))
-
-    for (nu, k, ju), (nd, _, jd) in zip(ups, downs):
-        off, rows = PIECES[ju]
-        cp.arrived(nu, ad, row(quarters[k], c) + off, rows)
-        if ju < pieces // 2:
-            tails.append((cp.put(up, ad, row(quarters[k], c) + off, rows), k, ju))
-        spread(k, ad, ju)
-        off, rows = PIECES[jd]
-        cp.arrived(nd, au, row(quarters[k], c) + off, rows)
-        if jd >= pieces // 2:
-            tails.append((cp.put(down, au, row(quarters[k], c) + off, rows), k, jd))
-        spread(k, au, jd)
-    for n, k, j in tails:
-        off, rows = PIECES[j]
-        cp.arrived(n, ao, row(quarters[k], c) + off, rows)
-        spread(k, ao, j)
+            n, slot, part, k, piece = zs.pop(0)
+            row, rows = rows_of(part, coming[k], c, piece)
+            cp.arrived(n, slot, row, rows)
+            twins.append((cp.put(twin, slot, row, rows), slot, rows_of(part, coming[k], 1 - c, piece)))
+
+    for pair in zip(ups, downs):
+        for (n, part, k, piece, further), slot, peer in zip(pair, (ad, au), (up, down)):
+            row, rows = rows_of(part, quarters[k], c, piece)
+            cp.arrived(n, slot, row, rows)
+            if further:
+                tails.append((cp.put(peer, slot, row, rows), part, k, piece))
+            spread(slot, part, k, piece)
+    for n, part, k, piece in tails:
+        row, rows = rows_of(part, quarters[k], c, piece)
+        cp.arrived(n, ao, row, rows)
+        spread(ao, part, k, piece)
         take(len(zs) - 2)
     take(0)
-    for n, slot, r, rows in twins:
-        cp.arrived(n, slot, r, rows)
+    for n, slot, (row, rows) in twins:
+        cp.arrived(n, slot, row, rows)
     cp.finish()
 
 
@@ -670,24 +719,33 @@
 ]
 
 
-def scan(name, axis, count, want_total, want_rest, own, others):
+def suffix_work(count):
+    return [
+        pltpu.VMEM((2, N, N), F32),
+        pltpu.VMEM((2, N, N), F32),
+        pltpu.VMEM((2, 8, N), F32),
+        pltpu.VMEM((N, N), BF16),
+        pltpu.VMEM((N, N), BF16),
+        pltpu.VMEM((count - 1, N, N), BF16),
+        pltpu.VMEM((count - 1, N, N), BF16),
+        pltpu.VMEM((N, N), F32),
+    ]
+
+
+def ring(name, collective_id, mine, axis, own, others):
     packet = shape(ROWS, N)
     return pl.pallas_call(
-        partial(scan_kernel, axis, count, want_total, want_rest),
+        partial(ring_kernel, mine, axis),
         name=name,
-        out_shape=[packet] * (want_total + want_rest),
+        out_shape=(packet, shape(4, ROWS, N), packet),
         in_specs=[VM, VM],
-        out_specs=[VM] * (want_total + want_rest),
-        scratch_shapes=[
-            pltpu.VMEM((2, N, N), F32),
-            pltpu.VMEM((2, N, N), F32),
-            pltpu.VMEM((2, 8, N), F32),
-            pltpu.VMEM((N, 2 * N), BF16),
-            pltpu.VMEM((N, 2 * N), BF16),
-        ]
-        + WORK,
-        compiler_params=params(BIG),
+        out_specs=(VM, VM, VM),
+        scratch_shapes=suffix_work(4) + [DMA((96,)), DMA((96,))],
+        compiler_params=params(RING_LIMIT, collective_id=collective_id, has_side_effects=True),
     )(own, others)
+
+
+RING_LIMIT = 24 * 1024 * 1024
 
 
 def on_device(filtered_cov, filtered_mean, noise_var, trans_blocks, pattern):
@@ -711,16 +769,27 @@
         scratch_shapes=[pltpu.VMEM((N, N), F32)] * 3 + [pltpu.VMEM((8, N), F32), pltpu.VMEM((N, N), F32), pltpu.VMEM((B, B), F32)],
         compiler_params=params(BIG),
     )(pattern, cov, filtered_mean, twin_mean, noise_var.reshape(1, N), trans_blocks)
-    twin = comm(swap_kernel, "swap", 1, shape(1, ROWS, N), [DMA, DMA], own)
-    (pair,) = scan("scan_core", "tm_2", 2, True, False, own, twin)
-    pairs = comm(gather_z_kernel, "gather_z", 2, shape(4, ROWS, N), [DMA((24,)), DMA((24,))], pair)
-    column, down = scan("scan_z", "state", 4, True, True, pair, pairs)
-    columns = comm(
-        partial(gather_ring_kernel, "tm_1"), "gather_x", 3, shape(4, ROWS, N), [DMA((96,)), DMA((96,))], column
-    )
-    row, across = scan("scan_x", "tm_1", 4, True, True, column, columns)
-    rows = comm(partial(gather_ring_kernel, "tm_0"), "gather_y", 4, shape(4, ROWS, N), [DMA((96,)), DMA((96,))], row)
-    (later,) = scan("scan_y", "tm_0", 4, False, True, row, rows)
+    packet, packets = shape(ROWS, N), shape(4, ROWS, N)
+    pair, pairs = pl.pallas_call(
+        pair_kernel,
+        name="pair",
+        out_shape=(packet, packets),
+        in_specs=[VM],
+        out_specs=(VM, VM),
+        scratch_shapes=[pltpu.VMEM((ROWS, N), F32)] + suffix_work(2) + [DMA((2,)), DMA((2,)), DMA((48,)), DMA((48,))],
+        compiler_params=params(RING_LIMIT, collective_id=2, has_side_effects=True),
+    )(own)
+    down, columns, column = ring("ring_x", 3, "state", "tm_1", pair, pairs)
+    across, rows, row = ring("ring_y", 4, "tm_1", "tm_0", column, columns)
+    later = pl.pallas_call(
+        scan_kernel,
+        name="scan_y",
+        out_shape=packet,
+        in_specs=[VM, VM],
+        out_specs=VM,
+        scratch_shapes=suffix_work(4),
+        compiler_params=params(BIG),
+    )(row, rows)
     slabs, mean = pl.pallas_call(
         apply_kernel,
         name="apply",

time: 210 us -> 193 us (0.919)
  Pallas kernels: 202 us -> 185 us
    pallas_call x6 -> x2, Pallas kernels: 126 us -> 31.4 us  [comm(): pl.pallas_call(kernel, name=name, out_shape=outs, in_specs=[ANY] * len(ar...]
    pallas_call x4, Pallas kernels: 32.3 us -> 109 us  [the longest x2 62.4 us: ring(): pl.pallas_call(partial(ring_kernel, mine, axis), name=name, out_shape=(pa...]
where the time goes in v4:
time: 193 us; the launch traced here: 192 us
  Pallas kernels  185 us (96%)
  local copies, waits for them, and re-layouts  6.66 us (3%)
    pallas_call x2, Pallas kernels, ring(): pl.pallas_call(partial(ring_kernel, mine, axis), name=name, out_shape=(pa...  62.4 us
    pallas_call x1, Pallas kernels, on_device(): pl.pallas_call(pair_kernel, name='pair', out_shape=(packet, packets), in_...  39.4 us
    pallas_call x1, Pallas kernels, on_device(): pl.pallas_call(element_kernel, name='element', out_shape=shape(ROWS, N),...  36.3 us
    pallas_call x2, Pallas kernels, comm(): pl.pallas_call(kernel, name=name, out_shape=outs, in_specs=[ANY] * len(ar...  31.4 us
    pallas_call x1, Pallas kernels, on_device(): pl.pallas_call(apply_kernel, name='apply', out_shape=(shape(4, B, N), sha...  8.01 us
    pallas_call x1, Pallas kernels, on_device(): pl.pallas_call(scan_kernel, name='scan_y', out_shape=packet, in_specs=[VM...  7.42 us
    unnamed x12, local copies, waits for them, and re-layouts  6.07 us

profile of v4, /device:TPU:1, one launch (start us, length us, event | category | flops | bytes accessed | tf_op | source)
XLA Modules:
  0.0 192.3 jit_solution(8984946296951567899)
XLA Ops:
  0.6 0.0 copy-start
  0.6 1.2 copy-done
  1.9 0.0 copy-start.2
  1.9 0.7 copy-done.2
  2.6 15.5 %gather_step.1 = (f32[4,128,512]{2,1,0:T(8,128)S(1)}, f32[4,512]{1,0:T(4,128)S(1)}) custom-call(f32[4,128,512]{2,1,0:T(8,128)S(1)} %copy-done, f32[4,512]{1,0:T(4,128)S(1)} %copy-done.2), custom_call_target="tpu_custom_call" | custom-call | tf_op jit(solution)/shard_map/gather_step/pallas_call | solution.py:701
  18.1 0.8 copy.7.pattern
  18.9 0.0 copy-start.1
  18.9 1.0 copy-done.1
  19.9 0.0 copy-start.3
  19.9 0.7 copy-done.3
  20.6 0.0 copy-start.4
  20.6 0.7 copy-done.4
  21.3 36.3 %element.1.own = f32[896,512]{1,0:T(8,128)S(1)} custom-call(s32[4,2]{1,0:T(4,128)S(1)} %copy.7.pattern, f32[4,128,512]{2,1,0:T(8,128)S(1)} %get-tuple-element.16.cov_in, f32[4,512]{1,0:T(4,128)S(1)} %copy-done.3, f32[4,512]{1,0:T(4,128)S(1)} %get-tuple-element.17.mean_b, f32[1,512]{1,0:T(1,128)S(1)} %bitcast.2, f32[4,2,128,128]{3,2,1,0:T(8,128)S(1)} %copy-done.1), custom_call_target="tpu_custom_call" | custom-call | tf_op jit(solution)/shard_map/element/pallas_call | solution.py:763
  57.6 39.4 %pair.1 = (f32[896,512]{1,0:T(8,128)S(1)}, f32[4,896,512]{2,1,0:T(8,128)S(1)}) custom-call(f32[896,512]{1,0:T(8,128)S(1)} %element.1.own), custom_call_target="tpu_custom_call" | custom-call | tf_op jit(solution)/shard_map/pair/pallas_call | solution.py:773
  96.9 29.1 %ring_x.1 = (f32[896,512]{1,0:T(8,128)S(1)}, f32[4,896,512]{2,1,0:T(8,128)S(1)}, f32[896,512]{1,0:T(8,128)S(1)}) custom-call(f32[896,512]{1,0:T(8,128)S(1)} %get-tuple-element.18.own.pair, f32[4,896,512]{2,1,0:T(8,128)S(1)} %get-tuple-element.19.others), custom_call_target="tpu_custom_call" | custom-call | tf_op jit(solution)/shard_map/ring_x/pallas_call | solution.py:737
  126.1 33.3 %ring_y.1 = (f32[896,512]{1,0:T(8,128)S(1)}, f32[4,896,512]{2,1,0:T(8,128)S(1)}, f32[896,512]{1,0:T(8,128)S(1)}) custom-call(f32[896,512]{1,0:T(8,128)S(1)} %get-tuple-element.20.own, f32[4,896,512]{2,1,0:T(8,128)S(1)} %get-tuple-element.21.others), custom_call_target="tpu_custom_call" | custom-call | tf_op jit(solution)/shard_map/ring_y/pallas_call | solution.py:737
  159.4 7.4 %scan_y.1.later = f32[896,512]{1,0:T(8,128)S(1)} custom-call(f32[896,512]{1,0:T(8,128)S(1)} %get-tuple-element.22.own, f32[4,896,512]{2,1,0:T(8,128)S(1)} %get-tuple-element.23.others), custom_call_target="tpu_custom_call" | custom-call | tf_op jit(solution)/shard_map/scan_y/pallas_call | solution.py:784
  166.8 8.0 %apply.1 = (f32[4,128,512]{2,1,0:T(8,128)S(1)}, f32[8,512]{1,0:T(8,128)S(1)}) custom-call(f32[896,512]{1,0:T(8,128)S(1)} %scan_y.1.later, f32[896,512]{1,0:T(8,128)S(1)} %get-tuple-element.24.across, f32[896,512]{1,0:T(8,128)S(1)} %get-tuple-element.25.down, f32[896,512]{1,0:T(8,128)S(1)} %get-tuple-element.18.own.pair, f32[896,512]{1,0:T(8,128)S(1)} %element.1.own), custom_call_target="tpu_custom_call" | custom-call | tf_op jit(solution)/shard_map/apply/pallas_call | solution.py:793
  174.8 15.9 %scatter_step.1 = (f32[4,128,512]{2,1,0:T(8,128)S(1)}, f32[4,8,512]{2,1,0:T(8,128)S(1)}) custom-call(f32[4,128,512]{2,1,0:T(8,128)S(1)} %get-tuple-element.26.slabs, f32[8,512]{1,0:T(8,128)S(1)} %get-tuple-element.27.mean), custom_call_target="tpu_custom_call" | custom-call | tf_op jit(solution)/shard_map/scatter_step/pallas_call | solution.py:701
  190.7 0.6 constant_dynamic-slice_fusion
  191.3 1.0 copy.9
  (1 shorter events, 0.0 us)
Async XLA Ops:
  0.6 1.2 copy-start
  1.9 0.7 copy-start.2
  18.9 1.0 copy-start.1
  19.9 0.7 copy-start.3
  20.6 0.7 copy-start.4

commit v5 on v4

--- a/solution.py
+++ b/solution.py
@@ -223,28 +223,40 @@
     pack_spread(out, lambda r, n, c: pred[r : r + n, c : c + B])
 
 
-def suffixes(count, me, own, other, total, rest, work, ready=lambda part: None, done=lambda part: None):
-    se, sl, sg, rh, rl, eh, el, lk = work
-
+def split_into(high, low, value):
+    for r in range(4):
+        rows = slice(r * B, r * B + B)
+        high[rows, :], low[rows, :] = split(value(rows))
+
+
+def chosen(me, own, other):
     def load(k, row, rows, lane=0, lanes=N):
         return jnp.where(k == me, own[row : row + rows, lane : lane + lanes], other(k, row, rows, lane, lanes))
 
-    last, steps = count - 1, count - 1
-
-    def split_into(high, low, value):
-        for r in range(4):
-            rows = slice(r * B, r * B + B)
-            high[rows, :], low[rows, :] = split(value(rows))
-
+    return load
+
+
+def split_gains(count, load, work):
+    eh, el = work[5:7]
+
+    def body(k, _):
+        split_into(eh.at[k], el.at[k], lambda rows: load(k, rows.start, B))
+        return 0
+
+    lax.fori_loop(0, count - 1, body, 0)
+
+
+def gains(count, me, load, total, rest, work):
+    se, _, _, rh, rl, eh, el, _ = work
+    last = count - 1
     if rest is not None:
 
         @pl.when(me == last)
         def _():
             same = lax.broadcasted_iota(jnp.int32, (N, N), 0) == lax.broadcasted_iota(jnp.int32, (N, N), 1)
             rest[0:N, :] = same.astype(F32)
-            rest[N:, :] = jnp.zeros((ROWS - N, N), F32)
-
-    def gains(t, _):
+
+    def step(t, _):
         k = last - 1 - t
         now = lax.rem(t, 2)
         if rest is not None:
@@ -258,21 +270,20 @@
         se[1 - now] = dot_s((eh[k], el[k]), (rh[...], rl[...]))
         return 0
 
-    ready(0)
-    if total is not None:
-        se[0] = load(last, 0, N)
-        lax.fori_loop(0, steps, gains, 0)
-        total[0:N, :] = se[steps % 2]
-        done(0)
-    else:
-
-        def just_split(t, _):
-            k = last - 1 - t
-            split_into(eh.at[k], el.at[k], lambda rows: load(k, rows.start, B))
-            return 0
-
-        lax.fori_loop(0, steps, just_split, 0)
-    ready(1)
+    se[0] = load(last, 0, N)
+    lax.fori_loop(0, last, step, 0)
+    total[0:N, :] = se[last % 2]
+
+
+def spreads(count, me, load, total, rest, work):
+    _, sl, sg, rh, rl, eh, el, lk = work
+    last = count - 1
+    if rest is not None:
+
+        @pl.when(me == last)
+        def _():
+            rest[N:, :] = jnp.zeros((ROWS - N, N), F32)
+
     unpack_spread(lambda r, n, c: load(last, r, n, c, B), sl.at[0])
     sg[0] = load(last, GROW, 8)
 
@@ -281,7 +292,7 @@
         ref[GROW : GROW + 8, :] = sg[slot]
         ref[GROW + 8 :, :] = jnp.zeros((ROWS - GROW - 8, N), F32)
 
-    def spreads(t, _):
+    def step(t, _):
         k = last - 1 - t
         now = lax.rem(t, 2)
         if rest is not None:
@@ -298,22 +309,20 @@
         sl[1 - now] = dot_s(half, e, 1) + lk[...]
         return 0
 
-    lax.fori_loop(0, steps, spreads, 0)
+    lax.fori_loop(0, last, step, 0)
     if total is not None:
-        keep(total, steps % 2)
-        done(1)
+        keep(total, last % 2)
+
+
+def from_slots(others):
+    return lambda k, row, rows, lane, lanes: others[k, row : row + rows, lane : lane + lanes]
 
 
 def scan_kernel(own, others, rest, *work):
-    suffixes(
-        4,
-        lax.axis_index("tm_0"),
-        own,
-        lambda k, row, rows, lane, lanes: others[k, row : row + rows, lane : lane + lanes],
-        None,
-        rest,
-        work,
-    )
+    me = lax.axis_index("tm_0")
+    load = chosen(me, own, from_slots(others))
+    split_gains(4, load, work)
+    spreads(4, me, load, None, rest, work)
 
 
 def apply_kernel(later, across, down, pair, own, out, mean_out, cov, mean, add, w, eh, el, lk):
@@ -380,11 +389,36 @@
     return ref.at[:, pl.ds(pl.multiple_of(lax.rem(j, 4) * B, B), B)]
 
 
-def gather_step_kernel(cov, mean, out, mean_out, relay, send, recv, relay_send, relay_recv, local, msend, mrecv):
+def gather_step_kernel(
+    cov,
+    mean,
+    noise,
+    blocks,
+    out,
+    mean_out,
+    mean_here,
+    noise_here,
+    blocks_here,
+    relay,
+    send,
+    recv,
+    relay_send,
+    relay_recv,
+    local,
+    msend,
+    mrecv,
+    small,
+):
     z, c = lax.axis_index("state"), lax.axis_index("tm_2")
     greet(column_peers(z, c))
     other = remote(mean, mean_out, msend, mrecv, {"tm_2": 1 - c})
     other.start()
+    here = [
+        pltpu.make_async_copy(src, dst, small.at[n])
+        for n, (src, dst) in enumerate(((mean, mean_here), (noise, noise_here), (blocks, blocks_here)))
+    ]
+    for copy_here in here:
+        copy_here.start()
 
     def start(src, dst, row, ssem, rsem, peer):
         for t in range(3):
@@ -454,6 +488,8 @@
             whole(out.at[s], send.at[0], recv.at[s]).wait_recv()
 
     other.wait()
+    for copy_here in here:
+        copy_here.wait()
 
 
 def scatter_step_kernel(slabs, mean, out, mean_out, relay, send, recv, relay_send, relay_recv, local, msend, mrecv):
@@ -579,17 +615,13 @@
                 n = cp.put(peer, z, row, rows, total.at[pl.ds(pl.multiple_of(row, 8), rows), :])
                 into.append((n, part, piece, j < len(pieces) // 2))
 
-    suffixes(
-        2,
-        c,
-        own,
-        lambda k, row, rows, lane, lanes: twin_buf[row : row + rows, lane : lane + lanes],
-        total,
-        None,
-        work,
-        lambda part: swaps[part].wait(),
-        first_hop,
-    )
+    load = chosen(c, own, lambda k, row, rows, lane, lanes: twin_buf[row : row + rows, lane : lane + lanes])
+    swaps[0].wait()
+    gains(2, c, load, total, None, work)
+    first_hop(0)
+    swaps[1].wait()
+    spreads(2, c, load, total, None, work)
+    first_hop(1)
 
     def hand(slot, part, piece):
         row, rows = rows_of(part, c, piece)
@@ -611,13 +643,14 @@
     cp.finish()
 
 
-R_PIECES = (((0, 32), (32, 32)), ((0, 24), (24, 24)))
-R_EIGHTH = (64, 48)
+QUARTER = (128, 96)
+PIECES = 4
 
 
 def ring_kernel(mine, axis, own, others, rest, out, total, *refs):
-    work, (send, recv) = refs[:8], refs[8:]
     z, c, a = lax.axis_index("state"), lax.axis_index("tm_2"), lax.axis_index(axis)
+    work, (send, recv, twin_send, twin_recv) = refs[:8], refs[8:]
+    me = lax.axis_index(mine)
     zu, zd, zo = lax.rem(z + 1, 4), lax.rem(z + 3, 4), lax.rem(z + 2, 4)
     au, ad, ao = lax.rem(a + 1, 4), lax.rem(a + 3, 4), lax.rem(a + 2, 4)
     up, down = {axis: au}, {axis: ad}
@@ -626,64 +659,77 @@
     barrier = pltpu.get_barrier_semaphore()
     for peer in peers:
         pl.semaphore_signal(barrier, inc=1, device_id=peer, device_id_type=MESH)
-    cp = Copies(out, send, recv)
     quarters = (z, zu)
     coming = (zd, zo)
-    ups, downs, twins, zs, tails = [], [], [], [], []
-
-    def rows_of(part, quarter, core, piece):
-        return (N if part else 0) + (2 * quarter + core) * R_EIGHTH[part] + piece[0], piece[1]
-
-    def first_hop(part):
-        if part == 0:
-            pl.semaphore_wait(barrier, len(peers))
-        pieces = R_PIECES[part]
-        for j, pair in enumerate(zip(pieces, pieces[::-1])):
+    load = chosen(me, own, from_slots(others))
+
+    def run(part):
+        base, size = N if part else 0, QUARTER[part] // PIECES
+        span = pl.ds(base, 4 * QUARTER[part])
+        if part:
+            split_gains(4, load, work)
+            spreads(4, me, load, total, rest, work)
+        else:
+            gains(4, me, load, total, rest, work)
+        pl.semaphore_wait(barrier, len(peers))
+        cp = Copies(out, send, recv)
+
+        def hand(src, dst, sem):
+            copy = remote(src, dst, twin_send.at[sem], twin_recv.at[sem], twin)
+            copy.start()
+
+        def row_of(quarter, j):
+            return pl.multiple_of(base + quarter * QUARTER[part] + j * size, 8)
+
+        ups, downs, zs, tails = [], [], [], []
+        for j in range(PIECES):
             for k in (0, 1):
-                for into, peer, piece in zip((ups, downs), (up, down), pair):
-                    row, rows = rows_of(part, quarters[k], c, piece)
-                    n = cp.put(peer, a, row, rows, total.at[pl.ds(pl.multiple_of(row, 8), rows), :])
-                    into.append((n, part, k, piece, j < len(pieces) // 2))
-
-    suffixes(
-        4,
-        lax.axis_index(mine),
-        own,
-        lambda k, row, rows, lane, lanes: others[k, row : row + rows, lane : lane + lanes],
-        total,
-        rest,
-        work,
-        done=first_hop,
-    )
-
-    def spread(slot, part, k, piece):
-        row, rows = rows_of(part, quarters[k], c, piece)
-        zs.append((cp.put(below if k else above, slot, row, rows), slot, part, k, piece))
-        twins.append((cp.put(twin, slot, row, rows), slot, rows_of(part, quarters[k], 1 - c, piece)))
-
-    def take(count):
-        while len(zs) > count:
-            n, slot, part, k, piece = zs.pop(0)
-            row, rows = rows_of(part, coming[k], c, piece)
-            cp.arrived(n, slot, row, rows)
-            twins.append((cp.put(twin, slot, row, rows), slot, rows_of(part, coming[k], 1 - c, piece)))
-
-    for pair in zip(ups, downs):
-        for (n, part, k, piece, further), slot, peer in zip(pair, (ad, au), (up, down)):
-            row, rows = rows_of(part, quarters[k], c, piece)
-            cp.arrived(n, slot, row, rows)
-            if further:
-                tails.append((cp.put(peer, slot, row, rows), part, k, piece))
-            spread(slot, part, k, piece)
-    for n, part, k, piece in tails:
-        row, rows = rows_of(part, quarters[k], c, piece)
-        cp.arrived(n, ao, row, rows)
-        spread(ao, part, k, piece)
-        take(len(zs) - 2)
-    take(0)
-    for n, slot, (row, rows) in twins:
-        cp.arrived(n, slot, row, rows)
-    cp.finish()
+                for into, peer, jj in ((ups, up, j), (downs, down, PIECES - 1 - j)):
+                    row = row_of(quarters[k], jj)
+                    n = cp.put(peer, a, row, size, total.at[pl.ds(row, size), :])
+                    into.append((n, k, jj, j < PIECES // 2))
+        hand(total.at[span], total.at[span], 0)
+        hand(rest.at[span], rest.at[span], 1)
+
+        def pass_on(slot, row):
+            place = out.at[slot, pl.ds(row, size), :]
+            hand(place, place, 2)
+
+        def spread(slot, k, j):
+            row = row_of(quarters[k], j)
+            zs.append((cp.put(below if k else above, slot, row, size), slot, k, j))
+            pass_on(slot, row)
+
+        def take(count):
+            while len(zs) > count:
+                n, slot, k, j = zs.pop(0)
+                row = row_of(coming[k], j)
+                cp.arrived(n, slot, row, size)
+                pass_on(slot, row)
+
+        for pair in zip(ups, downs):
+            for (n, k, j, further), slot, peer in zip(pair, (ad, au), (up, down)):
+                row = row_of(quarters[k], j)
+                cp.arrived(n, slot, row, size)
+                if further:
+                    tails.append((cp.put(peer, slot, row, size), k, j))
+                spread(slot, k, j)
+        for n, k, j in tails:
+            cp.arrived(n, ao, row_of(quarters[k], j), size)
+            spread(ao, k, j)
+            take(len(zs) - 2)
+        take(0)
+        cp.finish()
+        other = pl.ds(0 if part else N, 4 * QUARTER[1 - part])
+        for sem, ref in enumerate((total, rest)):
+            remote(ref.at[span], ref.at[span], twin_send.at[sem], twin_recv.at[sem], twin).wait_send()
+            remote(ref.at[other], ref.at[other], twin_send.at[sem], twin_recv.at[sem], twin).wait_recv()
+        sent, came = out.at[0:3, span], out.at[0:3, other]
+        remote(sent, sent, twin_send.at[2], twin_recv.at[2], twin).wait_send()
+        remote(came, came, twin_send.at[2], twin_recv.at[2], twin).wait_recv()
+
+    for part in (0, 1):
+        pl.when(c == part)(partial(run, part))
 
 
 def shape(*dims, dtype=F32):
@@ -697,12 +743,12 @@
 DMA = pltpu.SemaphoreType.DMA
 
 
-def comm(kernel, name, collective_id, outs, scratch, *args, out_spec=ANY):
+def comm(kernel, name, collective_id, outs, scratch, *args, in_spec=ANY, out_spec=ANY):
     return pl.pallas_call(
         kernel,
         name=name,
         out_shape=outs,
-        in_specs=[ANY] * len(args),
+        in_specs=[in_spec] * len(args),
         out_specs=jax.tree.map(lambda _: out_spec, outs),
         scratch_shapes=scratch,
         compiler_params=pltpu.CompilerParams(
@@ -740,7 +786,7 @@
         out_shape=(packet, shape(4, ROWS, N), packet),
         in_specs=[VM, VM],
         out_specs=(VM, VM, VM),
-        scratch_shapes=suffix_work(4) + [DMA((96,)), DMA((96,))],
+        scratch_shapes=suffix_work(4) + [DMA((48,)), DMA((48,)), DMA((3,)), DMA((3,))],
         compiler_params=params(RING_LIMIT, collective_id=collective_id, has_side_effects=True),
     )(own, others)
 
@@ -750,14 +796,17 @@
 
 def on_device(filtered_cov, filtered_mean, noise_var, trans_blocks, pattern):
     z = lax.axis_index("state")
-    cov, twin_mean = comm(
+    cov, twin_mean, mean_here, noise_here, blocks_here = comm(
         gather_step_kernel,
         "gather_step",
         0,
-        (shape(4, B, N), shape(4, N)),
-        [pltpu.VMEM((2, B, N), F32), DMA((4,)), DMA((4,)), DMA((2,)), DMA((2,)), DMA, DMA, DMA],
+        (shape(4, B, N), shape(4, N), shape(4, N), shape(1, N), shape(4, 2, B, B)),
+        [pltpu.VMEM((2, B, N), F32), DMA((4,)), DMA((4,)), DMA((2,)), DMA((2,)), DMA, DMA, DMA, DMA((3,))],
         filtered_cov,
         filtered_mean,
+        noise_var.reshape(1, N),
+        trans_blocks,
+        in_spec=pl.BlockSpec(memory_space=pltpu.HBM),
         out_spec=VM,
     )
     own = pl.pallas_call(
@@ -768,7 +817,7 @@
         out_specs=VM,
         scratch_shapes=[pltpu.VMEM((N, N), F32)] * 3 + [pltpu.VMEM((8, N), F32), pltpu.VMEM((N, N), F32), pltpu.VMEM((B, B), F32)],
         compiler_params=params(BIG),
-    )(pattern, cov, filtered_mean, twin_mean, noise_var.reshape(1, N), trans_blocks)
+    )(pattern, cov, mean_here, twin_mean, noise_here, blocks_here)
     packet, packets = shape(ROWS, N), shape(4, ROWS, N)
     pair, pairs = pl.pallas_call(
         pair_kernel,

time: 193 us -> 187 us (0.969)
  Pallas kernels: 185 us -> 180 us
    pallas_call x2, Pallas kernels: 62.4 us -> 57.1 us  [ring(): pl.pallas_call(partial(ring_kernel, mine, axis), name=name, out_shape=(pa...]
    unnamed x12 -> x10, local copies, waits for them, and re-layouts: 6.07 us -> 5.37 us
where the time goes in v5:
time: 187 us
  Pallas kernels  180 us (96%)
  local copies, waits for them, and re-layouts  5.96 us (3%)
    pallas_call x2, Pallas kernels, ring(): pl.pallas_call(partial(ring_kernel, mine, axis), name=name, out_shape=(pa...  57.1 us
    pallas_call x1, Pallas kernels, on_device(): pl.pallas_call(pair_kernel, name='pair', out_shape=(packet, packets), in_...  39.4 us
    pallas_call x1, Pallas kernels, on_device(): pl.pallas_call(element_kernel, name='element', out_shape=shape(ROWS, N),...  36.2 us
    pallas_call x2, Pallas kernels, comm(): pl.pallas_call(kernel, name=name, out_shape=outs, in_specs=[in_spec] * le...  31.8 us
    pallas_call x1, Pallas kernels, on_device(): pl.pallas_call(apply_kernel, name='apply', out_shape=(shape(4, B, N), sha...  8.02 us
    pallas_call x1, Pallas kernels, on_device(): pl.pallas_call(scan_kernel, name='scan_y', out_shape=packet, in_specs=[VM...  7.4 us
    unnamed x10, local copies, waits for them, and re-layouts  5.37 us

profile of v5, /device:TPU:1, one launch (start us, length us, event | category | flops | bytes accessed | tf_op | source)
XLA Modules:
  0.0 186.6 jit_solution(11866228169743406879)
XLA Ops:
  0.6 0.0 copy-start
  0.6 1.2 copy-done
  1.9 0.0 copy-start.1
  1.9 1.0 copy-done.1
  2.9 0.0 copy-start.2
  2.9 0.7 copy-done.2
  3.6 0.0 copy-start.3
  3.6 0.7 copy-done.3
  4.3 15.6 %gather_step.1 = (f32[4,128,512]{2,1,0:T(8,128)S(1)}, f32[4,512]{1,0:T(4,128)S(1)}, f32[4,512]{1,0:T(4,128)S(1)}, f32[1,512]{1,0:T(1,128)S(1)}, f32[4,2,128,128]{3,2,1,0:T(8,128)S(1)}) custom-call(f32[4,128,512]{2,1,0:T(8,128)S(1)} %copy-done, f32[4,512]{1,0:T(4,128)S(1)} %copy-done.2, f32[1,512]{1,0:T(1,128)S(1)} %bitcast.2, f32[4,2,128,128]{3,2,1,0:T(8,128)S(1)} %copy-done.1), custom_call_target="tpu_custom_call" | custom-call | tf_op jit(solution)/shard_map/gather_step/pallas_call | solution.py:747
  19.9 0.8 copy.7.pattern
  20.7 36.2 %element.1.own = f32[896,512]{1,0:T(8,128)S(1)} custom-call(s32[4,2]{1,0:T(4,128)S(1)} %copy.7.pattern, f32[4,128,512]{2,1,0:T(8,128)S(1)} %get-tuple-element.19.cov_in, f32[4,512]{1,0:T(4,128)S(1)} %get-tuple-element.20.mean_a, f32[4,512]{1,0:T(4,128)S(1)} %get-tuple-element.21.mean_b, f32[1,512]{1,0:T(1,128)S(1)} %get-tuple-element.22.noise, ...), custom_call_target="tpu_custom_call" | custom-call | tf_op jit(solution)/shard_map/element/pallas_call | solution.py:812
  56.9 39.4 %pair.1 = (f32[896,512]{1,0:T(8,128)S(1)}, f32[4,896,512]{2,1,0:T(8,128)S(1)}) custom-call(f32[896,512]{1,0:T(8,128)S(1)} %element.1.own), custom_call_target="tpu_custom_call" | custom-call | tf_op jit(solution)/shard_map/pair/pallas_call | solution.py:822
  96.3 26.7 %ring_x.1 = (f32[896,512]{1,0:T(8,128)S(1)}, f32[4,896,512]{2,1,0:T(8,128)S(1)}, f32[896,512]{1,0:T(8,128)S(1)}) custom-call(f32[896,512]{1,0:T(8,128)S(1)} %get-tuple-element.24.own.pair, f32[4,896,512]{2,1,0:T(8,128)S(1)} %get-tuple-element.25.others), custom_call_target="tpu_custom_call" | custom-call | tf_op jit(solution)/shard_map/ring_x/pallas_call | solution.py:783
  123.1 30.4 %ring_y.1 = (f32[896,512]{1,0:T(8,128)S(1)}, f32[4,896,512]{2,1,0:T(8,128)S(1)}, f32[896,512]{1,0:T(8,128)S(1)}) custom-call(f32[896,512]{1,0:T(8,128)S(1)} %get-tuple-element.26.own, f32[4,896,512]{2,1,0:T(8,128)S(1)} %get-tuple-element.27.others), custom_call_target="tpu_custom_call" | custom-call | tf_op jit(solution)/shard_map/ring_y/pallas_call | solution.py:783
  153.4 7.4 %scan_y.1.later = f32[896,512]{1,0:T(8,128)S(1)} custom-call(f32[896,512]{1,0:T(8,128)S(1)} %get-tuple-element.28.own, f32[4,896,512]{2,1,0:T(8,128)S(1)} %get-tuple-element.29.others), custom_call_target="tpu_custom_call" | custom-call | tf_op jit(solution)/shard_map/scan_y/pallas_call | solution.py:833
  160.8 8.0 %apply.1 = (f32[4,128,512]{2,1,0:T(8,128)S(1)}, f32[8,512]{1,0:T(8,128)S(1)}) custom-call(f32[896,512]{1,0:T(8,128)S(1)} %scan_y.1.later, f32[896,512]{1,0:T(8,128)S(1)} %get-tuple-element.30.across, f32[896,512]{1,0:T(8,128)S(1)} %get-tuple-element.31.down, f32[896,512]{1,0:T(8,128)S(1)} %get-tuple-element.24.own.pair, f32[896,512]{1,0:T(8,128)S(1)} %element.1.own), custom_call_target="tpu_custom_call" | custom-call | tf_op jit(solution)/shard_map/apply/pallas_call | solution.py:842
  168.9 16.1 %scatter_step.1 = (f32[4,128,512]{2,1,0:T(8,128)S(1)}, f32[4,8,512]{2,1,0:T(8,128)S(1)}) custom-call(f32[4,128,512]{2,1,0:T(8,128)S(1)} %get-tuple-element.32.slabs, f32[8,512]{1,0:T(8,128)S(1)} %get-tuple-element.33.mean), custom_call_target="tpu_custom_call" | custom-call | tf_op jit(solution)/shard_map/scatter_step/pallas_call | solution.py:747
  185.0 0.6 constant_dynamic-slice_fusion
  185.6 1.0 copy.9
  (1 shorter events, 0.0 us)
Async XLA Ops:
  0.6 1.2 copy-start
  1.9 1.0 copy-start.1
  2.9 0.7 copy-start.2
  3.6 0.7 copy-start.3

commit v6 on v5

--- a/solution.py
+++ b/solution.py
@@ -71,10 +71,15 @@
             full_ref[j * B : j * B + B, i * B : i * B + B] = jnp.transpose(block)
 
 
+def tree_sum(terms):
+    while len(terms) > 1:
+        terms = [sum(terms[i + 1 : i + 2], terms[i]) for i in range(0, len(terms), 2)]
+    return terms[0]
+
+
 def small_mul(a, b):
     return [
-        [sum((a[i][t] * b[t][j] for t in range(1, len(b))), a[i][0] * b[0][j]) for j in range(len(b[0]))]
-        for i in range(len(a))
+        [tree_sum([a[i][t] * b[t][j] for t in range(len(b))]) for j in range(len(b[0]))] for i in range(len(a))
     ]
 
 
@@ -136,7 +141,7 @@
                         new = jnp.where(row_id == s, new_rows[s], new)
                 else:
                     new = jnp.where(inside, 0.0, vs[k])
-                    new -= sum((cols[s][k] * new_rows[s] for s in range(1, 8)), cols[0][k] * new_rows[0])
+                    new -= tree_sum([cols[s][k] * new_rows[s] for s in range(8)])
                 vs[k] = new
         done = jnp.concatenate(vs, axis=0)
         rest = jnp.where(lanes < PANEL, 0.0, x) - dot6(top, done, 0, 0)
@@ -316,51 +321,6 @@
 
 def from_slots(others):
     return lambda k, row, rows, lane, lanes: others[k, row : row + rows, lane : lane + lanes]
-
-
-def scan_kernel(own, others, rest, *work):
-    me = lax.axis_index("tm_0")
-    load = chosen(me, own, from_slots(others))
-    split_gains(4, load, work)
-    spreads(4, me, load, None, rest, work)
-
-
-def apply_kernel(later, across, down, pair, own, out, mean_out, cov, mean, add, w, eh, el, lk):
-    unpack_spread(lambda r, n, c: later[r : r + n, c : c + B], cov)
-    mean[...] = later[GROW : GROW + 8, :]
-
-    def take(load):
-        for r in range(4):
-            rows = slice(r * B, r * B + B)
-            h, l = split(load(r * B, B))
-            eh[rows, :], el[rows, :] = h, l
-        unpack_spread(lambda r, n, c: load(r, n, c, B), lk)
-        add[...] = load(GROW, 8)
-
-    loads = (
-        lambda r, n, c=0, m=N: across[r : r + n, c : c + m],
-        lambda r, n, c=0, m=N: down[r : r + n, c : c + m],
-        lambda r, n, c=0, m=N: jnp.where(
-            lax.axis_index("tm_2") == 0, pair[r : r + n, c : c + m], own[r : r + n, c : c + m]
-        ),
-    )
-
-    def push(t, _):
-        for k in range(3):
-            pl.when(t == k)(partial(take, loads[k]))
-        for r in range(4):
-            rows = slice(r * B, r * B + B)
-            h, l = split(cov[rows, :])
-            w[0, rows, :], w[1, rows, :] = h, l
-        e = (eh[...], el[...])
-        mean[...] = dot_s(split(mean[...]), e, 1) + add[...]
-        cov[...] = dot_s(split(dot_s(e, (w[0], w[1]))), e, 1) + lk[...]
-        return 0
-
-    lax.fori_loop(0, 3, push, 0)
-    for z in range(4):
-        out[z] = cov[z * B : z * B + B, :]
-    mean_out[...] = mean[...]
 
 
 def greet(peers):
@@ -492,18 +452,115 @@
         copy_here.wait()
 
 
-def scatter_step_kernel(slabs, mean, out, mean_out, relay, send, recv, relay_send, relay_recv, local, msend, mrecv):
-    z, c = lax.axis_index("state"), lax.axis_index("tm_2")
-    greet(column_peers(z, c))
+def final_kernel(
+    row,
+    rows,
+    across,
+    down,
+    pair,
+    own,
+    out,
+    mean_out,
+    cov,
+    mean,
+    add,
+    relay,
+    sl,
+    sg,
+    rh,
+    rl,
+    eh,
+    el,
+    lk,
+    send,
+    recv,
+    relay_send,
+    relay_recv,
+    local,
+    msend,
+    mrecv,
+):
+    z, c, me = lax.axis_index("state"), lax.axis_index("tm_2"), lax.axis_index("tm_0")
+    barrier = pltpu.get_barrier_semaphore()
+    peers = column_peers(z, c)
+    for peer in peers:
+        pl.semaphore_signal(barrier, inc=1, device_id=peer, device_id_type=MESH)
+    load = chosen(me, row, from_slots(rows))
+
+    @pl.when(me == 3)
+    def _():
+        cov[...] = jnp.zeros((N, N), F32)
+        mean[...] = jnp.zeros((8, N), F32)
+
+    @pl.when(me == 2)
+    def _():
+        unpack_spread(lambda r, n, c: load(3, r, n, c, B), cov)
+        mean[...] = load(3, GROW, 8)
+
+    @pl.when(me < 2)
+    def _():
+        unpack_spread(lambda r, n, c: load(3, r, n, c, B), sl)
+        sg[...] = load(3, GROW, 8)
+
+    def take(get):
+        split_into(eh, el, lambda r: get(r.start, B))
+        unpack_spread(lambda r, n, c: get(r, n, c, B), lk)
+        add[...] = get(GROW, 8)
+
+    def push(state, offset):
+        split_into(rh, rl, lambda r: state[r, :])
+        e = (eh[...], el[...])
+        offset[...] = dot_s(split(offset[...]), e, 1) + add[...]
+        state[...] = dot_s(split(dot_s(e, (rh[...], rl[...]))), e, 1) + lk[...]
+
+    choices = (
+        lambda r, n, c=0, m=N: load(2, r, n, c, m),
+        lambda r, n, c=0, m=N: load(1, r, n, c, m),
+        lambda r, n, c=0, m=N: across[r : r + n, c : c + m],
+        lambda r, n, c=0, m=N: down[r : r + n, c : c + m],
+        lambda r, n, c=0, m=N: jnp.where(
+            lax.axis_index("tm_2") == 0, pair[r : r + n, c : c + m], own[r : r + n, c : c + m]
+        ),
+    )
+
+    def early(t, _):
+        @pl.when(me < 2 - t)
+        def _():
+            for k in range(2):
+                pl.when(t == k)(partial(take, choices[k]))
+            push(sl, sg)
+
+        @pl.when(me == 1 - t)
+        def _():
+            cov[...] = sl[...]
+            mean[...] = sg[...]
+
+        return 0
+
+    lax.fori_loop(0, 2, early, 0)
+
+    def late(t, _):
+        for k in range(3):
+            pl.when(t == k)(partial(take, choices[2 + k]))
+        push(cov, mean)
+        return 0
+
+    lax.fori_loop(0, 3, late, 0)
+    pl.semaphore_wait(barrier, len(peers))
+
     core = z // 2
     slot = 2 * lax.rem(z, 2) + c
     opposite = lax.rem(z + 2, 4)
     onward = lax.rem(z + 1 + 2 * c, 4)
-    far = remote(slabs.at[opposite], relay, relay_send.at[0], relay_recv, {"state": onward})
+
+    def slab(t):
+        return cov.at[pl.ds(pl.multiple_of(t * B, B), B), :]
+
+    far = remote(slab(opposite), relay, relay_send.at[0], relay_recv, {"state": onward})
     far.start()
 
     def copy(t):
-        return remote(slabs.at[t], out.at[slot], send.at[t], recv.at[slot], {"state": t, "tm_2": core})
+        return remote(slab(t), out.at[slot], send.at[t], recv.at[slot], {"state": t, "tm_2": core})
 
     def mean_copy(t):
         return remote(mean, mean_out.at[slot], msend.at[t], mrecv.at[slot], {"state": t, "tm_2": core})
@@ -512,7 +569,7 @@
         return (z == t) & (c == core)
 
     def copies(t):
-        return pltpu.make_async_copy(slabs.at[t], out.at[slot], local.at[0]), pltpu.make_async_copy(
+        return pltpu.make_async_copy(slab(t), out.at[slot], local.at[0]), pltpu.make_async_copy(
             mean, mean_out.at[slot], local.at[1]
         )
 
@@ -562,7 +619,7 @@
 
         @pl.when(jnp.logical_not((z == 2 * c + i // 2) & (c == i % 2)))
         def _():
-            remote(slabs.at[0], out.at[i], send.at[0], recv.at[i], {"state": 0, "tm_2": 0}).wait_recv()
+            remote(slab(0), out.at[i], send.at[0], recv.at[i], {"state": 0, "tm_2": 0}).wait_recv()
             remote(mean, mean_out.at[i], msend.at[0], mrecv.at[i], {"state": 0, "tm_2": 0}).wait_recv()
 
 
@@ -743,7 +800,7 @@
 DMA = pltpu.SemaphoreType.DMA
 
 
-def comm(kernel, name, collective_id, outs, scratch, *args, in_spec=ANY, out_spec=ANY):
+def comm(kernel, name, collective_id, outs, scratch, *args, limit, in_spec=ANY, out_spec=ANY):
     return pl.pallas_call(
         kernel,
         name=name,
@@ -752,19 +809,12 @@
         out_specs=jax.tree.map(lambda _: out_spec, outs),
         scratch_shapes=scratch,
         compiler_params=pltpu.CompilerParams(
-            collective_id=collective_id, has_side_effects=True, vmem_limit_bytes=4 * 1024 * 1024
+            collective_id=collective_id, has_side_effects=True, vmem_limit_bytes=limit
         ),
     )(*args)
 
 
 BIG = 32 * 1024 * 1024
-WORK = [
-    pltpu.VMEM((512, 512), BF16),
-    pltpu.VMEM((512, 512), BF16),
-    pltpu.VMEM((512, 512), F32),
-]
-
-
 def suffix_work(count):
     return [
         pltpu.VMEM((2, N, N), F32),
@@ -792,6 +842,7 @@
 
 
 RING_LIMIT = 24 * 1024 * 1024
+FIRST_LIMIT = 4 * 1024 * 1024
 
 
 def on_device(filtered_cov, filtered_mean, noise_var, trans_blocks, pattern):
@@ -806,7 +857,7 @@
         filtered_mean,
         noise_var.reshape(1, N),
         trans_blocks,
-        in_spec=pl.BlockSpec(memory_space=pltpu.HBM),
+        limit=FIRST_LIMIT,
         out_spec=VM,
     )
     own = pl.pallas_call(
@@ -830,35 +881,18 @@
     )(own)
     down, columns, column = ring("ring_x", 3, "state", "tm_1", pair, pairs)
     across, rows, row = ring("ring_y", 4, "tm_1", "tm_0", column, columns)
-    later = pl.pallas_call(
-        scan_kernel,
-        name="scan_y",
-        out_shape=packet,
-        in_specs=[VM, VM],
-        out_specs=VM,
-        scratch_shapes=suffix_work(4),
-        compiler_params=params(BIG),
-    )(row, rows)
-    slabs, mean = pl.pallas_call(
-        apply_kernel,
-        name="apply",
-        out_shape=(shape(4, B, N), shape(8, N)),
-        in_specs=[VM] * 5,
+    half = pltpu.VMEM((N, N), BF16)
+    smooth_cov, means = pl.pallas_call(
+        final_kernel,
+        name="final",
+        out_shape=(shape(4, B, N), shape(4, 8, N)),
+        in_specs=[VM] * 6,
         out_specs=(VM, VM),
-        scratch_shapes=[pltpu.VMEM((N, N), F32), pltpu.VMEM((8, N), F32), pltpu.VMEM((8, N), F32), pltpu.VMEM((2, N, N), BF16)]
-        + WORK,
-        compiler_params=params(BIG),
-    )(later, across, down, pair, own)
-    smooth_cov, means = comm(
-        scatter_step_kernel,
-        "scatter_step",
-        5,
-        (shape(4, B, N), shape(4, 8, N)),
-        [pltpu.VMEM((B, N), F32), DMA((4,)), DMA((4,)), DMA((2,)), DMA, DMA((2,)), DMA((4,)), DMA((4,))],
-        slabs,
-        mean,
-        out_spec=VM,
-    )
+        scratch_shapes=[pltpu.VMEM((N, N), F32), pltpu.VMEM((8, N), F32), pltpu.VMEM((8, N), F32), pltpu.VMEM((B, N), F32)]
+        + [pltpu.VMEM((N, N), F32), pltpu.VMEM((8, N), F32), half, half, half, half, pltpu.VMEM((N, N), F32)]
+        + [DMA((4,)), DMA((4,)), DMA((2,)), DMA, DMA((2,)), DMA((4,)), DMA((4,))],
+        compiler_params=params(RING_LIMIT, collective_id=5, has_side_effects=True),
+    )(row, rows, across, down, pair, own)
     return lax.dynamic_slice_in_dim(means[:, 0, :], z * B, B, 1), smooth_cov
 
 

time: 187 us -> 181 us (0.968)
  Pallas kernels: 180 us -> 174 us
    pallas_call x2 -> x1, Pallas kernels: 31.8 us -> 15.6 us  [comm(): pl.pallas_call(kernel, name=name, out_shape=outs, in_specs=[in_spec] * le...]
    pallas_call x2 -> x1, Pallas kernels: 15.4 us -> 28 us  [on_device(): pl.pallas_call(final_kernel, name='final', out_shape=(shape(4, B, N), sha...]
    pallas_call x1, Pallas kernels: 36.2 us -> 34.3 us  [on_device(): pl.pallas_call(element_kernel, name='element', out_shape=shape(ROWS, N),...]
where the time goes in v6:
time: 181 us
  Pallas kernels  174 us (96%)
  local copies, waits for them, and re-layouts  5.96 us (3%)
    pallas_call x2, Pallas kernels, ring(): pl.pallas_call(partial(ring_kernel, mine, axis), name=name, out_shape=(pa...  57.1 us
    pallas_call x1, Pallas kernels, on_device(): pl.pallas_call(pair_kernel, name='pair', out_shape=(packet, packets), in_...  39.4 us
    pallas_call x1, Pallas kernels, on_device(): pl.pallas_call(element_kernel, name='element', out_shape=shape(ROWS, N),...  34.3 us
    pallas_call x1, Pallas kernels, on_device(): pl.pallas_call(final_kernel, name='final', out_shape=(shape(4, B, N), sha...  28 us
    pallas_call x1, Pallas kernels, comm(): pl.pallas_call(kernel, name=name, out_shape=outs, in_specs=[in_spec] * le...  15.6 us
    unnamed x10, local copies, waits for them, and re-layouts  5.37 us

profile of v6, /device:TPU:1, one launch (start us, length us, event | category | flops | bytes accessed | tf_op | source)
XLA Modules:
  0.0 181.0 jit_solution(5463610657426365753)
XLA Ops:
  0.6 0.0 copy-start
  0.6 1.2 copy-done
  1.9 0.0 copy-start.1
  1.9 1.0 copy-done.1
  2.9 0.0 copy-start.2
  2.9 0.7 copy-done.2
  3.6 0.0 copy-start.3
  3.6 0.7 copy-done.3
  4.3 15.6 %gather_step.1 = (f32[4,128,512]{2,1,0:T(8,128)S(1)}, f32[4,512]{1,0:T(4,128)S(1)}, f32[4,512]{1,0:T(4,128)S(1)}, f32[1,512]{1,0:T(1,128)S(1)}, f32[4,2,128,128]{3,2,1,0:T(8,128)S(1)}) custom-call(f32[4,128,512]{2,1,0:T(8,128)S(1)} %copy-done, f32[4,512]{1,0:T(4,128)S(1)} %copy-done.2, f32[1,512]{1,0:T(1,128)S(1)} %bitcast.2, f32[4,2,128,128]{3,2,1,0:T(8,128)S(1)} %copy-done.1), custom_call_target="tpu_custom_call" | custom-call | tf_op jit(solution)/shard_map/gather_step/pallas_call | solution.py:804
  19.9 0.8 copy.7.pattern
  20.7 34.3 %element.1.own = f32[896,512]{1,0:T(8,128)S(1)} custom-call(s32[4,2]{1,0:T(4,128)S(1)} %copy.7.pattern, f32[4,128,512]{2,1,0:T(8,128)S(1)} %get-tuple-element.17.cov_in, f32[4,512]{1,0:T(4,128)S(1)} %get-tuple-element.18.mean_a, f32[4,512]{1,0:T(4,128)S(1)} %get-tuple-element.19.mean_b, f32[1,512]{1,0:T(1,128)S(1)} %get-tuple-element.20.noise, ...), custom_call_target="tpu_custom_call" | custom-call | tf_op jit(solution)/shard_map/element/pallas_call | solution.py:863
  55.0 39.4 %pair.1 = (f32[896,512]{1,0:T(8,128)S(1)}, f32[4,896,512]{2,1,0:T(8,128)S(1)}) custom-call(f32[896,512]{1,0:T(8,128)S(1)} %element.1.own), custom_call_target="tpu_custom_call" | custom-call | tf_op jit(solution)/shard_map/pair/pallas_call | solution.py:873
  94.4 26.7 %ring_x.1 = (f32[896,512]{1,0:T(8,128)S(1)}, f32[4,896,512]{2,1,0:T(8,128)S(1)}, f32[896,512]{1,0:T(8,128)S(1)}) custom-call(f32[896,512]{1,0:T(8,128)S(1)} %get-tuple-element.22.own.pair, f32[4,896,512]{2,1,0:T(8,128)S(1)} %get-tuple-element.23.others), custom_call_target="tpu_custom_call" | custom-call | tf_op jit(solution)/shard_map/ring_x/pallas_call | solution.py:833
  121.1 30.3 %ring_y.1 = (f32[896,512]{1,0:T(8,128)S(1)}, f32[4,896,512]{2,1,0:T(8,128)S(1)}, f32[896,512]{1,0:T(8,128)S(1)}) custom-call(f32[896,512]{1,0:T(8,128)S(1)} %get-tuple-element.24.own, f32[4,896,512]{2,1,0:T(8,128)S(1)} %get-tuple-element.25.others), custom_call_target="tpu_custom_call" | custom-call | tf_op jit(solution)/shard_map/ring_y/pallas_call | solution.py:833
  151.4 28.0 %final.1 = (f32[4,128,512]{2,1,0:T(8,128)S(1)}, f32[4,8,512]{2,1,0:T(8,128)S(1)}) custom-call(f32[896,512]{1,0:T(8,128)S(1)} %get-tuple-element.26.row, f32[4,896,512]{2,1,0:T(8,128)S(1)} %get-tuple-element.27.rows, f32[896,512]{1,0:T(8,128)S(1)} %get-tuple-element.28.across, f32[896,512]{1,0:T(8,128)S(1)} %get-tuple-element.29.down, ...), custom_call_target="tpu_custom_call" | custom-call | tf_op jit(solution)/shard_map/final/pallas_call | solution.py:885
  179.5 0.6 constant_dynamic-slice_fusion
  180.1 1.0 copy.9
  (1 shorter events, 0.0 us)
Async XLA Ops:
  0.6 1.2 copy-start
  1.9 1.0 copy-start.1
  2.9 0.7 copy-start.2
  3.6 0.7 copy-start.3

commit v7 on v6

--- a/solution.py
+++ b/solution.py
@@ -150,8 +150,8 @@
     return -lax.fori_loop(0, B // PANEL, body, block)
 
 
-def element_kernel(pattern, cov_in, mean_a, mean_b, noise, blocks, out, left, pred, sol, upd, cov, inv_ref):
-    y, x, c, z = (lax.axis_index(a) for a in ("tm_0", "tm_1", "tm_2", "state"))
+def predict_kernel(pattern, cov_in, mean_a, mean_b, noise, blocks, cov, left, pred, vectors):
+    c, z = lax.axis_index("tm_2"), lax.axis_index("state")
     for i in range(4):
         for t in range(3):
             lanes = slice((i + t) % 4 * B, (i + t) % 4 * B + B)
@@ -168,7 +168,7 @@
 
     place = lax.rem(2 * z + c, 4)
     mean = jnp.where(z // 2 == c, mean_a[pl.ds(place, 1), :], mean_b[pl.ds(place, 1), :])
-    upd[0:8, :] = jnp.broadcast_to(mean, (8, N))
+    vectors[0:8, :] = jnp.broadcast_to(mean, (8, N))
     pushed = []
     for r in range(4):
         t0, t1 = tb(r, 0), tb(r, 1)
@@ -176,10 +176,10 @@
             t1, rows_of(cov, pattern[r, 1])
         )
         pushed.append(
-            dot6(lanes_of(upd, 0, 8, pattern[r, 0]), t0, 1)
-            + dot6(lanes_of(upd, 0, 8, pattern[r, 1]), t1, 1)
+            dot6(lanes_of(vectors, 0, 8, pattern[r, 0]), t0, 1)
+            + dot6(lanes_of(vectors, 0, 8, pattern[r, 1]), t1, 1)
         )
-    pushed = jnp.concatenate(pushed, axis=1)
+    vectors[8:16, :] = jnp.concatenate(pushed, axis=1)
     eye = lax.broadcasted_iota(jnp.int32, (B, B), 0) == lax.broadcasted_iota(jnp.int32, (B, B), 1)
     for r in range(4):
         rows = (r + 1) * B
@@ -189,6 +189,11 @@
         pred[0:rows, r * B : r * B + B] = value
         q = jnp.where(eye, jnp.broadcast_to(noise[0:1, r * B : r * B + B], (B, B)), 0.0)
         pred[r * B : rows, r * B : r * B + B] += q
+
+
+def element(cov, left, pred_in, vectors, out, pred, sol, inv_ref, gain_ready):
+    y, x, c, z = (lax.axis_index(a) for a in ("tm_0", "tm_1", "tm_2", "state"))
+    pred[...] = pred_in[...]
     sol[...] = left[...]
 
     def eliminate(k, _):
@@ -222,7 +227,8 @@
             out[i * B : i * B + B, j * B : j * B + B] = (
                 jnp.transpose(sol[j * B : j * B + B, i * B : i * B + B]) * keep
             )
-    out[GROW : GROW + 8, :] = jnp.broadcast_to(mean, (8, N)) - keep * dot6(pushed, sol[...])
+    gain_ready()
+    out[GROW : GROW + 8, :] = vectors[0:8, :] - keep * dot6(vectors[8:16, :], sol[...])
     out[GROW + 8 :, :] = jnp.zeros((ROWS - GROW - 8, N), F32)
     pred[...] = cov[...] - dot6(out[0:N, :], left[...])
     pack_spread(out, lambda r, n, c: pred[r : r + n, c : c + B])
@@ -648,16 +654,25 @@
 Z_HALF = (256, 168)
 
 
-def pair_kernel(own, total, out, twin_buf, *refs):
-    work, (swap_send, swap_recv, send, recv) = refs[:8], refs[8:]
+def pair_kernel(cov, left, pred, vectors, own, total, out, twin_buf, *refs):
+    scratch, work, (swap_send, swap_recv, send, recv) = refs[:3], refs[3:11], refs[11:]
     z, c = lax.axis_index("state"), lax.axis_index("tm_2")
     zu, zd, zo = lax.rem(z + 1, 4), lax.rem(z + 3, 4), lax.rem(z + 2, 4)
     up, down, twin = {"state": zu}, {"state": zd}, {"tm_2": 1 - c}
-    greet([up, down, twin])
-    swaps = []
-    for part, rows in ((0, pl.ds(0, N)), (1, pl.ds(N, ROWS - N))):
-        swaps.append(remote(own.at[rows], twin_buf.at[rows], swap_send.at[part], swap_recv.at[part], twin))
-        swaps[part].start()
+    barrier = pltpu.get_barrier_semaphore()
+    for peer in (up, down, twin):
+        pl.semaphore_signal(barrier, inc=1, device_id=peer, device_id_type=MESH)
+    swaps = [
+        remote(own.at[rows], twin_buf.at[rows], swap_send.at[part], swap_recv.at[part], twin)
+        for part, rows in ((0, pl.ds(0, N)), (1, pl.ds(N, ROWS - N)))
+    ]
+
+    def gain_ready():
+        pl.semaphore_wait(barrier, 3)
+        swaps[0].start()
+
+    element(cov, left, pred, vectors, own, *scratch, gain_ready)
+    swaps[1].start()
     cp = Copies(out, send, recv)
     ups, downs, tails, twins = [], [], [], []
 
@@ -700,8 +715,8 @@
     cp.finish()
 
 
-QUARTER = (128, 96)
-PIECES = 4
+QUARTER = (128, 88)
+PIECES = (((0, 32), (32, 32), (64, 32), (96, 32)), ((0, 24), (24, 24), (48, 24), (72, 16)))
 
 
 def ring_kernel(mine, axis, own, others, rest, out, total, *refs):
@@ -721,7 +736,7 @@
     load = chosen(me, own, from_slots(others))
 
     def run(part):
-        base, size = N if part else 0, QUARTER[part] // PIECES
+        base, pieces = N if part else 0, PIECES[part]
         span = pl.ds(base, 4 * QUARTER[part])
         if part:
             split_gains(4, load, work)
@@ -736,43 +751,44 @@
             copy.start()
 
         def row_of(quarter, j):
-            return pl.multiple_of(base + quarter * QUARTER[part] + j * size, 8)
-
+            return pl.multiple_of(base + quarter * QUARTER[part] + pieces[j][0], 8)
+
+        count = len(pieces)
         ups, downs, zs, tails = [], [], [], []
-        for j in range(PIECES):
+        for j in range(count):
             for k in (0, 1):
-                for into, peer, jj in ((ups, up, j), (downs, down, PIECES - 1 - j)):
+                for into, peer, jj in ((ups, up, j), (downs, down, count - 1 - j)):
                     row = row_of(quarters[k], jj)
-                    n = cp.put(peer, a, row, size, total.at[pl.ds(row, size), :])
-                    into.append((n, k, jj, j < PIECES // 2))
+                    n = cp.put(peer, a, row, pieces[jj][1], total.at[pl.ds(row, pieces[jj][1]), :])
+                    into.append((n, k, jj, j < count // 2))
         hand(total.at[span], total.at[span], 0)
         hand(rest.at[span], rest.at[span], 1)
 
-        def pass_on(slot, row):
-            place = out.at[slot, pl.ds(row, size), :]
+        def pass_on(slot, row, j):
+            place = out.at[slot, pl.ds(row, pieces[j][1]), :]
             hand(place, place, 2)
 
         def spread(slot, k, j):
             row = row_of(quarters[k], j)
-            zs.append((cp.put(below if k else above, slot, row, size), slot, k, j))
-            pass_on(slot, row)
-
-        def take(count):
-            while len(zs) > count:
+            zs.append((cp.put(below if k else above, slot, row, pieces[j][1]), slot, k, j))
+            pass_on(slot, row, j)
+
+        def take(keep):
+            while len(zs) > keep:
                 n, slot, k, j = zs.pop(0)
                 row = row_of(coming[k], j)
-                cp.arrived(n, slot, row, size)
-                pass_on(slot, row)
+                cp.arrived(n, slot, row, pieces[j][1])
+                pass_on(slot, row, j)
 
         for pair in zip(ups, downs):
             for (n, k, j, further), slot, peer in zip(pair, (ad, au), (up, down)):
                 row = row_of(quarters[k], j)
-                cp.arrived(n, slot, row, size)
+                cp.arrived(n, slot, row, pieces[j][1])
                 if further:
-                    tails.append((cp.put(peer, slot, row, size), k, j))
+                    tails.append((cp.put(peer, slot, row, pieces[j][1]), k, j))
                 spread(slot, k, j)
         for n, k, j in tails:
-            cp.arrived(n, ao, row_of(quarters[k], j), size)
+            cp.arrived(n, ao, row_of(quarters[k], j), pieces[j][1])
             spread(ao, k, j)
             take(len(zs) - 2)
         take(0)
@@ -814,7 +830,6 @@
     )(*args)
 
 
-BIG = 32 * 1024 * 1024
 def suffix_work(count):
     return [
         pltpu.VMEM((2, N, N), F32),
@@ -860,25 +875,29 @@
         limit=FIRST_LIMIT,
         out_spec=VM,
     )
-    own = pl.pallas_call(
-        element_kernel,
-        name="element",
-        out_shape=shape(ROWS, N),
+    packet, packets = shape(ROWS, N), shape(4, ROWS, N)
+    square = shape(N, N)
+    predicted = pl.pallas_call(
+        predict_kernel,
+        name="predict",
+        out_shape=(square, square, square, shape(16, N)),
         in_specs=[SM] + [VM] * 5,
-        out_specs=VM,
-        scratch_shapes=[pltpu.VMEM((N, N), F32)] * 3 + [pltpu.VMEM((8, N), F32), pltpu.VMEM((N, N), F32), pltpu.VMEM((B, B), F32)],
-        compiler_params=params(BIG),
+        out_specs=(VM, VM, VM, VM),
+        compiler_params=params(RING_LIMIT),
     )(pattern, cov, mean_here, twin_mean, noise_here, blocks_here)
-    packet, packets = shape(ROWS, N), shape(4, ROWS, N)
-    pair, pairs = pl.pallas_call(
+    own, pair, pairs = pl.pallas_call(
         pair_kernel,
         name="pair",
-        out_shape=(packet, packets),
-        in_specs=[VM],
-        out_specs=(VM, VM),
-        scratch_shapes=[pltpu.VMEM((ROWS, N), F32)] + suffix_work(2) + [DMA((2,)), DMA((2,)), DMA((48,)), DMA((48,))],
+        out_shape=(packet, packet, packets),
+        in_specs=[VM] * 4,
+        out_specs=(VM, VM, VM),
+        scratch_shapes=[pltpu.VMEM((ROWS, N), F32)]
+        + [pltpu.VMEM((N, N), F32)] * 2
+        + [pltpu.VMEM((B, B), F32)]
+        + suffix_work(2)
+        + [DMA((2,)), DMA((2,)), DMA((48,)), DMA((48,))],
         compiler_params=params(RING_LIMIT, collective_id=2, has_side_effects=True),
-    )(own)
+    )(*predicted)
     down, columns, column = ring("ring_x", 3, "state", "tm_1", pair, pairs)
     across, rows, row = ring("ring_y", 4, "tm_1", "tm_0", column, columns)
     half = pltpu.VMEM((N, N), BF16)

time: 181 us -> 177 us (0.978)
  Pallas kernels: 174 us -> 170 us
    pallas_call x2, Pallas kernels: 73.7 us -> 69.2 us  [the longest x1 64.5 us: on_device(): pl.pallas_call(pair_kernel, name='pair', out_shape=(packet, packet, packe...]
where the time goes in v7:
time: 177 us; the launch traced here: 176 us
  Pallas kernels  170 us (96%)
  local copies, waits for them, and re-layouts  5.96 us (3%)
    pallas_call x1, Pallas kernels, on_device(): pl.pallas_call(pair_kernel, name='pair', out_shape=(packet, packet, packe...  64.5 us
    pallas_call x2, Pallas kernels, ring(): pl.pallas_call(partial(ring_kernel, mine, axis), name=name, out_shape=(pa...  56.4 us
    pallas_call x1, Pallas kernels, on_device(): pl.pallas_call(final_kernel, name='final', out_shape=(shape(4, B, N), sha...  28.5 us
    pallas_call x1, Pallas kernels, comm(): pl.pallas_call(kernel, name=name, out_shape=outs, in_specs=[in_spec] * le...  15.6 us
    unnamed x10, local copies, waits for them, and re-layouts  5.37 us
    pallas_call x1, Pallas kernels, on_device(): pl.pallas_call(predict_kernel, name='predict', out_shape=(square, square,...  4.78 us

profile of v7, /device:TPU:1, one launch (start us, length us, event | category | flops | bytes accessed | tf_op | source)
XLA Modules:
  0.0 176.5 jit_solution(8740536018205079227)
XLA Ops:
  0.6 0.0 copy-start
  0.6 1.2 copy-done
  1.9 0.0 copy-start.1
  1.9 1.0 copy-done.1
  2.9 0.0 copy-start.2
  2.9 0.7 copy-done.2
  3.6 0.0 copy-start.3
  3.6 0.7 copy-done.3
  4.3 15.6 %gather_step.1 = (f32[4,128,512]{2,1,0:T(8,128)S(1)}, f32[4,512]{1,0:T(4,128)S(1)}, f32[4,512]{1,0:T(4,128)S(1)}, f32[1,512]{1,0:T(1,128)S(1)}, f32[4,2,128,128]{3,2,1,0:T(8,128)S(1)}) custom-call(f32[4,128,512]{2,1,0:T(8,128)S(1)} %copy-done, f32[4,512]{1,0:T(4,128)S(1)} %copy-done.2, f32[1,512]{1,0:T(1,128)S(1)} %bitcast.2, f32[4,2,128,128]{3,2,1,0:T(8,128)S(1)} %copy-done.1), custom_call_target="tpu_custom_call" | custom-call | tf_op jit(solution)/shard_map/gather_step/pallas_call | solution.py:820
  19.9 0.8 copy.7.pattern
  20.7 4.8 %predict.1 = (f32[512,512]{1,0:T(8,128)S(1)}, f32[512,512]{1,0:T(8,128)S(1)}, f32[512,512]{1,0:T(8,128)S(1)}, f32[16,512]{1,0:T(8,128)S(1)}) custom-call(s32[4,2]{1,0:T(4,128)S(1)} %copy.7.pattern, f32[4,128,512]{2,1,0:T(8,128)S(1)} %get-tuple-element.22.cov_in, f32[4,512]{1,0:T(4,128)S(1)} %get-tuple-element.23.mean_a, ...), custom_call_target="tpu_custom_call" | custom-call | tf_op jit(solution)/shard_map/predict/pallas_call | solution.py:880
  25.5 64.5 %pair.1 = (f32[896,512]{1,0:T(8,128)S(1)}, f32[896,512]{1,0:T(8,128)S(1)}, f32[4,896,512]{2,1,0:T(8,128)S(1)}) custom-call(f32[512,512]{1,0:T(8,128)S(1)} %get-tuple-element.27.cov, f32[512,512]{1,0:T(8,128)S(1)} %get-tuple-element.28.left, f32[512,512]{1,0:T(8,128)S(1)} %get-tuple-element.29.pred, f32[16,512]{1,0:T(8,128)S(1)} %get-tuple-element.30.vectors), custom_call_target="tpu_custom_call" | custom-call | tf_op jit(solution)/shard_map/pair/pallas_call | solution.py:888
  90.0 28.1 %ring_x.1 = (f32[896,512]{1,0:T(8,128)S(1)}, f32[4,896,512]{2,1,0:T(8,128)S(1)}, f32[896,512]{1,0:T(8,128)S(1)}) custom-call(f32[896,512]{1,0:T(8,128)S(1)} %get-tuple-element.31.own.pair, f32[4,896,512]{2,1,0:T(8,128)S(1)} %get-tuple-element.32.others), custom_call_target="tpu_custom_call" | custom-call | tf_op jit(solution)/shard_map/ring_x/pallas_call | solution.py:848
  118.1 28.3 %ring_y.1 = (f32[896,512]{1,0:T(8,128)S(1)}, f32[4,896,512]{2,1,0:T(8,128)S(1)}, f32[896,512]{1,0:T(8,128)S(1)}) custom-call(f32[896,512]{1,0:T(8,128)S(1)} %get-tuple-element.33.own, f32[4,896,512]{2,1,0:T(8,128)S(1)} %get-tuple-element.34.others), custom_call_target="tpu_custom_call" | custom-call | tf_op jit(solution)/shard_map/ring_y/pallas_call | solution.py:848
  146.4 28.5 %final.1 = (f32[4,128,512]{2,1,0:T(8,128)S(1)}, f32[4,8,512]{2,1,0:T(8,128)S(1)}) custom-call(f32[896,512]{1,0:T(8,128)S(1)} %get-tuple-element.35.row, f32[4,896,512]{2,1,0:T(8,128)S(1)} %get-tuple-element.36.rows, f32[896,512]{1,0:T(8,128)S(1)} %get-tuple-element.37.across, f32[896,512]{1,0:T(8,128)S(1)} %get-tuple-element.38.down, ...), custom_call_target="tpu_custom_call" | custom-call | tf_op jit(solution)/shard_map/final/pallas_call | solution.py:904
  174.9 0.6 constant_dynamic-slice_fusion
  175.5 1.0 copy.9
  (1 shorter events, 0.0 us)
Async XLA Ops:
  0.6 1.2 copy-start
  1.9 1.0 copy-start.1
  2.9 0.7 copy-start.2
  3.6 0.7 copy-start.3

commit v8 on v7

--- a/solution.py
+++ b/solution.py
@@ -405,7 +405,14 @@
 
         @pl.when(far)
         def _():
-            start(cov.at[i], relay.at[e], z, send.at[i], relay_recv.at[e], {"state": lax.rem(z + (3 if e else 1), 4)})
+            for t in range(3):
+                remote(
+                    lanes_of_block(cov.at[i], z + t),
+                    lanes_of_block(relay.at[e], z + t),
+                    send.at[i],
+                    relay_recv.at[e, t],
+                    {"state": lax.rem(z + (3 if e else 1), 4)},
+                ).start()
 
     for i in range(4):
         dz, e, mine, far = target(i)
@@ -418,16 +425,22 @@
         def _():
             start(cov.at[i], out.at[z], z, send.at[i], recv.at[z], {"state": dz, "tm_2": e})
 
-    duties = []
-    for e in range(2):
-        source, dz = lax.rem(z + (1 if e else 3), 4), lax.rem(z + (3 if e else 1), 4)
-        duty = source // 2 != c
-        duties.append(duty)
-
-        @pl.when(duty)
-        def _():
-            whole(relay.at[e], send.at[0], relay_recv.at[e]).wait_recv()
-            start(relay.at[e], out.at[source], source, relay_send.at[e], recv.at[source], {"state": dz, "tm_2": e})
+    sources = [lax.rem(z + (1 if e else 3), 4) for e in range(2)]
+    duties = [source // 2 != c for source in sources]
+    for t in range(3):
+        for e in range(2):
+
+            @pl.when(duties[e])
+            def _():
+                here = lanes_of_block(relay.at[e], sources[e] + t)
+                remote(here, here, send.at[0], relay_recv.at[e, t], {"state": 0, "tm_2": 0}).wait_recv()
+                remote(
+                    here,
+                    lanes_of_block(out.at[sources[e]], sources[e] + t),
+                    relay_send.at[e],
+                    recv.at[sources[e]],
+                    {"state": lax.rem(z + (3 if e else 1), 4), "tm_2": e},
+                ).start()
 
     for i in range(4):
         dz, e, mine, far = target(i)
@@ -562,8 +575,16 @@
     def slab(t):
         return cov.at[pl.ds(pl.multiple_of(t * B, B), B), :]
 
-    far = remote(slab(opposite), relay, relay_send.at[0], relay_recv, {"state": onward})
-    far.start()
+    parts = [pl.ds(B // 4 * p, B // 4) for p in range(4)]
+    far = remote(slab(opposite), relay, relay_send.at[0], relay_recv.at[0], {"state": onward})
+    for p, part in enumerate(parts):
+        remote(
+            cov.at[pl.ds(pl.multiple_of(opposite * B + B // 4 * p, 8), B // 4), :],
+            relay.at[part],
+            relay_send.at[0],
+            relay_recv.at[p],
+            {"state": onward},
+        ).start()
 
     def copy(t):
         return remote(slab(t), out.at[slot], send.at[t], recv.at[slot], {"state": t, "tm_2": core})
@@ -595,15 +616,21 @@
             copy(t).start()
 
     source = lax.rem(z + 3 + 2 * c, 4)
-    far.wait_recv()
-    on = remote(
-        relay,
-        out.at[2 * lax.rem(source, 2) + c],
-        relay_send.at[1],
-        recv.at[2 * lax.rem(source, 2) + c],
-        {"state": onward, "tm_2": source // 2},
-    )
-    on.start()
+    there = out.at[2 * lax.rem(source, 2) + c]
+
+    def onto(part):
+        return remote(
+            relay.at[part],
+            there.at[part],
+            relay_send.at[1],
+            recv.at[2 * lax.rem(source, 2) + c],
+            {"state": onward, "tm_2": source // 2},
+        )
+
+    for p, part in enumerate(parts):
+        here = relay.at[part]
+        remote(here, here, relay_send.at[0], relay_recv.at[p], {"state": onward}).wait_recv()
+        onto(part).start()
     for t in range(4):
 
         @pl.when(mine(t))
@@ -620,7 +647,7 @@
             copy(t).wait_send()
 
     far.wait_send()
-    on.wait_send()
+    onto(pl.ds(0, B)).wait_send()
     for i in range(4):
 
         @pl.when(jnp.logical_not((z == 2 * c + i // 2) & (c == i % 2)))
@@ -719,7 +746,7 @@
 PIECES = (((0, 32), (32, 32), (64, 32), (96, 32)), ((0, 24), (24, 24), (48, 24), (72, 16)))
 
 
-def ring_kernel(mine, axis, own, others, rest, out, total, *refs):
+def ring_kernel(mine, axis, coarse, own, others, rest, out, total, *refs):
     z, c, a = lax.axis_index("state"), lax.axis_index("tm_2"), lax.axis_index(axis)
     work, (send, recv, twin_send, twin_recv) = refs[:8], refs[8:]
     me = lax.axis_index(mine)
@@ -764,32 +791,41 @@
         hand(total.at[span], total.at[span], 0)
         hand(rest.at[span], rest.at[span], 1)
 
-        def pass_on(slot, row, j):
-            place = out.at[slot, pl.ds(row, pieces[j][1]), :]
+        came_in = {}
+
+        def pass_on(slot, quarter, j, key):
+            came_in.setdefault(key, []).append(j)
+            if len(came_in[key]) * coarse == count:
+                row, rows = row_of(quarter, 0), QUARTER[part]
+            elif not coarse:
+                row, rows = row_of(quarter, j), pieces[j][1]
+            else:
+                return
+            place = out.at[slot, pl.ds(row, rows), :]
             hand(place, place, 2)
 
-        def spread(slot, k, j):
+        def spread(slot, k, j, name):
             row = row_of(quarters[k], j)
-            zs.append((cp.put(below if k else above, slot, row, pieces[j][1]), slot, k, j))
-            pass_on(slot, row, j)
+            zs.append((cp.put(below if k else above, slot, row, pieces[j][1]), slot, k, j, name))
+            pass_on(slot, quarters[k], j, (name, k))
 
         def take(keep):
             while len(zs) > keep:
-                n, slot, k, j = zs.pop(0)
+                n, slot, k, j, name = zs.pop(0)
                 row = row_of(coming[k], j)
                 cp.arrived(n, slot, row, pieces[j][1])
-                pass_on(slot, row, j)
+                pass_on(slot, coming[k], j, (name, k + 2))
 
         for pair in zip(ups, downs):
-            for (n, k, j, further), slot, peer in zip(pair, (ad, au), (up, down)):
+            for (n, k, j, further), slot, peer, name in zip(pair, (ad, au), (up, down), ("below", "above")):
                 row = row_of(quarters[k], j)
                 cp.arrived(n, slot, row, pieces[j][1])
                 if further:
                     tails.append((cp.put(peer, slot, row, pieces[j][1]), k, j))
-                spread(slot, k, j)
+                spread(slot, k, j, name)
         for n, k, j in tails:
             cp.arrived(n, ao, row_of(quarters[k], j), pieces[j][1])
-            spread(ao, k, j)
+            spread(ao, k, j, "opposite")
             take(len(zs) - 2)
         take(0)
         cp.finish()
@@ -843,10 +879,10 @@
     ]
 
 
-def ring(name, collective_id, mine, axis, own, others):
+def ring(name, collective_id, mine, axis, own, others, coarse=1):
     packet = shape(ROWS, N)
     return pl.pallas_call(
-        partial(ring_kernel, mine, axis),
+        partial(ring_kernel, mine, axis, coarse),
         name=name,
         out_shape=(packet, shape(4, ROWS, N), packet),
         in_specs=[VM, VM],
@@ -867,7 +903,7 @@
         "gather_step",
         0,
         (shape(4, B, N), shape(4, N), shape(4, N), shape(1, N), shape(4, 2, B, B)),
-        [pltpu.VMEM((2, B, N), F32), DMA((4,)), DMA((4,)), DMA((2,)), DMA((2,)), DMA, DMA, DMA, DMA((3,))],
+        [pltpu.VMEM((2, B, N), F32), DMA((4,)), DMA((4,)), DMA((2,)), DMA((2, 3)), DMA, DMA, DMA, DMA((3,))],
         filtered_cov,
         filtered_mean,
         noise_var.reshape(1, N),
@@ -909,7 +945,7 @@
         out_specs=(VM, VM),
         scratch_shapes=[pltpu.VMEM((N, N), F32), pltpu.VMEM((8, N), F32), pltpu.VMEM((8, N), F32), pltpu.VMEM((B, N), F32)]
         + [pltpu.VMEM((N, N), F32), pltpu.VMEM((8, N), F32), half, half, half, half, pltpu.VMEM((N, N), F32)]
-        + [DMA((4,)), DMA((4,)), DMA((2,)), DMA, DMA((2,)), DMA((4,)), DMA((4,))],
+        + [DMA((4,)), DMA((4,)), DMA((2,)), DMA((4,)), DMA((2,)), DMA((4,)), DMA((4,))],
         compiler_params=params(RING_LIMIT, collective_id=5, has_side_effects=True),
     )(row, rows, across, down, pair, own)
     return lax.dynamic_slice_in_dim(means[:, 0, :], z * B, B, 1), smooth_cov

time: 177 us -> 177 us (level)
  no operation moved by 1% of the time
where the time goes in v8:
time: 177 us; the launch traced here: 176 us
  Pallas kernels  170 us (96%)
  local copies, waits for them, and re-layouts  5.96 us (3%)
    pallas_call x1, Pallas kernels, on_device(): pl.pallas_call(pair_kernel, name='pair', out_shape=(packet, packet, packe...  64.5 us
    pallas_call x2, Pallas kernels, ring(): pl.pallas_call(partial(ring_kernel, mine, axis, coarse), name=name, out_s...  56.8 us
    pallas_call x1, Pallas kernels, on_device(): pl.pallas_call(final_kernel, name='final', out_shape=(shape(4, B, N), sha...  27.9 us
    pallas_call x1, Pallas kernels, comm(): pl.pallas_call(kernel, name=name, out_shape=outs, in_specs=[in_spec] * le...  15.7 us
    unnamed x10, local copies, waits for them, and re-layouts  5.37 us
    pallas_call x1, Pallas kernels, on_device(): pl.pallas_call(predict_kernel, name='predict', out_shape=(square, square,...  4.78 us

profile of v8, /device:TPU:1, one launch (start us, length us, event | category | flops | bytes accessed | tf_op | source)
XLA Modules:
  0.0 176.3 jit_solution(8679463995549457337)
XLA Ops:
  0.6 0.0 copy-start
  0.6 1.2 copy-done
  1.9 0.0 copy-start.1
  1.9 1.0 copy-done.1
  2.9 0.0 copy-start.2
  2.9 0.7 copy-done.2
  3.6 0.0 copy-start.3
  3.6 0.7 copy-done.3
  4.3 15.7 %gather_step.1 = (f32[4,128,512]{2,1,0:T(8,128)S(1)}, f32[4,512]{1,0:T(4,128)S(1)}, f32[4,512]{1,0:T(4,128)S(1)}, f32[1,512]{1,0:T(1,128)S(1)}, f32[4,2,128,128]{3,2,1,0:T(8,128)S(1)}) custom-call(f32[4,128,512]{2,1,0:T(8,128)S(1)} %copy-done, f32[4,512]{1,0:T(4,128)S(1)} %copy-done.2, f32[1,512]{1,0:T(1,128)S(1)} %bitcast.2, f32[4,2,128,128]{3,2,1,0:T(8,128)S(1)} %copy-done.1), custom_call_target="tpu_custom_call" | custom-call | tf_op jit(solution)/shard_map/gather_step/pallas_call | solution.py:856
  20.0 0.8 copy.7.pattern
  20.7 4.8 %predict.1 = (f32[512,512]{1,0:T(8,128)S(1)}, f32[512,512]{1,0:T(8,128)S(1)}, f32[512,512]{1,0:T(8,128)S(1)}, f32[16,512]{1,0:T(8,128)S(1)}) custom-call(s32[4,2]{1,0:T(4,128)S(1)} %copy.7.pattern, f32[4,128,512]{2,1,0:T(8,128)S(1)} %get-tuple-element.22.cov_in, f32[4,512]{1,0:T(4,128)S(1)} %get-tuple-element.23.mean_a, ...), custom_call_target="tpu_custom_call" | custom-call | tf_op jit(solution)/shard_map/predict/pallas_call | solution.py:916
  25.5 64.5 %pair.1 = (f32[896,512]{1,0:T(8,128)S(1)}, f32[896,512]{1,0:T(8,128)S(1)}, f32[4,896,512]{2,1,0:T(8,128)S(1)}) custom-call(f32[512,512]{1,0:T(8,128)S(1)} %get-tuple-element.27.cov, f32[512,512]{1,0:T(8,128)S(1)} %get-tuple-element.28.left, f32[512,512]{1,0:T(8,128)S(1)} %get-tuple-element.29.pred, f32[16,512]{1,0:T(8,128)S(1)} %get-tuple-element.30.vectors), custom_call_target="tpu_custom_call" | custom-call | tf_op jit(solution)/shard_map/pair/pallas_call | solution.py:924
  90.0 27.4 %ring_x.1 = (f32[896,512]{1,0:T(8,128)S(1)}, f32[4,896,512]{2,1,0:T(8,128)S(1)}, f32[896,512]{1,0:T(8,128)S(1)}) custom-call(f32[896,512]{1,0:T(8,128)S(1)} %get-tuple-element.31.own.pair, f32[4,896,512]{2,1,0:T(8,128)S(1)} %get-tuple-element.32.others), custom_call_target="tpu_custom_call" | custom-call | tf_op jit(solution)/shard_map/ring_x/pallas_call | solution.py:884
  117.4 29.5 %ring_y.1 = (f32[896,512]{1,0:T(8,128)S(1)}, f32[4,896,512]{2,1,0:T(8,128)S(1)}, f32[896,512]{1,0:T(8,128)S(1)}) custom-call(f32[896,512]{1,0:T(8,128)S(1)} %get-tuple-element.33.own, f32[4,896,512]{2,1,0:T(8,128)S(1)} %get-tuple-element.34.others), custom_call_target="tpu_custom_call" | custom-call | tf_op jit(solution)/shard_map/ring_y/pallas_call | solution.py:884
  146.8 27.9 %final.1 = (f32[4,128,512]{2,1,0:T(8,128)S(1)}, f32[4,8,512]{2,1,0:T(8,128)S(1)}) custom-call(f32[896,512]{1,0:T(8,128)S(1)} %get-tuple-element.35.row, f32[4,896,512]{2,1,0:T(8,128)S(1)} %get-tuple-element.36.rows, f32[896,512]{1,0:T(8,128)S(1)} %get-tuple-element.37.across, f32[896,512]{1,0:T(8,128)S(1)} %get-tuple-element.38.down, ...), custom_call_target="tpu_custom_call" | custom-call | tf_op jit(solution)/shard_map/final/pallas_call | solution.py:940
  174.8 0.6 constant_dynamic-slice_fusion
  175.4 1.0 copy.9
  (1 shorter events, 0.0 us)
Async XLA Ops:
  0.6 1.2 copy-start
  1.9 1.0 copy-start.1
  2.9 0.7 copy-start.2
  3.6 0.7 copy-start.3

commit v9 on v7

--- a/solution.py
+++ b/solution.py
@@ -158,34 +158,30 @@
             cov[i * B : i * B + B, lanes] = cov_in[i, :, lanes]
         j = (i + 3) % 4
         cov[i * B : i * B + B, j * B : j * B + B] = jnp.transpose(cov_in[j, :, i * B : i * B + B])
-    tb = lambda r, j: blocks[r, j]
-
-    def rows_of(ref, block):
-        return ref[pl.ds(pl.multiple_of(block * B, B), B), :]
-
-    def lanes_of(ref, row, rows, block):
-        return ref[row : row + rows, pl.ds(pl.multiple_of(block * B, B), B)]
+    both = [jnp.concatenate([blocks[r, 0], blocks[r, 1]], axis=1) for r in range(4)]
+
+    def rows_of(ref, r):
+        return jnp.concatenate(
+            [ref[pl.ds(pl.multiple_of(pattern[r, j] * B, B), B), :] for j in range(2)], axis=0
+        )
+
+    def lanes_of(ref, rows, r):
+        return jnp.concatenate(
+            [ref[0:rows, pl.ds(pl.multiple_of(pattern[r, j] * B, B), B)] for j in range(2)], axis=1
+        )
 
     place = lax.rem(2 * z + c, 4)
     mean = jnp.where(z // 2 == c, mean_a[pl.ds(place, 1), :], mean_b[pl.ds(place, 1), :])
     vectors[0:8, :] = jnp.broadcast_to(mean, (8, N))
     pushed = []
     for r in range(4):
-        t0, t1 = tb(r, 0), tb(r, 1)
-        left[r * B : r * B + B, :] = dot6(t0, rows_of(cov, pattern[r, 0])) + dot6(
-            t1, rows_of(cov, pattern[r, 1])
-        )
-        pushed.append(
-            dot6(lanes_of(vectors, 0, 8, pattern[r, 0]), t0, 1)
-            + dot6(lanes_of(vectors, 0, 8, pattern[r, 1]), t1, 1)
-        )
+        left[r * B : r * B + B, :] = dot6(both[r], rows_of(cov, r))
+        pushed.append(dot6(lanes_of(vectors, 8, r), both[r], 1))
     vectors[8:16, :] = jnp.concatenate(pushed, axis=1)
     eye = lax.broadcasted_iota(jnp.int32, (B, B), 0) == lax.broadcasted_iota(jnp.int32, (B, B), 1)
     for r in range(4):
         rows = (r + 1) * B
-        value = dot6(lanes_of(left, 0, rows, pattern[r, 0]), tb(r, 0), 1) + dot6(
-            lanes_of(left, 0, rows, pattern[r, 1]), tb(r, 1), 1
-        )
+        value = dot6(lanes_of(left, rows, r), both[r], 1)
         pred[0:rows, r * B : r * B + B] = value
         q = jnp.where(eye, jnp.broadcast_to(noise[0:1, r * B : r * B + B], (B, B)), 0.0)
         pred[r * B : rows, r * B : r * B + B] += q

time: 177 us -> 176 us (level)
  no operation moved by 1% of the time
where the time goes in v9:
time: 176 us; the launch traced here: 175 us
  Pallas kernels  169 us (96%)
  local copies, waits for them, and re-layouts  5.96 us (3%)
    pallas_call x1, Pallas kernels, on_device(): pl.pallas_call(pair_kernel, name='pair', out_shape=(packet, packet, packe...  64.5 us
    pallas_call x2, Pallas kernels, ring(): pl.pallas_call(partial(ring_kernel, mine, axis), name=name, out_shape=(pa...  56.4 us
    pallas_call x1, Pallas kernels, on_device(): pl.pallas_call(final_kernel, name='final', out_shape=(shape(4, B, N), sha...  28.6 us
    pallas_call x1, Pallas kernels, comm(): pl.pallas_call(kernel, name=name, out_shape=outs, in_specs=[in_spec] * le...  15.6 us
    unnamed x10, local copies, waits for them, and re-layouts  5.37 us

profile of v9, /device:TPU:1, one launch (start us, length us, event | category | flops | bytes accessed | tf_op | source)
XLA Modules:
  0.0 175.2 jit_solution(541589446311806359)
XLA Ops:
  0.6 0.0 copy-start
  0.6 1.2 copy-done
  1.9 0.0 copy-start.1
  1.9 1.0 copy-done.1
  2.9 0.0 copy-start.2
  2.9 0.7 copy-done.2
  3.6 0.0 copy-start.3
  3.6 0.7 copy-done.3
  4.3 15.6 %gather_step.1 = (f32[4,128,512]{2,1,0:T(8,128)S(1)}, f32[4,512]{1,0:T(4,128)S(1)}, f32[4,512]{1,0:T(4,128)S(1)}, f32[1,512]{1,0:T(1,128)S(1)}, f32[4,2,128,128]{3,2,1,0:T(8,128)S(1)}) custom-call(f32[4,128,512]{2,1,0:T(8,128)S(1)} %copy-done, f32[4,512]{1,0:T(4,128)S(1)} %copy-done.2, f32[1,512]{1,0:T(1,128)S(1)} %bitcast.2, f32[4,2,128,128]{3,2,1,0:T(8,128)S(1)} %copy-done.1), custom_call_target="tpu_custom_call" | custom-call | tf_op jit(solution)/shard_map/gather_step/pallas_call | solution.py:816
  19.9 0.8 copy.7.pattern
  20.7 3.5 %predict.1 = (f32[512,512]{1,0:T(8,128)S(1)}, f32[512,512]{1,0:T(8,128)S(1)}, f32[512,512]{1,0:T(8,128)S(1)}, f32[16,512]{1,0:T(8,128)S(1)}) custom-call(s32[4,2]{1,0:T(4,128)S(1)} %copy.7.pattern, f32[4,128,512]{2,1,0:T(8,128)S(1)} %get-tuple-element.22.cov_in, f32[4,512]{1,0:T(4,128)S(1)} %get-tuple-element.23.mean_a, ...), custom_call_target="tpu_custom_call" | custom-call | tf_op jit(solution)/shard_map/predict/pallas_call | solution.py:876
  24.2 64.5 %pair.1 = (f32[896,512]{1,0:T(8,128)S(1)}, f32[896,512]{1,0:T(8,128)S(1)}, f32[4,896,512]{2,1,0:T(8,128)S(1)}) custom-call(f32[512,512]{1,0:T(8,128)S(1)} %get-tuple-element.27.cov, f32[512,512]{1,0:T(8,128)S(1)} %get-tuple-element.28.left, f32[512,512]{1,0:T(8,128)S(1)} %get-tuple-element.29.pred, f32[16,512]{1,0:T(8,128)S(1)} %get-tuple-element.30.vectors), custom_call_target="tpu_custom_call" | custom-call | tf_op jit(solution)/shard_map/pair/pallas_call | solution.py:884
  88.7 28.1 %ring_x.1 = (f32[896,512]{1,0:T(8,128)S(1)}, f32[4,896,512]{2,1,0:T(8,128)S(1)}, f32[896,512]{1,0:T(8,128)S(1)}) custom-call(f32[896,512]{1,0:T(8,128)S(1)} %get-tuple-element.31.own.pair, f32[4,896,512]{2,1,0:T(8,128)S(1)} %get-tuple-element.32.others), custom_call_target="tpu_custom_call" | custom-call | tf_op jit(solution)/shard_map/ring_x/pallas_call | solution.py:844
  116.8 28.3 %ring_y.1 = (f32[896,512]{1,0:T(8,128)S(1)}, f32[4,896,512]{2,1,0:T(8,128)S(1)}, f32[896,512]{1,0:T(8,128)S(1)}) custom-call(f32[896,512]{1,0:T(8,128)S(1)} %get-tuple-element.33.own, f32[4,896,512]{2,1,0:T(8,128)S(1)} %get-tuple-element.34.others), custom_call_target="tpu_custom_call" | custom-call | tf_op jit(solution)/shard_map/ring_y/pallas_call | solution.py:844
  145.1 28.6 %final.1 = (f32[4,128,512]{2,1,0:T(8,128)S(1)}, f32[4,8,512]{2,1,0:T(8,128)S(1)}) custom-call(f32[896,512]{1,0:T(8,128)S(1)} %get-tuple-element.35.row, f32[4,896,512]{2,1,0:T(8,128)S(1)} %get-tuple-element.36.rows, f32[896,512]{1,0:T(8,128)S(1)} %get-tuple-element.37.across, f32[896,512]{1,0:T(8,128)S(1)} %get-tuple-element.38.down, ...), custom_call_target="tpu_custom_call" | custom-call | tf_op jit(solution)/shard_map/final/pallas_call | solution.py:900
  173.7 0.6 constant_dynamic-slice_fusion
  174.2 1.0 copy.9
  (1 shorter events, 0.0 us)
Async XLA Ops:
  0.6 1.2 copy-start
  1.9 1.0 copy-start.1
  2.9 0.7 copy-start.2
  3.6 0.7 copy-start.3
